TPU v7x, 32 devices: a whole 2x2x4 slice. The times are simulated.
32 devices in a mesh: shard: 4 (over z), context: 2 (over y), tensor: 4 (over x, core).
Axes of the slice: x: 2, y: 2, z: 4, core: 2. Of those that a mesh axis runs over, the one named last changes fastest.
Arguments:
- tokens: bfloat16 [16, 1024, 1024], P('shard', 'context'), may hold values from -6 to 6
- cotangent: bfloat16 [16, 1024, 1024], P('shard', 'context'), may hold values from -6 to 6
- adapter_index: int32 [16], P('shard'), may hold values from 0 to 7, as said below
- ln1_gain: float32 [1024], replicated, may hold values from 0.5 to 1.5
- ln1_bias: float32 [1024], replicated, may hold values from -1.5 to 1.5
- ln2_gain: float32 [1024], replicated, may hold values from 0.5 to 1.5
- ln2_bias: float32 [1024], replicated, may hold values from -1.5 to 1.5
- layer_scale: float32 [2, 1024], replicated, may hold values from 0.4 to 1.2
- w_qkv: bfloat16 [1024, 3, 1024], P(('shard', 'context'), None, 'tensor'), may hold values from -0.1875 to 0.1875
- w_proj: bfloat16 [1024, 1024], P(('shard', 'context'), 'tensor'), may hold values from -0.5 to 0.5
- w_fc1: bfloat16 [1024, 4096], P(('shard', 'context'), 'tensor'), may hold values from -0.1875 to 0.1875
- w_fc2: bfloat16 [1024, 4096], P(('shard', 'context'), 'tensor'), may hold values from -0.09375 to 0.09375
- down_in: bfloat16 [8, 4, 1024, 16], replicated, may hold values from -0.1875 to 0.1875
- qkv_up: bfloat16 [8, 3, 16, 1024], P(None, None, None, 'tensor'), may hold values from -1.5 to 1.5
- fc1_up: bfloat16 [8, 16, 4096], P(None, None, 'tensor'), may hold values from -1.5 to 1.5
- proj_down: bfloat16 [8, 1024, 16], P(None, 'tensor'), may hold values from -0.5 to 0.5
- fc2_down: bfloat16 [8, 4096, 16], P(None, 'tensor'), may hold values from -0.09375 to 0.09375
- out_up: bfloat16 [8, 2, 16, 1024], replicated, may hold values from -1.5 to 1.5
Outputs:
- result: bfloat16 [16, 1024, 1024], P('shard', 'context')
- input_grad: float32 [16, 1024, 1024], P('shard', 'context')
- down_in_grad: float32 [8, 4, 1024, 16], replicated
- qkv_up_grad: float32 [8, 3, 16, 1024], P(None, None, None, 'tensor')
- fc1_up_grad: float32 [8, 16, 4096], P(None, None, 'tensor')
- proj_down_grad: float32 [8, 1024, 16], P(None, 'tensor')
- fc2_down_grad: float32 [8, 4096, 16], P(None, 'tensor')
- out_up_grad: float32 [8, 2, 16, 1024], replicated
Inputs may be any that keep to these rules, and one draw needn't show every extreme that they name: `adapter_index`: every adapter index is used by exactly 2 images.
All inputs are finite; a program needn't handle non-finite values.
Results may differ from a plain program's by a relative error of at most 0.015.
The roundings to bfloat16 on the way count: a program that leaves them out, or rounds other values in their place, can miss the bound.
Values may be sent and summed in bfloat16 or wider, within the bound.
No kernel may reach another device: no remote copies, remote signals or barrier semaphores. Data moves between devices by JAX's collectives and lax.ppermute only.
A program may use at most 256 MiB of HBM per device.

v0:
```python
import functools
import math

import jax
import jax.numpy as jnp
import numpy as np
from jax import lax
from jax.experimental import pallas as pl
from jax.experimental.pallas import tpu as pltpu
from jax.sharding import PartitionSpec as P

HEAD_DIM = 64
PAIR = 2 * HEAD_DIM
EPS = 1e-06
LOG2E = math.log2(math.e)
SCORE = 1.0 / math.sqrt(HEAD_DIM)
F32 = jnp.float32
BF16 = jnp.bfloat16
NT = (((1,), (1,)), ((), ()))
TN = (((0,), (0,)), ((), ()))
BRIEF = pl.CostEstimate(flops=1000, bytes_accessed=1000, transcendentals=0)


def dot(a, b):
    return jnp.dot(a, b, preferred_element_type=F32)


def dot_nt(a, b):
    return lax.dot_general(a, b, NT, preferred_element_type=F32)


def dot_tn(a, b):
    return lax.dot_general(a, b, TN, preferred_element_type=F32)


def head_masks(rows):
    lane = lax.broadcasted_iota(jnp.int32, (rows, PAIR), 1)
    return lane < HEAD_DIM


def attend_kernel(block, q_ref, k_ref, v_ref, _, o_ref, lse_ref):
    rows = q_ref.shape[0]
    keys = k_ref[...]
    values = jnp.concatenate([v_ref[...], jnp.ones((rows, PAIR), BF16)], axis=1)
    first = head_masks(block)

    def step(i, carry):
        at = pl.ds(pl.multiple_of(i * block, block), block)
        q = q_ref[at, :]
        outs = []
        logs = []
        for head in range(2):
            mine = first if head == 0 else jnp.logical_not(first)
            s = dot_nt(jnp.where(mine, q, jnp.zeros_like(q)), keys)
            peak = jnp.max(s, axis=1, keepdims=True)
            e = jnp.exp2((s - peak) * (SCORE * LOG2E))
            acc = dot(e.astype(BF16), values)
            total = acc[:, PAIR:]
            outs.append(acc[:, :PAIR] / total)
            logs.append(peak * (SCORE * LOG2E) + jnp.log2(total))
        o_ref[at, :] = jnp.where(first, outs[0], outs[1]).astype(BF16)
        lane = lax.broadcasted_iota(jnp.int32, (block, PAIR), 1)
        both = jnp.where(lane == 0, logs[0], logs[1])
        lse_ref[0, :, at] = jnp.transpose(both)[:8]
        return carry

    lax.fori_loop(0, rows // block, step, 0)


def thirds(rows, group, near):
    return [
        pl.BlockSpec((rows, PAIR), lambda p, j=j: (0, (group * 3 + j) * near + p))
        for j in range(3)
    ]


def attend(qkv, group, near, o):
    rows, width = qkv.shape
    pairs = width // (3 * PAIR)
    block = min(256, rows)
    anywhere = pl.BlockSpec(memory_space=pl.ANY)
    operands = [qkv, qkv, qkv, qkv if o is None else o]
    return pl.pallas_call(
        functools.partial(attend_kernel, block),
        grid=(near,),
        in_specs=thirds(rows, group, near) + [anywhere],
        out_specs=[
            pl.BlockSpec((rows, PAIR), lambda p: (0, group * near + p)),
            pl.BlockSpec((1, 8, rows), lambda p: (p, 0, 0)),
        ],
        out_shape=[
            jax.ShapeDtypeStruct((rows, pairs * PAIR), BF16),
            jax.ShapeDtypeStruct((near, 8, rows), F32),
        ],
        input_output_aliases={} if o is None else {3: 0},
        cost_estimate=BRIEF,
        name="attend",
    )(*operands)


def attend_back_kernel(
    block, near, q_ref, k_ref, v_ref, go_ref, o_ref, lse_ref, _, g_ref, gq_ref, d_ref
):
    rows = q_ref.shape[0]
    pair = pl.program_id(0)
    lanes = [pl.ds(pl.multiple_of((j * near + pair) * PAIR, PAIR), PAIR) for j in range(3)]
    first = head_masks(block)
    prod = o_ref[...].astype(F32) * go_ref[...].astype(F32)
    lane8 = lax.broadcasted_iota(jnp.int32, (8, PAIR), 1) // HEAD_DIM
    row8 = lax.broadcasted_iota(jnp.int32, (8, PAIR), 0)
    d_ref[...] = lax.dot_general(
        (lane8 == row8).astype(F32),
        prod,
        NT,
        preferred_element_type=F32,
        precision=lax.Precision.HIGHEST,
    )
    gq_ref[...] = jnp.zeros_like(gq_ref)

    def step(i, carry):
        at = pl.ds(pl.multiple_of(i * block, block), block)
        k = k_ref[at, :]
        v = v_ref[at, :]
        q = q_ref[...]
        go = go_ref[...]
        gks = []
        gvs = []
        gq = None
        for head in range(2):
            mine = first if head == 0 else jnp.logical_not(first)
            k_own = jnp.where(mine, k, jnp.zeros_like(k))
            v_own = jnp.where(mine, v, jnp.zeros_like(v))
            s = dot_nt(k_own, q)
            gp = dot_nt(v_own, go)
            p = jnp.exp2(s * (SCORE * LOG2E) - lse_ref[0, head : head + 1, :])
            gs = (p * (gp - d_ref[head : head + 1, :])).astype(BF16)
            gks.append(dot(gs, q))
            gvs.append(dot(p.astype(BF16), go))
            part = dot(jnp.transpose(k_own), gs)
            gq = part if gq is None else gq + part
        gq_ref[...] += gq
        g_ref[at, lanes[1]] = (jnp.where(first, gks[0], gks[1]) * SCORE).astype(BF16)
        g_ref[at, lanes[2]] = jnp.where(first, gvs[0], gvs[1]).astype(BF16)
        return carry

    lax.fori_loop(0, rows // block, step, 0)
    g_ref[:, lanes[0]] = (jnp.transpose(gq_ref[...]) * SCORE).astype(BF16)


def attend_back(qkv, go, o, lse, group, near, g):
    rows, width = qkv.shape
    block = min(256, rows)
    mine = pl.BlockSpec((rows, PAIR), lambda p: (0, group * near + p))
    anywhere = pl.BlockSpec(memory_space=pl.ANY)
    operands = [qkv, qkv, qkv, go, o, lse, qkv if g is None else g]
    return pl.pallas_call(
        functools.partial(attend_back_kernel, block, near),
        grid=(near,),
        in_specs=thirds(rows, group, near)
        + [mine, mine, pl.BlockSpec((1, 8, rows), lambda p: (p, 0, 0)), anywhere],
        out_specs=pl.BlockSpec((rows, 3 * near * PAIR), lambda p: (0, group)),
        out_shape=jax.ShapeDtypeStruct((rows, width), BF16),
        scratch_shapes=[pltpu.VMEM((PAIR, rows), F32), pltpu.VMEM((8, rows), F32)],
        input_output_aliases={} if g is None else {6: 0},
        cost_estimate=BRIEF,
        name="attend_back",
    )(*operands)


def mlp_kernel(
    block,
    own,
    moves,
    pieces,
    place_ref,
    gb_ref,
    down_ref,
    up_ref,
    u1_ref,
    d2_ref,
    n_own,
    n_far,
    *refs,
):
    parts = refs[:pieces]
    outs, scratch = refs[pieces : pieces + 10], refs[pieces + 10 :]
    branch_own, branch_far, gn_own, gn_far = outs[:4]
    m_own, m_far, gf_own, gf_far, gf1_ref, gf2_ref = outs[4:]
    w1_all, w2_all, n_ref, f_ref, gm_ref, branch_ref, gn_ref, m_ref, gf_ref, sems = scratch
    rows = n_ref.shape[0]
    chunk = u1_ref.shape[1]
    at_chunk = pl.ds(pl.multiple_of(pl.program_id(0) * chunk, chunk), chunk)

    @pl.when(pl.program_id(0) == 0)
    def _():
        copies = [
            pltpu.make_async_copy(n_own, n_ref.at[:own, :], sems.at[len(moves)]),
            pltpu.make_async_copy(n_far, n_ref.at[own:, :], sems.at[len(moves) + 1]),
        ]
        for k, (part, start, depth, which) in enumerate(moves):
            width = parts[part].shape[1]
            down = pl.ds(pl.multiple_of(place_ref[0, k] * depth, depth), depth)
            along = pl.ds(pl.multiple_of(place_ref[1, k] * width, width), width)
            copies.append(
                pltpu.make_async_copy(
                    parts[part].at[pl.ds(start, depth), :],
                    (w1_all, w2_all)[which].at[down, along],
                    sems.at[k],
                )
            )
        for copy in copies:
            copy.start()
        branch_ref[...] = jnp.zeros_like(branch_ref)
        gn_ref[...] = jnp.zeros_like(gn_ref)
        m_ref[...] = jnp.zeros_like(m_ref)
        gf_ref[...] = jnp.zeros_like(gf_ref)
        gm_ref[...] = dot_nt(gb_ref[...], up_ref[...]).astype(BF16)
        for copy in copies:
            copy.wait()
        f_ref[...] = dot_nt(n_ref[...], down_ref[...]).astype(BF16)

    gf1_ref[...] = jnp.zeros_like(gf1_ref)
    gf2_ref[...] = jnp.zeros_like(gf2_ref)

    def step(i, carry):
        at = pl.ds(pl.multiple_of(i * block, block), block)
        w1 = w1_all[:, at_chunk]
        w2 = w2_all[:, at_chunk]
        u1 = u1_ref[...]
        d2 = d2_ref[...]
        z = dot(n_ref[at, :], w1) + dot(f_ref[at, :], u1)
        cdf = 0.5 * (1.0 + lax.erf(z * (1.0 / math.sqrt(2.0))))
        a = (z * cdf).astype(BF16)
        slope = cdf + z * (jnp.exp2(z * z * (-0.5 * LOG2E)) * (1.0 / math.sqrt(2.0 * math.pi)))
        ga = dot(gb_ref[at, :], w2) + dot(gm_ref[at, :], d2)
        gz = (ga * slope).astype(BF16)
        branch_ref[at, :] += dot_nt(a, w2)
        m_ref[at, :] += dot_nt(a, d2)
        gn_ref[at, :] += dot_nt(gz, w1)
        gf_ref[at, :] += dot_nt(gz, u1)
        gf1_ref[...] += dot_tn(f_ref[at, :], gz)
        gf2_ref[...] += dot_tn(gm_ref[at, :], a)
        return carry

    lax.fori_loop(0, rows // block, step, 0)

    @pl.when(pl.program_id(0) == pl.num_programs(0) - 1)
    def _():
        branch_own[...] = branch_ref[:own, :]
        branch_far[...] = branch_ref[own:, :].astype(BF16)
        gn_own[...] = gn_ref[:own, :]
        gn_far[...] = gn_ref[own:, :]
        m_own[...] = m_ref[:own, :]
        m_far[...] = m_ref[own:, :]
        gf_own[...] = gf_ref[:own, :]
        gf_far[...] = gf_ref[own:, :]


def mlp(n_own, n_far, gb, down, up, parts, moves, place, u1, d2):
    own, model = n_own.shape
    rows = gb.shape[0]
    hidden = u1.shape[1]
    rank = down.shape[0]
    chunk = min(512, hidden)
    block = min(256, rows)
    whole = lambda shape: pl.BlockSpec(shape, lambda j, place: (0, 0))
    part = lambda depth: pl.BlockSpec((depth, chunk), lambda j, place: (0, j))
    far = rows - own
    shapes = [
        ((own, model), F32),
        ((far, model), BF16),
        ((own, model), F32),
        ((far, model), F32),
        ((own, rank), F32),
        ((far, rank), F32),
        ((own, rank), F32),
        ((far, rank), F32),
    ]
    return pl.pallas_call(
        functools.partial(mlp_kernel, block, own, moves, len(parts)),
        grid_spec=pltpu.PrefetchScalarGridSpec(
            num_scalar_prefetch=1,
            grid=(hidden // chunk,),
            in_specs=[
                whole((rows, model)),
                whole((rank, model)),
                whole((rank, model)),
                part(rank),
                part(rank),
            ]
            + [pl.BlockSpec(memory_space=pl.ANY)] * (2 + len(parts)),
            out_specs=[whole(shape) for shape, _ in shapes] + [part(rank), part(rank)],
            scratch_shapes=[
                pltpu.VMEM((model, hidden), BF16),
                pltpu.VMEM((model, hidden), BF16),
                pltpu.VMEM((rows, model), BF16),
                pltpu.VMEM((rows, rank), BF16),
                pltpu.VMEM((rows, rank), BF16),
                pltpu.VMEM((rows, model), F32),
                pltpu.VMEM((rows, model), F32),
                pltpu.VMEM((rows, rank), F32),
                pltpu.VMEM((rows, rank), F32),
                pltpu.SemaphoreType.DMA((len(moves) + 2,)),
            ],
        ),
        out_shape=[jax.ShapeDtypeStruct(*shape) for shape in shapes]
        + [jax.ShapeDtypeStruct((rank, hidden), F32)] * 2,
        cost_estimate=BRIEF,
        name="mlp",
    )(place, gb, down, up, u1, d2, n_own, n_far, *parts)


def project_kernel(moves, pieces, block, place_ref, n_ref, u_ref, lift_ref, *refs):
    parts, (w_in, w_out, qkv_ref, sems) = refs[:pieces], refs[pieces:]
    copies = []
    column = 0
    for j, out in enumerate((w_in, w_out)):
        width = out.shape[1] // 2
        for k, (part, start, depth) in enumerate(moves):
            down = pl.ds(pl.multiple_of(place_ref[0, k] * depth, depth), depth)
            along = pl.ds(pl.multiple_of(place_ref[1, k] * width, width), width)
            copies.append(
                pltpu.make_async_copy(
                    parts[part].at[pl.ds(start, depth), pl.ds(column, width)],
                    out.at[down, along],
                    sems.at[j, k],
                )
            )
        column += width
    for copy in copies:
        copy.start()
    for copy in copies[: len(moves)]:
        copy.wait()

    def step(i, carry):
        at = pl.ds(pl.multiple_of(i * block, block), block)
        sums = dot(n_ref[at, :], w_in[...]) + dot(u_ref[at, :], lift_ref[...])
        qkv_ref[at, :] = sums.astype(BF16)
        return carry

    lax.fori_loop(0, n_ref.shape[0] // block, step, 0)
    for copy in copies[len(moves) :]:
        copy.wait()


def project(n, u, lift, parts, moves, place, width):
    rows, model = n.shape
    block = min(256, rows)
    whole = lambda shape: pl.BlockSpec(shape, lambda i, place: (0, 0))
    shapes = [(model, 6 * width), (model, 2 * width), (rows, 6 * width)]
    return pl.pallas_call(
        functools.partial(project_kernel, moves, len(parts), block),
        grid_spec=pltpu.PrefetchScalarGridSpec(
            num_scalar_prefetch=1,
            grid=(1,),
            in_specs=[whole(n.shape), whole(u.shape), whole(lift.shape)]
            + [pl.BlockSpec(memory_space=pl.ANY)] * len(parts),
            out_specs=[whole(shape) for shape in shapes],
            scratch_shapes=[pltpu.SemaphoreType.DMA((2, len(moves)))],
        ),
        out_shape=[jax.ShapeDtypeStruct(shape, BF16) for shape in shapes],
        cost_estimate=BRIEF,
        name="project",
    )(place, n, u, lift, *parts)


def pick_kernel(sides, _, *refs):
    sources, outs = refs[: 4 * sides], refs[4 * sides :]
    for far, out in enumerate(outs):
        up, fc1, proj, fc2 = sources[4 * far : 4 * far + 4]
        column = 0
        for piece in [up[0, 0], up[0, 1], up[0, 2], fc1[0], proj[0], fc2[0]]:
            out[:, column : column + piece.shape[1]] = piece
            column += piece.shape[1]


def pick(chosen, ups):
    rank = ups[1].shape[1]
    wide = sum(up.shape[-1] for up in ups) + 2 * ups[0].shape[-1]
    sides = chosen.shape[0]
    specs = [
        pl.BlockSpec(
            (1,) + up.shape[1:],
            lambda i, e, far=far, n=up.ndim: (e[far],) + (0,) * (n - 1),
        )
        for far in range(sides)
        for up in ups
    ]
    return pl.pallas_call(
        functools.partial(pick_kernel, sides),
        grid_spec=pltpu.PrefetchScalarGridSpec(
            num_scalar_prefetch=1,
            grid=(1,),
            in_specs=specs,
            out_specs=[pl.BlockSpec((rank, wide), lambda i, e: (0, 0))] * sides,
        ),
        out_shape=[jax.ShapeDtypeStruct((rank, wide), BF16)] * sides,
        name="pick",
    )(chosen, *(list(ups) * sides))


def lifts_kernel(sizes, *refs):
    packs, (qkv_ref, fc1_ref, proj_ref, fc2_ref) = refs[:-4], refs[-4:]
    rank = fc1_ref.shape[0]
    width, hidden = sizes
    qkv_ref[...] = jnp.zeros_like(qkv_ref)
    for far, pack in enumerate(packs):
        for j in range(3):
            column = (3 * far + j) * width
            qkv_ref[j * rank : (j + 1) * rank, column : column + width] = pack[
                :, j * width : (j + 1) * width
            ]
        start = 3 * width
        for ref, size in ((fc1_ref, hidden), (proj_ref, width), (fc2_ref, hidden)):
            ref[:, far * size : (far + 1) * size] = pack[:, start : start + size]
            start += size


def lifts(packs, width, hidden):
    rank = packs[0].shape[0]
    sides = len(packs)
    shapes = [(3 * rank, 3 * width), (rank, hidden), (rank, width), (rank, hidden)]
    return pl.pallas_call(
        functools.partial(lifts_kernel, (width, hidden)),
        out_shape=[jax.ShapeDtypeStruct((r, sides * c), BF16) for r, c in shapes],
        name="lifts",
    )(*packs)


def totals_kernel(blocks, widths, *refs):
    sources, outs = refs[:blocks], refs[blocks:]
    for out in outs:
        out[...] = jnp.zeros_like(out)
    total = sum(widths)
    for source in sources:
        for k in range(source.shape[0]):
            owner = jnp.max(source[k, :, total:].astype(F32)).astype(jnp.int32)
            column = 0
            for out, width in zip(outs, widths):
                out[owner] += source[k, :, column : column + width].astype(F32)
                column += width


def totals(blocks, widths, adapters):
    rank = blocks[0].shape[1]
    return pl.pallas_call(
        functools.partial(totals_kernel, len(blocks), widths),
        out_shape=[jax.ShapeDtypeStruct((adapters, rank, width), F32) for width in widths],
        name="totals",
    )(*blocks)


def spread_kernel(order, core_ref, *refs):
    halves, target = refs[:-1], refs[-1]
    cut = target.shape[3] // 2
    first = core_ref[0] == 0
    for j, (pair, k) in enumerate(order):
        own = halves[2 * pair][:, :, k * cut : (k + 1) * cut]
        other = halves[2 * pair + 1][:, :, k * cut : (k + 1) * cut]
        target[:, j, :, :cut] = jnp.where(first, own, other)
        target[:, j, :, cut:] = jnp.where(first, other, own)


def spread(core, halves, order, cut):
    adapters, rank, _ = halves[0].shape
    return pl.pallas_call(
        functools.partial(spread_kernel, order),
        in_specs=[pl.BlockSpec(memory_space=pltpu.SMEM)]
        + [pl.BlockSpec(memory_space=pltpu.VMEM)] * len(halves),
        out_shape=jax.ShapeDtypeStruct((adapters, len(order), rank, 2 * cut), F32),
        name="spread",
    )(jnp.reshape(core, (1,)), *halves)


def settle_kernel(count, where_ref, *refs):
    parts, out = refs[:count], refs[-1]
    for k, part in enumerate(parts):

        @pl.when(pl.program_id(0) == k)
        def _():
            out[0] = part[...].astype(out.dtype)


def settle(parts, where, kind, images, base=None):
    rows, model = parts[0].shape
    extra = [] if base is None else [base]
    return pl.pallas_call(
        functools.partial(settle_kernel, len(parts)),
        grid_spec=pltpu.PrefetchScalarGridSpec(
            num_scalar_prefetch=1,
            grid=(len(parts),),
            in_specs=[pl.BlockSpec((rows, model), lambda k, where: (0, 0))] * len(parts)
            + [pl.BlockSpec(memory_space=pl.ANY)] * len(extra),
            out_specs=pl.BlockSpec((1, rows, model), lambda k, where: (where[k], 0, 0)),
        ),
        out_shape=jax.ShapeDtypeStruct((images, rows, model), kind),
        input_output_aliases={1 + len(parts): 0} if extra else {},
        name="settle",
    )(where, *parts, *extra)


def normalize(values, gain, shift):
    centre = values - jnp.mean(values, axis=-1, keepdims=True)
    inverse = lax.rsqrt(jnp.mean(centre * centre, axis=-1, keepdims=True) + EPS)
    unit = centre * inverse
    return unit * gain + shift, unit, inverse


def norm_back(grad, unit, inverse, gain):
    scaled = grad * gain
    centred = scaled - jnp.mean(scaled, axis=-1, keepdims=True)
    return inverse * (centred - unit * jnp.mean(scaled * unit, axis=-1, keepdims=True))


def per_device(
    sizes,
    tokens,
    cotangent,
    adapter_index,
    ln1_gain,
    ln1_bias,
    ln2_gain,
    ln2_bias,
    layer_scale,
    w_qkv,
    w_proj,
    w_fc1,
    w_fc2,
    down_in,
    qkv_up,
    fc1_up,
    proj_down,
    fc2_down,
    out_up,
):
    shards, contexts, tensors = sizes
    half = contexts // 2
    sides = tensors // 2
    images, rows, model = tokens.shape
    rank = down_in.shape[-1]
    depth = w_fc1.shape[0]
    width = w_proj.shape[1]
    hidden = w_fc1.shape[1]
    pairs = width // PAIR
    adapters = down_in.shape[0]
    shard = lax.axis_index("shard")
    context = lax.axis_index("context")
    tensor = lax.axis_index("tensor")
    side, core = tensor // 2, tensor % 2
    high = context // half

    ring = {
        "shard": [(i, (i + 1) % shards) for i in range(shards)],
        "context": [(i, (i + 1) % contexts) for i in range(contexts)],
        "tensor": [(i, (i + 2) % tensors) for i in range(tensors)],
    }
    count = {"shard": shards, "context": contexts, "tensor": sides}
    twin = [(i, i ^ 1) for i in range(tensors)]
    plane = ("context", "tensor")

    def hop(value, axis):
        return lax.ppermute(value, axis, ring[axis])

    def swap(value):
        return lax.ppermute(value, "tensor", twin)

    def around(value, axis):
        out = [value]
        for _ in range(count[axis] - 1):
            out.append(hop(out[-1], axis))
        return out

    def fence(*values):
        return lax.optimization_barrier(values)

    to_owner = []
    to_home = {far: [] for far in range(sides)}
    for c in range(contexts):
        for s in range(sides):
            for k in range(2):
                here = c * tensors + 2 * s + k
                source = 2 * (c % half) + k
                to_owner.append((source * tensors + 2 * s + c // half, here))
                for far in range(sides):
                    there = (s + far) % sides
                    to_home[far].append((here, source * tensors + 2 * there + c // half))

    ringed = contexts == 2 and sides == 2 and shards == 4
    cross = {0: [], 1: []}
    if ringed:
        for c in range(2):
            for s in range(2):
                for k in range(2):
                    here = c * tensors + 2 * s + k
                    along = c * tensors + 2 * (1 - s) + k
                    aside = (1 - c) * tensors + 2 * s + k
                    cross[0].append((here, along if k == 0 else aside))
                    cross[1].append((here, aside if k == 0 else along))

    def block_of(array, index):
        return lax.dynamic_index_in_dim(array, index, 0, keepdims=False)

    def deliver(value, pairs):
        stay = np.zeros(contexts * tensors, np.int32)
        for a, b in pairs:
            stay[a] = a == b
        got = lax.ppermute(value, plane, [(a, b) for a, b in pairs if a != b])
        if not stay.any():
            return got
        return jnp.where(jnp.asarray(stay)[context * tensors + tensor] == 1, value, got)

    def pair_up(a, b):
        return jnp.concatenate([a, b], axis=0)

    def adapter_of(index, far):
        return block_of(index, 2 * ((side + far) % sides) + high)

    def up_packs(index, ups):
        chosen = jnp.stack([adapter_of(index, far) for far in range(sides)])
        packs = list(pick(chosen, ups))
        for far in range(1, sides):
            send = [(i, (i + 2 * far) % tensors) for i in range(tensors)]
            packs[far] = lax.ppermute(packs[far], "tensor", send)
        return packs

    attn_own = jnp.concatenate([w_qkv[:, j] for j in range(3)] + [w_proj], axis=1)
    ups = (qkv_up, fc1_up, jnp.transpose(proj_down, (0, 2, 1)), jnp.transpose(fc2_down, (0, 2, 1)))
    flows = {}

    def cross_to(value, turn):
        return lax.ppermute(value, plane, cross[turn])

    if ringed:
        z, b, c, d = [attn_own], [], [], []
        ff_own = pair_up(w_fc1, w_fc2)
        got = fence(
            hop(attn_own, "shard"),
            cross_to(attn_own, 0),
            cross_to(attn_own, 1),
            deliver(block_of(tokens, tensor), to_owner),
            hop(ff_own, "shard"),
            ff_own,
            cotangent,
            adapter_index,
            down_in,
            out_up,
            *ups,
        )
        z.append(got[0])
        b.append(got[1])
        c.append(got[2])
        x_own = got[3]
        own = [got[5], got[4]]
        cotangent, adapter_index, down_in, out_up = got[6:10]
        ups = got[10:]
        got = fence(
            hop(z[1], "shard"),
            cross_to(z[1], 0),
            cross_to(z[1], 1),
            cross_to(b[0], 1),
            cross_to(own[0], 0),
            x_own,
            own[1],
            adapter_index,
            *ups,
        )
        z.append(got[0])
        b.append(got[1])
        c.append(got[2])
        d.append(got[3])
        aside = [got[4]]
        x_own, own[1], adapter_index = got[5:8]
        ups = got[8:]
        got = fence(
            hop(z[2], "shard"),
            cross_to(z[2], 0),
            cross_to(z[2], 1),
            cross_to(b[1], 1),
            swap(x_own),
            x_own,
            own[1],
            aside[0],
        )
        z.append(got[0])
        b.append(got[1])
        c.append(got[2])
        d.append(got[3])
        x_other, x_own, own[1], aside[0] = got[4:]
        packs = up_packs(adapter_index, ups)
        own.append(hop(own[1], "shard"))
        aside.append(hop(aside[0], "shard"))
        got = fence(cross_to(z[3], 0), cross_to(z[3], 1), cross_to(b[2], 1), cotangent)
        b.append(got[0])
        c.append(got[1])
        d.append(got[2])
        cotangent = got[3]
        last = cross_to(b[3], 1)
        own_over, aside_over = [], []

        step_of = np.repeat(np.arange(shards), 4)
        near_0 = np.tile([0, 0, 1, 1], shards)
        far_0 = np.tile([0, 1, 0, 1], shards)
        near = jnp.where(core == 0, near_0, far_0)
        across = jnp.where(core == 0, far_0, near_0)
        row = (shard - step_of) % shards * contexts + (context - near) % contexts
        attn_place = jnp.stack([row, across]).astype(jnp.int32)
        attn_moves = [(k, 0, depth) for k in range(4 * shards)]
        ff_moves = [(k, which * depth, depth, which) for which in range(2) for k in range(4 * shards)]
        ff_place = jnp.concatenate([attn_place, attn_place], axis=1)
        gy_own = None

        def start(*values):
            got = fence(*values, last, packs[1], own[0], aside[0])
            d.append(got[-4])
            packs[1], own[0], aside[0] = got[-3:]
            own_over.append(cross_to(own[0], 1))
            aside_over.append(cross_to(aside[0], 1))
            return got[:-4]

        def advance(stage, *values):
            count = len(values)
            if stage == 0:
                got = fence(*values, own[2], aside[1], own_over[0], aside_over[0])
                own[2], aside[1], own_over[0], aside_over[0] = got[count:]
                own.append(hop(own[2], "shard"))
                own_over.append(cross_to(own[1], 1))
                aside_over.append(cross_to(aside[1], 1))
            elif stage == 1:
                got = fence(*values, own[3], own_over[1], aside_over[1], aside[1], cotangent)
                own[3], own_over[1], aside_over[1], aside[1], late_cotangent = got[count:]
                aside.append(hop(aside[1], "shard"))
                own_over.append(cross_to(own[2], 1))
                return (*got[:count], deliver(block_of(late_cotangent, tensor), to_owner))
            elif stage == 2:
                got = fence(*values, aside[2], own_over[2])
                aside[2], own_over[2] = got[count:]
                aside.append(hop(aside[2], "shard"))
                own_over.append(cross_to(own[3], 1))
                aside_over.append(cross_to(aside[2], 1))
            else:
                got = fence(*values, aside[3], own_over[3], aside_over[2])
                aside[3], own_over[3], aside_over[2] = got[count:]
                aside_over.append(cross_to(aside[3], 1))
            return got[:count]

    else:

        def gather_plain(value):
            whole = lax.all_gather(value, ("shard", "context"), axis=0, tiled=True)
            return around(whole, "tensor")

        attn_parts = gather_plain(attn_own)
        fc1_parts = gather_plain(w_fc1)
        fc2_parts = gather_plain(w_fc2)
        packs = up_packs(adapter_index, ups)
        x_own = deliver(block_of(tokens, tensor), to_owner)
        x_other = swap(x_own)
        gy_own = deliver(block_of(cotangent, tensor), to_owner)
        attn_moves = [(k, 0, model) for k in range(sides)]
        attn_place = jnp.asarray([[0] * sides, list(range(sides))], jnp.int32)
        ff_moves = [(k, 0, model, k // sides) for k in range(2 * sides)]
        ff_place = jnp.concatenate([attn_place, attn_place], axis=1)

        def start(*values):
            return values

        def advance(stage, *values):
            return (*values, gy_own) if stage == 1 else values

    mine = adapter_of(adapter_index, 0)
    down = block_of(down_in, mine)
    down_t = jnp.transpose(down, (0, 2, 1)).reshape(4 * rank, model)
    out_t = block_of(out_up, mine)

    x_all = pair_up(x_own, x_other).astype(F32)
    normed, unit_one, inverse_one = normalize(x_all, ln1_gain, ln1_bias)
    n1 = normed.astype(BF16)
    u = dot_nt(n1, down_t[: 3 * rank]).astype(BF16)
    n1, u = start(n1, u)
    qkv_lift, fc1_lift, proj_t, fc2_t = lifts(packs, width, hidden)
    if ringed:
        attn_parts = [part for i in range(shards) for part in (z[i], b[i], c[i], d[i])]
    w_in, w_out, qkv = project(n1, u, qkv_lift, attn_parts, attn_moves, attn_place, width)
    (qkv,) = advance(0, qkv)

    steps = [[h * half + i for i in range(half)] for h in range(2)]
    per_side = width // PAIR
    pairs = per_side * sides
    near, group_count = (per_side, sides) if half == 1 else (1, pairs // half)

    def to_heads(array, thirds_each):
        if half == 1:
            return array
        cells = array.reshape(array.shape[0], sides, thirds_each, per_side, PAIR)
        cells = jnp.transpose(cells, (0, 1, 3, 2, 4)).reshape(array.shape[0], pairs, -1)
        moved = lax.all_to_all(cells, "context", 1, 0, axis_index_groups=steps, tiled=True)
        return moved.reshape(moved.shape[0], -1)

    def to_rows(array, thirds_each):
        if half == 1:
            return array
        cells = array.reshape(array.shape[0], pairs // half, -1)
        moved = lax.all_to_all(cells, "context", 0, 1, axis_index_groups=steps, tiled=True)
        moved = moved.reshape(moved.shape[0], sides, per_side, thirds_each, PAIR)
        return jnp.transpose(moved, (0, 1, 3, 2, 4)).reshape(moved.shape[0], -1)

    qkv_heads = to_heads(qkv, 3)
    o_heads = None
    logs = []
    for group in range(group_count):
        o_heads, lse = attend(qkv_heads, group, near, o_heads)
        logs.append(lse)
        if group == 0:
            o_heads, qkv_heads, gy_own = advance(1, o_heads, qkv_heads)
    (o_heads,) = advance(2, o_heads)
    o = to_rows(o_heads, 1)
    attn_far = dot_nt(o[rows:], w_out)
    c_part = dot_nt(o, proj_t)
    attn_sum = swap(attn_far) + dot_nt(o[:rows], w_out)
    c_own = (c_part[:rows] + swap(c_part[rows:])).astype(BF16)
    h = x_all[:rows] + layer_scale[0] * (attn_sum + dot(c_own, out_t[0]))
    normed, unit_two, inverse_two = normalize(h, ln2_gain, ln2_bias)
    n2_own = normed.astype(BF16)
    n2_own, gy_own = advance(3, n2_own, gy_own)
    n2_far = swap(n2_own)
    gy_all = pair_up(gy_own, swap(gy_own))
    gb = (gy_all.astype(F32) * layer_scale[1]).astype(BF16)
    if ringed:
        ff_parts = [
            part
            for i in range(shards)
            for part in (own[i], aside[i], own_over[i], aside_over[i])
        ]
    else:
        ff_parts = fc1_parts + fc2_parts
    branch_own, branch_far, gn2_own, gn2_far, m_part, m_far, gf_part, gf_far, g_fc1, g_fc2 = mlp(
        n2_own, n2_far, gb, down_t[3 * rank :], out_t[1], ff_parts, ff_moves, ff_place, fc1_lift, fc2_t
    )
    m_own = (m_part + swap(m_far)).astype(BF16)
    gf_own = (gf_part + swap(gf_far)).astype(BF16)
    branch = branch_own + swap(branch_far).astype(F32) + dot(m_own, out_t[1])
    result_own = (h + layer_scale[1] * branch).astype(BF16)
    gn2 = gn2_own + swap(gn2_far) + dot(gf_own, down_t[3 * rank :])
    g_out1 = dot_tn(m_own, gb[:rows])
    g_down3 = dot_tn(gf_own, n2_own)

    cut = model // 2
    one = jnp.where(context % half == 0, mine, 0)
    mark = jnp.full((rank, 128), one).astype(BF16)

    def halves(shared):
        shared = jnp.stack(shared)
        away = lax.dynamic_slice_in_dim(shared, (1 - core) * cut, cut, 2)
        keep = lax.dynamic_slice_in_dim(shared, core * cut, cut, 2)
        both = keep + swap(away)
        return [both[j] for j in range(len(both))]

    def to_sides(slices, shared):
        packed = []
        for far in range(sides):
            pack = jnp.concatenate([part.astype(BF16) for part in slices[far] + shared] + [mark], axis=1)
            if far:
                send = [(i, (i - 2 * far) % tensors) for i in range(tensors)]
                pack = lax.ppermute(pack, "tensor", send)
            packed.append(pack)
        return jnp.stack(packed)

    def to_contexts(block):
        if half > 1:
            total = lax.psum(block.astype(F32), "context", axis_index_groups=steps)
            block = total.astype(BF16)
            opposite = [(i, (i + half) % contexts) for i in range(contexts)]
        else:
            opposite = ring["context"]
        return pair_up(block, lax.ppermute(block, "context", opposite))

    def columns(array, far, size):
        return array[:, far * size : (far + 1) * size]

    early = to_sides(
        [[columns(g_fc1, far, hidden), columns(g_fc2, far, hidden)] for far in range(sides)],
        halves([g_down3, g_out1]),
    )
    gh = gy_own.astype(F32) + norm_back(gn2, unit_two, inverse_two, ln2_gain)
    gattn_own = (layer_scale[0] * gh).astype(BF16)
    gattn_own, early = fence(gattn_own, early)
    gattn = pair_up(gattn_own, swap(gattn_own))
    early = to_contexts(early)
    g_out0 = dot_tn(c_own, gattn_own)
    gc = dot_nt(gattn, out_t[0]).astype(BF16)
    g_proj = dot_tn(gc, o)
    mid = to_sides([[columns(g_proj, far, width)] for far in range(sides)], halves([g_out0]))
    go = (dot(gattn, w_out) + dot(gc, proj_t)).astype(BF16)
    early, mid, go = fence(early, mid, go)
    early_line = [early, hop(early, "shard")]
    mid = to_contexts(mid)
    go_heads = to_heads(go, 1)
    g_heads = None
    for group in range(group_count):
        g_heads = attend_back(qkv_heads, go_heads, o_heads, logs[group], group, near, g_heads)
        if group == 0:
            g_heads, early_line[-1], mid, result_own = fence(
                g_heads, early_line[-1], mid, result_own
            )
            early_line.append(hop(early_line[-1], "shard"))
            mid_line = [mid, hop(mid, "shard")]
            sent = [deliver(result_own, to_home[far]) for far in range(sides)]
    g_heads, early_line[-1], mid_line[-1] = fence(g_heads, early_line[-1], mid_line[-1])
    for _ in range(3, shards):
        early_line.append(hop(early_line[-1], "shard"))
    g = to_rows(g_heads, 3)

    gu_part = dot_nt(g, qkv_lift)
    gu_own = (gu_part[:rows] + swap(gu_part[rows:])).astype(BF16)
    gn1_far = swap(dot_nt(g[rows:], w_in))
    g_up = dot_tn(u, g)
    gn1 = dot_nt(g[:rows], w_in) + gn1_far + dot(gu_own, down_t[: 3 * rank])
    g_down = dot_tn(gu_own, n1[:rows])
    late_slices = [
        [
            g_up[j * rank : (j + 1) * rank, (far * 3 + j) * width : (far * 3 + j + 1) * width]
            for j in range(3)
        ]
        for far in range(sides)
    ]
    late = to_sides(late_slices, halves([g_down[j * rank : (j + 1) * rank] for j in range(3)]))
    input_own = gh + norm_back(gn1, unit_one[:rows], inverse_one[:rows], ln1_gain)
    input_own = input_own.astype(BF16)
    late, input_own, early_line[-1], *sent = fence(late, input_own, early_line[-1], *sent)
    late = to_contexts(late)
    mid_line.append(hop(mid_line[-1], "shard"))
    sent += [swap(part) for part in sent]
    late, input_own, mid_line[-1], *sent = fence(late, input_own, mid_line[-1], *sent)

    aways = np.arange(sides)
    mine_at = (2 * ((side - aways) % sides) + core).astype(jnp.int32)
    twin_at = (2 * ((side - aways) % sides) + 1 - core).astype(jnp.int32)
    late_line = [late, hop(late, "shard")]
    input_sent = [deliver(input_own, to_home[far]) for far in range(sides)]
    for _ in range(3, shards):
        mid_line.append(hop(mid_line[-1], "shard"))
    result = settle(sent, jnp.concatenate([mine_at, twin_at]), BF16, images)
    fc1_grad, fc2_grad, early_half = totals(early_line, (hidden, hidden, 2 * cut), adapters)
    late_line[1], early_half, result, *mid_line = fence(
        late_line[1], early_half, result, *mid_line
    )
    for _ in range(2, shards - 1):
        late_line.append(hop(late_line[-1], "shard"))
    early_twin = swap(early_half)
    proj_grad, mid_half = totals(mid_line, (width, cut), adapters)
    mid_twin = swap(mid_half)
    got = fence(late_line[-1], proj_grad, early_half, early_twin, mid_half, mid_twin, *input_sent)
    late_line[-1], proj_grad, early_half, early_twin, mid_half, mid_twin = got[:6]
    input_sent = got[6:]
    if shards > 2:
        late_line.append(hop(late_line[-1], "shard"))
    input_twins = [swap(part) for part in input_sent]
    out_grad = spread(
        core, [mid_half, mid_twin, early_half, early_twin], ((0, 0), (1, 1)), cut
    )
    input_grad = settle(list(input_sent), mine_at, F32, images)
    late_line[-1], input_grad, out_grad, *input_twins = fence(
        late_line[-1], input_grad, out_grad, *input_twins
    )
    qkv_grad, late_half = totals(late_line, (3 * width, 3 * cut), adapters)
    late_twin = swap(late_half)
    input_grad = settle(input_twins, twin_at, F32, images, input_grad)
    down_grad = spread(
        core,
        [late_half, late_twin, early_half, early_twin],
        ((0, 0), (0, 1), (0, 2), (1, 0)),
        cut,
    )
    qkv_grad = jnp.transpose(qkv_grad.reshape(adapters, rank, 3, width), (0, 2, 1, 3))
    return (
        result,
        input_grad,
        jnp.transpose(down_grad, (0, 1, 3, 2)),
        qkv_grad,
        fc1_grad,
        jnp.transpose(proj_grad, (0, 2, 1)),
        jnp.transpose(fc2_grad, (0, 2, 1)),
        out_grad,
    )


def solution(mesh):
    sizes = (mesh.shape["shard"], mesh.shape["context"], mesh.shape["tensor"])
    placed = (
        P("shard", "context", None),
        P("shard", "context", None),
        P("shard"),
        P(),
        P(),
        P(),
        P(),
        P(),
        P(("shard", "context"), None, "tensor"),
        P(("shard", "context"), "tensor"),
        P(("shard", "context"), "tensor"),
        P(("shard", "context"), "tensor"),
        P(),
        P(None, None, None, "tensor"),
        P(None, None, "tensor"),
        P(None, "tensor", None),
        P(None, "tensor", None),
        P(),
    )
    return jax.shard_map(
        functools.partial(per_device, sizes),
        mesh=mesh,
        in_specs=placed,
        out_specs=(
            P("shard", "context", None),
            P("shard", "context", None),
            P(),
            P(None, None, None, "tensor"),
            P(None, None, "tensor"),
            P(None, "tensor", None),
            P(None, "tensor", None),
            P(),
        ),
        check_vma=False,
    )
```

profile of v0, /device:TPU:1, one launch (start us, length us, event | category | flops | bytes accessed | tf_op | source)
XLA Modules:
  0.0 374.8 jit_solution(13632525126045982118)
XLA Ops:
  2.1 4.5 %collective-permute-start.3 = (bf16[512,1024]{1,0:T(8,128)(2,1)S(1)}, bf16[512,1024]{1,0:T(8,128)(2,1)}, u32[]{:S(2)}, u32[]{:S(2)}) collective-permute-start(bf16[512,1024]{1,0:T(8,128)(2,1)S(1)} %dynamic-slice_bitcast_fusion.1), channel_id=1, source_target_pairs={{4,1},{6,3},{1,4},{3,6},{12,9},{14,11},{9,12},{11,14},{20,17},{22,... | collective-permute-start | bytes 3145736 | tf_op jit(solution)/shard_map/ppermute | solution.py:607
  12.0 10.4 %collective-permute-done.3 = bf16[512,1024]{1,0:T(8,128)(2,1)} collective-permute-done((bf16[512,1024]{1,0:T(8,128)(2,1)S(1)}, bf16[512,1024]{1,0:T(8,128)(2,1)}, u32[]{:S(2)}, u32[]{:S(2)}) %collective-permute-start.3) | collective-permute-done | bytes 1048608 | tf_op jit(solution)/shard_map/ppermute | solution.py:607
  29.9 5.8 %collective-permute-done.5.refs_8_ = bf16[128,1024]{1,0:T(8,128)(2,1)} collective-permute-done((bf16[128,1024]{1,0:T(8,128)(2,1)}, bf16[128,1024]{1,0:T(8,128)(2,1)}, u32[]{:S(2)}, u32[]{:S(2)}) %collective-permute-start.5) | collective-permute-done | bytes 262176 | tf_op jit(solution)/shard_map/ppermute | solution.py:562
  35.6 8.0 %collective-permute-done.6.refs_5_ = bf16[128,1024]{1,0:T(8,128)(2,1)} collective-permute-done((bf16[128,1024]{1,0:T(8,128)(2,1)}, bf16[128,1024]{1,0:T(8,128)(2,1)}, u32[]{:S(2)}, u32[]{:S(2)}) %collective-permute-start.6) | collective-permute-done | bytes 262176 | tf_op jit(solution)/shard_map/ppermute | solution.py:631
  71.7 3.4 collective-permute-done.18.refs_15_
  79.8 12.3 %project.1 = (bf16[1024,1536]{1,0:T(8,128)(2,1)}, bf16[1024,512]{1,0:T(8,128)(2,1)}, bf16[1024,1536]{1,0:T(8,128)(2,1)}) custom-call(s32[2,16]{1,0:T(2,128)} %pad_add_fusion.place_ref, bf16[1024,1024]{1,0:T(8,128)(2,1)} %copy-done.7, bf16[1024,48]{1,0:T(8,128)(2,1)} %convolution_convert_fusion.1.u_ref, bf16[48,1536]{1,0:T(8,128)(2,1)} %get-tuple-element.179.lift_ref, ...), custom_call_target="tpu_custom_call" | custom-call | flops 1000 | bytes 1000 | tf_op jit(solution)/shard_map/project/pallas_call | solution.py:351
  94.9 11.2 %attend.2 = (bf16[1024,512]{1,0:T(8,128)(2,1)}, f32[2,8,1024]{2,1,0:T(8,128)}) custom-call(bf16[1024,1536]{1,0:T(8,128)(2,1)} %get-tuple-element.197.q_ref.k_ref.v_ref._, bf16[1024,1536]{1,0:T(8,128)(2,1)} %get-tuple-element.197.q_ref.k_ref.v_ref._, bf16[1024,1536]{1,0:T(8,128)(2,1)} %get-tuple-element.197.q_ref.k_ref.v_ref._, ...), custom_call_target="tpu_custom_call" | custom-call | flops 1000 | bytes 1000 | tf_op jit(solution)/shard_map/attend/pallas_call | solution.py:83
  107.6 11.2 %attend.3 = (bf16[1024,512]{1,0:T(8,128)(2,1)}, f32[2,8,1024]{2,1,0:T(8,128)}) custom-call(bf16[1024,1536]{1,0:T(8,128)(2,1)} %get-tuple-element.197.q_ref.k_ref.v_ref._, bf16[1024,1536]{1,0:T(8,128)(2,1)} %get-tuple-element.197.q_ref.k_ref.v_ref._, bf16[1024,1536]{1,0:T(8,128)(2,1)} %get-tuple-element.197.q_ref.k_ref.v_ref._, ...), custom_call_target="tpu_custom_call", output_to_operand_aliasing={{0}: (3, {})} | custom-call | flops 1000 | bytes 1000 | tf_op jit(solution)/shard_map/attend/pallas_call | solution.py:83
  134.0 16.5 %collective-permute-done.31 = bf16[512,1024]{1,0:T(8,128)(2,1)S(1)} collective-permute-done((bf16[512,1024]{1,0:T(8,128)(2,1)S(1)}, bf16[512,1024]{1,0:T(8,128)(2,1)S(1)}, u32[]{:S(2)}, u32[]{:S(2)}) %collective-permute-start.31) | collective-permute-done | bytes 1048608 | tf_op jit(solution)/shard_map/ppermute | solution.py:607
  161.5 3.5 multiply_convert_fusion.gb_ref
  167.4 37.5 %mlp.1 = (f32[512,1024]{1,0:T(8,128)}, bf16[512,1024]{1,0:T(8,128)(2,1)}, f32[512,1024]{1,0:T(8,128)}, f32[512,1024]{1,0:T(8,128)}, f32[512,16]{1,0:T(8,128)}, /...) custom-call(s32[2,32]{1,0:T(2,128)} %add_add_fusion.place_ref, ...), custom_call_target="tpu_custom_call" | custom-call | flops 1000 | bytes 1000 | tf_op jit(solution)/shard_map/mlp/pallas_call | solution.py:279
  215.0 4.0 %collective-permute-done.42 = bf16[16,3200]{1,0:T(8,128)(2,1)S(1)} collective-permute-done((bf16[16,3200]{1,0:T(8,128)(2,1)S(1)}, bf16[16,3200]{1,0:T(8,128)(2,1)S(1)}, u32[]{:S(2)}, u32[]{:S(2)}) %collective-permute-start.42) | collective-permute-done | bytes 102432 | tf_op jit(solution)/shard_map/ppermute | solution.py:864
  229.4 4.8 %collective-permute-done.43 = bf16[2,16,3200]{2,1,0:T(8,128)(2,1)S(1)} collective-permute-done((bf16[2,16,3200]{2,1,0:T(8,128)(2,1)S(1)}, bf16[2,16,3200]{2,1,0:T(8,128)(2,1)S(1)}, u32[]{:S(2)}, u32[]{:S(2)}) %collective-permute-start.43) | collective-permute-done | bytes 204832 | tf_op jit(solution)/shard_map/ppermute | solution.py:875
  239.3 9.9 %collective-permute-start.47 = (bf16[4,16,3200]{2,1,0:T(8,128)(2,1)S(1)}, bf16[4,16,3200]{2,1,0:T(8,128)(2,1)S(1)}, u32[]{:S(2)}, u32[]{:S(2)}) collective-permute-start(bf16[4,16,3200]{2,1,0:T(8,128)(2,1)S(1)} %pad_maximum_fusion.1.refs_0_), channel_id=1, source_target_pairs={{0,8},{8,16},{16,24},{24,0},{1,9},{9,17},{17,25},{25,1},{2,10},{10... | collective-permute-start | bytes 1228808 | tf_op jit(solution)/shard_map/ppermute | solution.py:562
  250.5 15.5 %attend_back.2._ = bf16[1024,1536]{1,0:T(8,128)(2,1)} custom-call(bf16[1024,1536]{1,0:T(8,128)(2,1)} %get-tuple-element.197.q_ref.k_ref.v_ref._, bf16[1024,1536]{1,0:T(8,128)(2,1)} %get-tuple-element.197.q_ref.k_ref.v_ref._, bf16[1024,1536]{1,0:T(8,128)(2,1)} %get-tuple-element.197.q_ref.k_ref.v_ref._, bf16[1024,512]{1,0:T(8,128)(2,1)} %add_convert_fusion.3.go_ref, ...), custom_call_target="tpu_custom_call" | custom-call | flops 1000 | bytes 1000 | tf_op jit(solution)/shard_map/attend_back/pallas_call | solution.py:156
  266.5 5.4 %collective-permute-start.57 = (bf16[512,1024]{1,0:T(8,128)(2,1)S(1)}, bf16[512,1024]{1,0:T(8,128)(2,1)S(1)}, u32[]{:S(2)}, u32[]{:S(2)}) collective-permute-start(bf16[512,1024]{1,0:T(8,128)(2,1)S(1)} %copy-done.12), channel_id=1, source_target_pairs={{1,4},{3,6},{4,1},{6,3},{9,12},{11,14},{12,9},{14,11},{17,20},{19,... | collective-permute-start | bytes 3145736 | tf_op jit(solution)/shard_map/ppermute | solution.py:607
  272.2 15.4 %attend_back.3 = bf16[1024,1536]{1,0:T(8,128)(2,1)} custom-call(bf16[1024,1536]{1,0:T(8,128)(2,1)} %get-tuple-element.197.q_ref.k_ref.v_ref._, bf16[1024,1536]{1,0:T(8,128)(2,1)} %get-tuple-element.197.q_ref.k_ref.v_ref._, bf16[1024,1536]{1,0:T(8,128)(2,1)} %get-tuple-element.197.q_ref.k_ref.v_ref._, ...), custom_call_target="tpu_custom_call", output_to_operand_aliasing={{}: (6, {})} | custom-call | flops 1000 | bytes 1000 | tf_op jit(solution)/shard_map/attend_back/pallas_call | solution.py:156
  287.7 4.4 %fusion = f32[512,1024]{1,0:T(8,128)S(1)} fusion(bf16[1024,1536]{1,0:T(8,128)(2,1)} %get-tuple-element.241, bf16[1024,1536]{1,0:T(8,128)(2,1)} %attend_back.3), kind=kOutput, calls=%fused_computation.20 | convolution fusion | flops 1610612736 | bytes 6815744 | tf_op jit(solution)/shard_map/dot_general | solution.py:29
  317.5 3.4 collective-permute-start.68
  327.1 5.4 %settle.3 = bf16[4,512,1024]{2,1,0:T(8,128)(2,1)} custom-call(s32[4]{0:T(128)} %pad_add_fusion.2.where_ref, bf16[512,1024]{1,0:T(8,128)(2,1)} %copy-done.13, bf16[512,1024]{1,0:T(8,128)(2,1)} %collective-permute-done.58.refs_1_, bf16[512,1024]{1,0:T(8,128)(2,1)} %copy-done.23, bf16[512,1024]{1,0:T(8,128)(2,1)} %copy-done.24), custom_call_target="tpu_custom_call" | custom-call | tf_op jit(solution)/shard_map/settle/pallas_call | solution.py:487
  339.5 5.7 %collective-permute-done.68 = bf16[512,1024]{1,0:T(8,128)(2,1)} collective-permute-done((bf16[512,1024]{1,0:T(8,128)(2,1)S(1)}, bf16[512,1024]{1,0:T(8,128)(2,1)}, u32[]{:S(2)}, u32[]{:S(2)}) %collective-permute-start.68) | collective-permute-done | bytes 1048608 | tf_op jit(solution)/shard_map/ppermute | solution.py:607
  349.2 4.4 %settle.4.refs_2_ = f32[4,512,1024]{2,1,0:T(8,128)} custom-call(s32[2]{0:T(128)} %copy-done.79, bf16[512,1024]{1,0:T(8,128)(2,1)} %copy-done.14, bf16[512,1024]{1,0:T(8,128)(2,1)} %collective-permute-done.69.refs_1_), custom_call_target="tpu_custom_call" | custom-call | tf_op jit(solution)/shard_map/settle/pallas_call | solution.py:487
  356.0 3.5 collective-permute-done.70.refs_3_
  366.1 4.5 %settle.5 = f32[4,512,1024]{2,1,0:T(8,128)} custom-call(s32[2]{0:T(128)} %copy-done.75, bf16[512,1024]{1,0:T(8,128)(2,1)} %copy-done.27, bf16[512,1024]{1,0:T(8,128)(2,1)} %collective-permute-done.72.refs_1_, f32[4,512,1024]{2,1,0:T(8,128)} %settle.4.refs_2_), custom_call_target="tpu_custom_call", output_to_operand_aliasing={{}: (3, {})} | custom-call | tf_op jit(solution)/shard_map/settle/pallas_call | solution.py:487
  (409 shorter events, 158.8 us)
Async XLA Ops:
  2.1 20.2 %collective-permute-start.3 = (bf16[512,1024]{1,0:T(8,128)(2,1)S(1)}, bf16[512,1024]{1,0:T(8,128)(2,1)}, u32[]{:S(2)}, u32[]{:S(2)}) collective-permute-start(bf16[512,1024]{1,0:T(8,128)(2,1)S(1)} %dynamic-slice_bitcast_fusion.1), channel_id=1, source_target_pairs={{4,1},{6,3},{1,4},{3,6},{12,9},{14,11},{9,12},{11,14},{20,17},{22,... | collective-permute-start | bytes 3145736 | tf_op jit(solution)/shard_map/ppermute | solution.py:607
  6.8 20.1 %collective-permute-start.4 = (bf16[256,1024]{1,0:T(8,128)(2,1)S(1)}, bf16[256,1024]{1,0:T(8,128)(2,1)S(1)}, u32[]{:S(2)}, u32[]{:S(2)}) collective-permute-start(bf16[256,1024]{1,0:T(8,128)(2,1)S(1)} %constant_dynamic-update-slice_fusion.refs_0_), channel_id=1, source_target_pairs={{0,8},{8,16},{16,24},{24,0},{1,9},{9,17},{17,25},{25,1},{2,10},{10... | collective-permute-start | bytes 1572872 | tf_op jit(solution)/shard_map/ppermute | solution.py:562
  8.2 18.6 %collective-permute-start = (bf16[128,1024]{1,0:T(8,128)(2,1)S(1)}, bf16[128,1024]{1,0:T(8,128)(2,1)}, u32[]{:S(2)}, u32[]{:S(2)}) collective-permute-start(bf16[128,1024]{1,0:T(8,128)(2,1)S(1)} %pad_maximum_fusion.3.refs_0_), channel_id=1, source_target_pairs={{0,8},{8,16},{16,24},{24,0},{1,9},{9,17},{17,25},{25,1},{2,10},{10... | collective-permute-start | bytes 786440 | tf_op jit(solution)/shard_map/ppermute | solution.py:562
  9.5 17.3 %collective-permute-start.1 = (bf16[128,1024]{1,0:T(8,128)(2,1)S(1)}, bf16[128,1024]{1,0:T(8,128)(2,1)}, u32[]{:S(2)}, u32[]{:S(2)}) collective-permute-start(bf16[128,1024]{1,0:T(8,128)(2,1)S(1)} %pad_maximum_fusion.3.refs_0_), channel_id=1, source_target_pairs={{0,2},{1,5},{2,0},{3,7},{4,6},{5,1},{6,4},{7,3},{8,10},{9,13},{10,... | collective-permute-start | bytes 786440 | tf_op jit(solution)/shard_map/ppermute | solution.py:631
  9.5 17.3 %collective-permute-start.2 = (bf16[128,1024]{1,0:T(8,128)(2,1)S(1)}, bf16[128,1024]{1,0:T(8,128)(2,1)}, u32[]{:S(2)}, u32[]{:S(2)}) collective-permute-start(bf16[128,1024]{1,0:T(8,128)(2,1)S(1)} %pad_maximum_fusion.3.refs_0_), channel_id=1, source_target_pairs={{0,4},{1,3},{2,6},{3,1},{4,0},{5,7},{6,2},{7,5},{8,12},{9,11},{10,... | collective-permute-start | bytes 786440 | tf_op jit(solution)/shard_map/ppermute | solution.py:631
  26.9 16.9 %collective-permute-start.9 = (bf16[256,1024]{1,0:T(8,128)(2,1)S(1)}, bf16[256,1024]{1,0:T(8,128)(2,1)}, u32[]{:S(2)}, u32[]{:S(2)}) collective-permute-start(bf16[256,1024]{1,0:T(8,128)(2,1)S(1)} %constant_dynamic-update-slice_fusion.refs_0_), channel_id=1, source_target_pairs={{0,2},{1,5},{2,0},{3,7},{4,6},{5,1},{6,4},{7,3},{8,10},{9,13},{10,... | collective-permute-start | bytes 1572872 | tf_op jit(solution)/shard_map/ppermute | solution.py:631
  60.5 31.6 %collective-permute-start.20 = (bf16[256,1024]{1,0:T(8,128)(2,1)S(1)}, bf16[256,1024]{1,0:T(8,128)(2,1)}, u32[]{:S(2)}, u32[]{:S(2)}) collective-permute-start(bf16[256,1024]{1,0:T(8,128)(2,1)S(1)} %copy-done.31), channel_id=1, source_target_pairs={{0,8},{8,16},{16,24},{24,0},{1,9},{9,17},{17,25},{25,1},{2,10},{10... | collective-permute-start | bytes 1572872 | tf_op jit(solution)/shard_map/ppermute | solution.py:562
  65.0 27.1 %collective-permute-start.21 = (bf16[256,1024]{1,0:T(8,128)(2,1)}, bf16[256,1024]{1,0:T(8,128)(2,1)S(1)}, u32[]{:S(2)}, u32[]{:S(2)}) collective-permute-start(bf16[256,1024]{1,0:T(8,128)(2,1)} %collective-permute-done.9.refs_1_), channel_id=1, source_target_pairs={{0,8},{8,16},{16,24},{24,0},{1,9},{9,17},{17,25},{25,1},{2,10},{10... | collective-permute-start | bytes 1572872 | tf_op jit(solution)/shard_map/ppermute | solution.py:562
  75.1 17.0 %collective-permute-start.22 = (bf16[256,1024]{1,0:T(8,128)(2,1)S(1)}, bf16[256,1024]{1,0:T(8,128)(2,1)S(1)}, u32[]{:S(2)}, u32[]{:S(2)}) collective-permute-start(bf16[256,1024]{1,0:T(8,128)(2,1)S(1)} %copy-done.22), channel_id=1, source_target_pairs={{0,4},{1,3},{2,6},{3,1},{4,0},{5,7},{6,2},{7,5},{8,12},{9,11},{10,... | collective-permute-start | bytes 1572872 | tf_op jit(solution)/shard_map/ppermute | solution.py:631
  77.3 28.9 %collective-permute-start.25 = (bf16[256,1024]{1,0:T(8,128)(2,1)S(1)}, bf16[256,1024]{1,0:T(8,128)(2,1)}, u32[]{:S(2)}, u32[]{:S(2)}) collective-permute-start(bf16[256,1024]{1,0:T(8,128)(2,1)S(1)} %copy-done.31), channel_id=1, source_target_pairs={{0,4},{1,3},{2,6},{3,1},{4,0},{5,7},{6,2},{7,5},{8,12},{9,11},{10,... | collective-permute-start | bytes 1572872 | tf_op jit(solution)/shard_map/ppermute | solution.py:631
  94.2 24.7 %collective-permute-start.28 = (bf16[256,1024]{1,0:T(8,128)(2,1)}, bf16[256,1024]{1,0:T(8,128)(2,1)}, u32[]{:S(2)}, u32[]{:S(2)}) collective-permute-start(bf16[256,1024]{1,0:T(8,128)(2,1)} %collective-permute-done.20.refs_8_), channel_id=1, source_target_pairs={{0,4},{1,3},{2,6},{3,1},{4,0},{5,7},{6,2},{7,5},{8,12},{9,11},{10,... | collective-permute-start | bytes 1572872 | tf_op jit(solution)/shard_map/ppermute | solution.py:631
  122.3 30.5 %collective-permute-start.29 = (f32[512,1024]{1,0:T(8,128)S(1)}, f32[512,1024]{1,0:T(8,128)S(1)}, u32[]{:S(2)}, u32[]{:S(2)}) collective-permute-start(f32[512,1024]{1,0:T(8,128)S(1)} %fusion.9), channel_id=1, source_target_pairs={{0,1},{1,0},{2,3},{3,2},{4,5},{5,4},{6,7},{7,6},{8,9},{9,8},{10,11... | collective-permute-start | bytes 6291464 | tf_op jit(solution)/shard_map/ppermute | solution.py:565
  126.4 24.1 %collective-permute-start.31 = (bf16[512,1024]{1,0:T(8,128)(2,1)S(1)}, bf16[512,1024]{1,0:T(8,128)(2,1)S(1)}, u32[]{:S(2)}, u32[]{:S(2)}) collective-permute-start(bf16[512,1024]{1,0:T(8,128)(2,1)S(1)} %dynamic-slice_bitcast_fusion), channel_id=1, source_target_pairs={{4,1},{6,3},{1,4},{3,6},{12,9},{14,11},{9,12},{11,14},{20,17},{22,... | collective-permute-start | bytes 3145736 | tf_op jit(solution)/shard_map/ppermute | solution.py:607
  130.8 25.7 %collective-permute-start.33 = (bf16[256,1024]{1,0:T(8,128)(2,1)S(1)}, bf16[256,1024]{1,0:T(8,128)(2,1)S(1)}, u32[]{:S(2)}, u32[]{:S(2)}) collective-permute-start(bf16[256,1024]{1,0:T(8,128)(2,1)S(1)} %copy-done.35), channel_id=1, source_target_pairs={{0,4},{1,3},{2,6},{3,1},{4,0},{5,7},{6,2},{7,5},{8,12},{9,11},{10,... | collective-permute-start | bytes 1572872 | tf_op jit(solution)/shard_map/ppermute | solution.py:631
  132.8 23.7 %collective-permute-start.32 = (bf16[256,1024]{1,0:T(8,128)(2,1)S(1)}, bf16[256,1024]{1,0:T(8,128)(2,1)}, u32[]{:S(2)}, u32[]{:S(2)}) collective-permute-start(bf16[256,1024]{1,0:T(8,128)(2,1)S(1)} %copy-done.37), channel_id=1, source_target_pairs={{0,8},{8,16},{16,24},{24,0},{1,9},{9,17},{17,25},{25,1},{2,10},{10... | collective-permute-start | bytes 1572872 | tf_op jit(solution)/shard_map/ppermute | solution.py:562
  133.1 23.4 %collective-permute-start.34 = (bf16[256,1024]{1,0:T(8,128)(2,1)S(1)}, bf16[256,1024]{1,0:T(8,128)(2,1)S(1)}, u32[]{:S(2)}, u32[]{:S(2)}) collective-permute-start(bf16[256,1024]{1,0:T(8,128)(2,1)S(1)} %copy-done.37), channel_id=1, source_target_pairs={{0,4},{1,3},{2,6},{3,1},{4,0},{5,7},{6,2},{7,5},{8,12},{9,11},{10,... | collective-permute-start | bytes 1572872 | tf_op jit(solution)/shard_map/ppermute | solution.py:631
  239.3 26.7 %collective-permute-start.47 = (bf16[4,16,3200]{2,1,0:T(8,128)(2,1)S(1)}, bf16[4,16,3200]{2,1,0:T(8,128)(2,1)S(1)}, u32[]{:S(2)}, u32[]{:S(2)}) collective-permute-start(bf16[4,16,3200]{2,1,0:T(8,128)(2,1)S(1)} %pad_maximum_fusion.1.refs_0_), channel_id=1, source_target_pairs={{0,8},{8,16},{16,24},{24,0},{1,9},{9,17},{17,25},{25,1},{2,10},{10... | collective-permute-start | bytes 1228808 | tf_op jit(solution)/shard_map/ppermute | solution.py:562
  249.2 16.7 %collective-permute-start.48 = (bf16[2,16,896]{2,1,0:T(8,128)(2,1)S(1)}, bf16[2,16,896]{2,1,0:T(8,128)(2,1)S(1)}, u32[]{:S(2)}, u32[]{:S(2)}) collective-permute-start(bf16[2,16,896]{2,1,0:T(8,128)(2,1)S(1)} %pad_maximum_fusion.8), channel_id=1, source_target_pairs={{0,4},{4,0},{1,5},{5,1},{2,6},{6,2},{3,7},{7,3},{8,12},{12,8},{9,1... | collective-permute-start | bytes 172040 | tf_op jit(solution)/shard_map/ppermute | solution.py:875
  266.0 21.6 %collective-permute-start.50 = (bf16[4,16,3200]{2,1,0:T(8,128)(2,1)S(1)}, bf16[4,16,3200]{2,1,0:T(8,128)(2,1)S(1)}, u32[]{:S(2)}, u32[]{:S(2)}) collective-permute-start(bf16[4,16,3200]{2,1,0:T(8,128)(2,1)S(1)} %collective-permute-done.47.refs_1_), channel_id=1, source_target_pairs={{0,8},{8,16},{16,24},{24,0},{1,9},{9,17},{17,25},{25,1},{2,10},{10... | collective-permute-start | bytes 1228808 | tf_op jit(solution)/shard_map/ppermute | solution.py:562
  266.1 21.5 %collective-permute-start.51 = (bf16[4,16,896]{2,1,0:T(8,128)(2,1)S(1)}, bf16[4,16,896]{2,1,0:T(8,128)(2,1)S(1)}, u32[]{:S(2)}, u32[]{:S(2)}) collective-permute-start(bf16[4,16,896]{2,1,0:T(8,128)(2,1)S(1)} %pad_maximum_fusion.7.refs_0_), channel_id=1, source_target_pairs={{0,8},{8,16},{16,24},{24,0},{1,9},{9,17},{17,25},{25,1},{2,10},{10... | collective-permute-start | bytes 344072 | tf_op jit(solution)/shard_map/ppermute | solution.py:562
  266.5 39.3 %collective-permute-start.57 = (bf16[512,1024]{1,0:T(8,128)(2,1)S(1)}, bf16[512,1024]{1,0:T(8,128)(2,1)S(1)}, u32[]{:S(2)}, u32[]{:S(2)}) collective-permute-start(bf16[512,1024]{1,0:T(8,128)(2,1)S(1)} %copy-done.12), channel_id=1, source_target_pairs={{1,4},{3,6},{4,1},{6,3},{9,12},{11,14},{12,9},{14,11},{17,20},{19,... | collective-permute-start | bytes 3145736 | tf_op jit(solution)/shard_map/ppermute | solution.py:607
  271.9 37.2 %collective-permute-start.58 = (bf16[512,1024]{1,0:T(8,128)(2,1)S(1)}, bf16[512,1024]{1,0:T(8,128)(2,1)}, u32[]{:S(2)}, u32[]{:S(2)}) collective-permute-start(bf16[512,1024]{1,0:T(8,128)(2,1)S(1)} %copy-done.12), channel_id=1, source_target_pairs={{0,2},{1,6},{2,0},{3,4},{4,3},{5,7},{6,1},{7,5},{8,10},{9,14},{10,... | collective-permute-start | bytes 3145736 | tf_op jit(solution)/shard_map/ppermute | solution.py:607
  317.5 27.8 %collective-permute-start.68 = (bf16[512,1024]{1,0:T(8,128)(2,1)S(1)}, bf16[512,1024]{1,0:T(8,128)(2,1)}, u32[]{:S(2)}, u32[]{:S(2)}) collective-permute-start(bf16[512,1024]{1,0:T(8,128)(2,1)S(1)} %add_convert_fusion.1), channel_id=1, source_target_pairs={{1,4},{3,6},{4,1},{6,3},{9,12},{11,14},{12,9},{14,11},{17,20},{19,... | collective-permute-start | bytes 3145736 | tf_op jit(solution)/shard_map/ppermute | solution.py:607
  320.9 27.3 %collective-permute-start.69 = (bf16[512,1024]{1,0:T(8,128)(2,1)S(1)}, bf16[512,1024]{1,0:T(8,128)(2,1)}, u32[]{:S(2)}, u32[]{:S(2)}) collective-permute-start(bf16[512,1024]{1,0:T(8,128)(2,1)S(1)} %add_convert_fusion.1), channel_id=1, source_target_pairs={{0,2},{1,6},{2,0},{3,4},{4,3},{5,7},{6,1},{7,5},{8,10},{9,14},{10,... | collective-permute-start | bytes 3145736 | tf_op jit(solution)/shard_map/ppermute | solution.py:607
  (133 other events, 1133.9 us)
where the time goes:
time: 380 us; the launch traced here: 375 us
  Pallas kernels  134 us (35%)
  waiting for transfers between devices  87.3 us (23%)
  starting transfers between devices  78.7 us (21%)
  other arithmetic  25.8 us (7%)
  matrix products  25.1 us (7%)
  local copies, waits for them, and re-layouts  18.1 us (5%)
  between operations  5.39 us (1%)
    pallas_call x1, Pallas kernels, mlp(): pl.pallas_call(functools.partial(mlp_kernel, block, own, moves, len(parts...  37.5 us
    ppermute x6, waiting for transfers between devices, deliver(): got = lax.ppermute(value, plane, [(a, b) for a, b in pairs if a != b])  32.6 us
    pallas_call x2, Pallas kernels, attend_back(): pl.pallas_call(functools.partial(attend_back_kernel, block, near), grid=(...  30.9 us
    ppermute x18, starting transfers between devices, hop(): return lax.ppermute(value, axis, ring[axis])  26.4 us
    pallas_call x2, Pallas kernels, attend(): pl.pallas_call(functools.partial(attend_kernel, block), grid=(near,), in_...  22.5 us
    ppermute x18, waiting for transfers between devices, hop(): return lax.ppermute(value, axis, ring[axis])  21 us
    ppermute x21, waiting for transfers between devices, cross_to(): return lax.ppermute(value, plane, cross[turn])  17.9 us
    ppermute x6, starting transfers between devices, deliver(): got = lax.ppermute(value, plane, [(a, b) for a, b in pairs if a != b])  17.8 us
  transfers between devices with their start and end apart: 74, of which 27 were waited for; matrix products, arithmetic and copies ran while one was open for 13% of the time, Pallas kernels for 24%

commit v1 on v0

--- a/solution.py
+++ b/solution.py
@@ -183,42 +183,45 @@
     *refs,
 ):
     parts = refs[:pieces]
-    outs, scratch = refs[pieces : pieces + 10], refs[pieces + 10 :]
+    outs, scratch = refs[pieces : pieces + 8], refs[pieces + 8 :]
     branch_own, branch_far, gn_own, gn_far = outs[:4]
-    m_own, m_far, gf_own, gf_far, gf1_ref, gf2_ref = outs[4:]
-    w1_all, w2_all, n_ref, f_ref, gm_ref, branch_ref, gn_ref, m_ref, gf_ref, sems = scratch
+    rank_own, rank_far, gf1_out, gf2_out = outs[4:]
+    w1_all, w2_all, n_ref, f_ref, gm_ref, branch_ref, gn_ref = scratch[:7]
+    rank_ref, gf1_ref, gf2_ref, sems, row_sems = scratch[7:]
+    rank = f_ref.shape[0]
     rows = n_ref.shape[0]
     chunk = u1_ref.shape[1]
     at_chunk = pl.ds(pl.multiple_of(pl.program_id(0) * chunk, chunk), chunk)
 
     @pl.when(pl.program_id(0) == 0)
     def _():
-        copies = [
-            pltpu.make_async_copy(n_own, n_ref.at[:own, :], sems.at[len(moves)]),
-            pltpu.make_async_copy(n_far, n_ref.at[own:, :], sems.at[len(moves) + 1]),
+        rows_in = [
+            pltpu.make_async_copy(n_own, n_ref.at[:own, :], row_sems.at[0]),
+            pltpu.make_async_copy(n_far, n_ref.at[own:, :], row_sems.at[1]),
         ]
-        for k, (part, start, depth, which) in enumerate(moves):
-            width = parts[part].shape[1]
-            down = pl.ds(pl.multiple_of(place_ref[0, k] * depth, depth), depth)
-            along = pl.ds(pl.multiple_of(place_ref[1, k] * width, width), width)
-            copies.append(
+        for copy in rows_in:
+            copy.start()
+        for split in range(parts[0].shape[1] // chunk):
+            for k, (part, start, depth, which) in enumerate(moves):
+                number = place_ref[1, k] * (parts[part].shape[1] // chunk) + split
+                down = pl.ds(pl.multiple_of(place_ref[0, k] * depth, depth), depth)
+                along = pl.ds(pl.multiple_of(number * chunk, chunk), chunk)
                 pltpu.make_async_copy(
-                    parts[part].at[pl.ds(start, depth), :],
+                    parts[part].at[pl.ds(start, depth), pl.ds(split * chunk, chunk)],
                     (w1_all, w2_all)[which].at[down, along],
-                    sems.at[k],
-                )
-            )
-        for copy in copies:
-            copy.start()
+                    sems.at[which, number],
+                ).start()
         branch_ref[...] = jnp.zeros_like(branch_ref)
         gn_ref[...] = jnp.zeros_like(gn_ref)
-        m_ref[...] = jnp.zeros_like(m_ref)
-        gf_ref[...] = jnp.zeros_like(gf_ref)
-        gm_ref[...] = dot_nt(gb_ref[...], up_ref[...]).astype(BF16)
-        for copy in copies:
+        rank_ref[...] = jnp.zeros_like(rank_ref)
+        gm_ref[...] = dot_nt(up_ref[...], gb_ref[...]).astype(BF16)
+        for copy in rows_in:
             copy.wait()
-        f_ref[...] = dot_nt(n_ref[...], down_ref[...]).astype(BF16)
-
+        f_ref[...] = dot_nt(down_ref[...], n_ref[...]).astype(BF16)
+
+    for which, target in enumerate((w1_all, w2_all)):
+        area = target.at[:, at_chunk]
+        pltpu.make_async_copy(area, area, sems.at[which, pl.program_id(0)]).wait()
     gf1_ref[...] = jnp.zeros_like(gf1_ref)
     gf2_ref[...] = jnp.zeros_like(gf2_ref)
 
@@ -228,32 +231,32 @@
         w2 = w2_all[:, at_chunk]
         u1 = u1_ref[...]
         d2 = d2_ref[...]
-        z = dot(n_ref[at, :], w1) + dot(f_ref[at, :], u1)
+        z = dot(n_ref[at, :], w1) + dot_tn(f_ref[:, at], u1)
         cdf = 0.5 * (1.0 + lax.erf(z * (1.0 / math.sqrt(2.0))))
         a = (z * cdf).astype(BF16)
         slope = cdf + z * (jnp.exp2(z * z * (-0.5 * LOG2E)) * (1.0 / math.sqrt(2.0 * math.pi)))
-        ga = dot(gb_ref[at, :], w2) + dot(gm_ref[at, :], d2)
+        ga = dot(gb_ref[at, :], w2) + dot_tn(gm_ref[:, at], d2)
         gz = (ga * slope).astype(BF16)
         branch_ref[at, :] += dot_nt(a, w2)
-        m_ref[at, :] += dot_nt(a, d2)
+        rank_ref[:rank, at] += dot_nt(d2, a)
         gn_ref[at, :] += dot_nt(gz, w1)
-        gf_ref[at, :] += dot_nt(gz, u1)
-        gf1_ref[...] += dot_tn(f_ref[at, :], gz)
-        gf2_ref[...] += dot_tn(gm_ref[at, :], a)
+        rank_ref[rank:, at] += dot_nt(u1, gz)
+        gf1_ref[...] += dot(f_ref[:, at], gz)
+        gf2_ref[...] += dot(gm_ref[:, at], a)
         return carry
 
     lax.fori_loop(0, rows // block, step, 0)
+    gf1_out[...] = gf1_ref[...].astype(BF16)
+    gf2_out[...] = gf2_ref[...].astype(BF16)
 
     @pl.when(pl.program_id(0) == pl.num_programs(0) - 1)
     def _():
+        rank_own[...] = rank_ref[:, :own]
+        rank_far[...] = rank_ref[:, own:]
         branch_own[...] = branch_ref[:own, :]
         branch_far[...] = branch_ref[own:, :].astype(BF16)
         gn_own[...] = gn_ref[:own, :]
         gn_far[...] = gn_ref[own:, :]
-        m_own[...] = m_ref[:own, :]
-        m_far[...] = m_ref[own:, :]
-        gf_own[...] = gf_ref[:own, :]
-        gf_far[...] = gf_ref[own:, :]
 
 
 def mlp(n_own, n_far, gb, down, up, parts, moves, place, u1, d2):
@@ -271,10 +274,8 @@
         ((far, model), BF16),
         ((own, model), F32),
         ((far, model), F32),
-        ((own, rank), F32),
-        ((far, rank), F32),
-        ((own, rank), F32),
-        ((far, rank), F32),
+        ((2 * rank, own), F32),
+        ((2 * rank, far), F32),
     ]
     return pl.pallas_call(
         functools.partial(mlp_kernel, block, own, moves, len(parts)),
@@ -294,69 +295,92 @@
                 pltpu.VMEM((model, hidden), BF16),
                 pltpu.VMEM((model, hidden), BF16),
                 pltpu.VMEM((rows, model), BF16),
-                pltpu.VMEM((rows, rank), BF16),
-                pltpu.VMEM((rows, rank), BF16),
+                pltpu.VMEM((rank, rows), BF16),
+                pltpu.VMEM((rank, rows), BF16),
                 pltpu.VMEM((rows, model), F32),
                 pltpu.VMEM((rows, model), F32),
-                pltpu.VMEM((rows, rank), F32),
-                pltpu.VMEM((rows, rank), F32),
-                pltpu.SemaphoreType.DMA((len(moves) + 2,)),
+                pltpu.VMEM((2 * rank, rows), F32),
+                pltpu.VMEM((rank, chunk), F32),
+                pltpu.VMEM((rank, chunk), F32),
+                pltpu.SemaphoreType.DMA((2, hidden // chunk)),
+                pltpu.SemaphoreType.DMA((2,)),
             ],
         ),
         out_shape=[jax.ShapeDtypeStruct(*shape) for shape in shapes]
-        + [jax.ShapeDtypeStruct((rank, hidden), F32)] * 2,
+        + [jax.ShapeDtypeStruct((rank, hidden), BF16)] * 2,
         cost_estimate=BRIEF,
         name="mlp",
     )(place, gb, down, up, u1, d2, n_own, n_far, *parts)
 
 
-def project_kernel(moves, pieces, block, place_ref, n_ref, u_ref, lift_ref, *refs):
-    parts, (w_in, w_out, qkv_ref, sems) = refs[:pieces], refs[pieces:]
-    copies = []
-    column = 0
-    for j, out in enumerate((w_in, w_out)):
-        width = out.shape[1] // 2
-        for k, (part, start, depth) in enumerate(moves):
-            down = pl.ds(pl.multiple_of(place_ref[0, k] * depth, depth), depth)
-            along = pl.ds(pl.multiple_of(place_ref[1, k] * width, width), width)
-            copies.append(
-                pltpu.make_async_copy(
+def project_kernel(moves, pieces, place_ref, n_ref, u_ref, lift_ref, *refs):
+    parts, (w_in, w_out, qkv_ref, in_all, out_all, sems, back) = refs[:pieces], refs[pieces:]
+
+    def copies():
+        column = 0
+        for j, target in enumerate((in_all, out_all)):
+            width = target.shape[1] // 2
+            for k, (part, start, depth) in enumerate(moves):
+                down = pl.ds(pl.multiple_of(place_ref[0, k] * depth, depth), depth)
+                along = pl.ds(pl.multiple_of(place_ref[1, k] * width, width), width)
+                yield pltpu.make_async_copy(
                     parts[part].at[pl.ds(start, depth), pl.ds(column, width)],
-                    out.at[down, along],
+                    target.at[down, along],
                     sems.at[j, k],
                 )
-            )
-        column += width
-    for copy in copies:
-        copy.start()
-    for copy in copies[: len(moves)]:
-        copy.wait()
-
-    def step(i, carry):
-        at = pl.ds(pl.multiple_of(i * block, block), block)
-        sums = dot(n_ref[at, :], w_in[...]) + dot(u_ref[at, :], lift_ref[...])
-        qkv_ref[at, :] = sums.astype(BF16)
-        return carry
-
-    lax.fori_loop(0, n_ref.shape[0] // block, step, 0)
-    for copy in copies[len(moves) :]:
-        copy.wait()
+            column += width
+
+    backs = [
+        pltpu.make_async_copy(in_all, w_in, back.at[0]),
+        pltpu.make_async_copy(out_all, w_out, back.at[1]),
+    ]
+
+    @pl.when(pl.program_id(0) == 0)
+    def _():
+        pending = list(copies())
+        for copy in pending:
+            copy.start()
+        for copy in pending:
+            copy.wait()
+        for copy in backs:
+            copy.start()
+
+    sums = dot(n_ref[...], in_all[...]) + dot_tn(u_ref[...], lift_ref[...])
+    qkv_ref[...] = sums.astype(BF16)
+
+    @pl.when(pl.program_id(0) == pl.num_programs(0) - 1)
+    def _():
+        for copy in backs:
+            copy.wait()
 
 
 def project(n, u, lift, parts, moves, place, width):
     rows, model = n.shape
     block = min(256, rows)
-    whole = lambda shape: pl.BlockSpec(shape, lambda i, place: (0, 0))
+    anywhere = pl.BlockSpec(memory_space=pl.ANY)
     shapes = [(model, 6 * width), (model, 2 * width), (rows, 6 * width)]
     return pl.pallas_call(
-        functools.partial(project_kernel, moves, len(parts), block),
+        functools.partial(project_kernel, moves, len(parts)),
         grid_spec=pltpu.PrefetchScalarGridSpec(
             num_scalar_prefetch=1,
-            grid=(1,),
-            in_specs=[whole(n.shape), whole(u.shape), whole(lift.shape)]
-            + [pl.BlockSpec(memory_space=pl.ANY)] * len(parts),
-            out_specs=[whole(shape) for shape in shapes],
-            scratch_shapes=[pltpu.SemaphoreType.DMA((2, len(moves)))],
+            grid=(rows // block,),
+            in_specs=[
+                pl.BlockSpec((block, model), lambda i, place: (i, 0)),
+                pl.BlockSpec((u.shape[0], block), lambda i, place: (0, i)),
+                pl.BlockSpec(lift.shape, lambda i, place: (0, 0)),
+            ]
+            + [anywhere] * len(parts),
+            out_specs=[
+                anywhere,
+                anywhere,
+                pl.BlockSpec((block, 6 * width), lambda i, place: (i, 0)),
+            ],
+            scratch_shapes=[
+                pltpu.VMEM((model, 6 * width), BF16),
+                pltpu.VMEM((model, 2 * width), BF16),
+                pltpu.SemaphoreType.DMA((2, len(moves))),
+                pltpu.SemaphoreType.DMA((2,)),
+            ],
         ),
         out_shape=[jax.ShapeDtypeStruct(shape, BF16) for shape in shapes],
         cost_estimate=BRIEF,
@@ -437,15 +461,29 @@
             owner = jnp.max(source[k, :, total:].astype(F32)).astype(jnp.int32)
             column = 0
             for out, width in zip(outs, widths):
-                out[owner] += source[k, :, column : column + width].astype(F32)
-                column += width
-
-
-def totals(blocks, widths, adapters):
+                split = out.shape[1] if len(out.shape) == 4 else 1
+                for j in range(split):
+                    part = source[k, :, column : column + width // split].astype(F32)
+                    if split > 1:
+                        out[owner, j] += part
+                    else:
+                        out[owner] += part
+                    column += width // split
+
+
+def totals(blocks, widths, adapters, split=1):
     rank = blocks[0].shape[1]
     return pl.pallas_call(
         functools.partial(totals_kernel, len(blocks), widths),
-        out_shape=[jax.ShapeDtypeStruct((adapters, rank, width), F32) for width in widths],
+        out_shape=[
+            jax.ShapeDtypeStruct(
+                (adapters, split, rank, width // split)
+                if split > 1 and k == 0
+                else (adapters, rank, width),
+                F32,
+            )
+            for k, width in enumerate(widths)
+        ],
         name="totals",
     )(*blocks)
 
@@ -481,7 +519,7 @@
             out[0] = part[...].astype(out.dtype)
 
 
-def settle(parts, where, kind, images, base=None):
+def settle(parts, where, first, stride, kind, images, base=None):
     rows, model = parts[0].shape
     extra = [] if base is None else [base]
     return pl.pallas_call(
@@ -491,7 +529,7 @@
             grid=(len(parts),),
             in_specs=[pl.BlockSpec((rows, model), lambda k, where: (0, 0))] * len(parts)
             + [pl.BlockSpec(memory_space=pl.ANY)] * len(extra),
-            out_specs=pl.BlockSpec((1, rows, model), lambda k, where: (where[k], 0, 0)),
+            out_specs=pl.BlockSpec((1, rows, model), lambda k, where: (where[first + stride * k], 0, 0)),
         ),
         out_shape=jax.ShapeDtypeStruct((images, rows, model), kind),
         input_output_aliases={1 + len(parts): 0} if extra else {},
@@ -608,6 +646,29 @@
         if not stay.any():
             return got
         return jnp.where(jnp.asarray(stay)[context * tensors + tensor] == 1, value, got)
+
+    def stays(value, other):
+        return jnp.where(core == context, value, other)
+
+    relay = [[], []]
+    for c in range(2 if ringed else 0):
+        for s in range(2):
+            for k in range(2):
+                here = c * tensors + 2 * s + k
+                along = c * tensors + 2 * (1 - s) + k
+                relay[0].append((here, along if k == c else (1 - c) * tensors + 2 * s + 1 - k))
+                if k != c:
+                    relay[1].append((here, along))
+
+    def send_first(value):
+        if ringed:
+            return [lax.ppermute(value, plane, relay[0])]
+        return [deliver(value, to_home[far]) for far in range(sides)]
+
+    def send_second(value, got):
+        if ringed:
+            return [got[0], stays(value, lax.ppermute(got[0], plane, relay[1]))]
+        return got
 
     def pair_up(a, b):
         return jnp.concatenate([a, b], axis=0)
@@ -688,12 +749,11 @@
         x_other, x_own, own[1], aside[0] = got[4:]
         packs = up_packs(adapter_index, ups)
         own.append(hop(own[1], "shard"))
-        aside.append(hop(aside[0], "shard"))
-        got = fence(cross_to(z[3], 0), cross_to(z[3], 1), cross_to(b[2], 1), cotangent)
+        got = fence(cross_to(z[3], 0), cross_to(z[3], 1), cross_to(b[2], 1), cotangent, packs[1])
         b.append(got[0])
         c.append(got[1])
         d.append(got[2])
-        cotangent = got[3]
+        cotangent, packs[1] = got[3:]
         last = cross_to(b[3], 1)
         own_over, aside_over = [], []
 
@@ -707,12 +767,12 @@
         attn_moves = [(k, 0, depth) for k in range(4 * shards)]
         ff_moves = [(k, which * depth, depth, which) for which in range(2) for k in range(4 * shards)]
         ff_place = jnp.concatenate([attn_place, attn_place], axis=1)
-        gy_own = None
 
         def start(*values):
-            got = fence(*values, last, packs[1], own[0], aside[0])
+            got = fence(*values, last, own[0], aside[0], own[2])
             d.append(got[-4])
-            packs[1], own[0], aside[0] = got[-3:]
+            own[0], aside[0], own[2] = got[-3:]
+            aside.append(hop(aside[0], "shard"))
             own_over.append(cross_to(own[0], 1))
             aside_over.append(cross_to(aside[0], 1))
             return got[:-4]
@@ -720,20 +780,22 @@
         def advance(stage, *values):
             count = len(values)
             if stage == 0:
-                got = fence(*values, own[2], aside[1], own_over[0], aside_over[0])
-                own[2], aside[1], own_over[0], aside_over[0] = got[count:]
+                got = fence(*values, own[2], aside[1], own_over[0], aside_over[0], cotangent)
+                own[2], aside[1], own_over[0], aside_over[0], late_cotangent = got[count:]
                 own.append(hop(own[2], "shard"))
                 own_over.append(cross_to(own[1], 1))
+                flows["gy"] = deliver(block_of(late_cotangent, tensor), to_owner)
+            elif stage == 1:
+                got = fence(*values, own[3], own[2], aside[1])
+                own[3], own[2], aside[1] = got[count:]
+                aside.append(hop(aside[1], "shard"))
                 aside_over.append(cross_to(aside[1], 1))
-            elif stage == 1:
-                got = fence(*values, own[3], own_over[1], aside_over[1], aside[1], cotangent)
-                own[3], own_over[1], aside_over[1], aside[1], late_cotangent = got[count:]
-                aside.append(hop(aside[1], "shard"))
                 own_over.append(cross_to(own[2], 1))
-                return (*got[:count], deliver(block_of(late_cotangent, tensor), to_owner))
             elif stage == 2:
-                got = fence(*values, aside[2], own_over[2])
-                aside[2], own_over[2] = got[count:]
+                got = fence(
+                    *values, aside[2], own_over[1], own_over[2], aside_over[1], own[3], flows["gy"]
+                )
+                aside[2], own_over[1], own_over[2], aside_over[1], own[3], flows["gy"] = got[count:]
                 aside.append(hop(aside[2], "shard"))
                 own_over.append(cross_to(own[3], 1))
                 aside_over.append(cross_to(aside[2], 1))
@@ -755,7 +817,7 @@
         packs = up_packs(adapter_index, ups)
         x_own = deliver(block_of(tokens, tensor), to_owner)
         x_other = swap(x_own)
-        gy_own = deliver(block_of(cotangent, tensor), to_owner)
+        flows["gy"] = deliver(block_of(cotangent, tensor), to_owner)
         attn_moves = [(k, 0, model) for k in range(sides)]
         attn_place = jnp.asarray([[0] * sides, list(range(sides))], jnp.int32)
         ff_moves = [(k, 0, model, k // sides) for k in range(2 * sides)]
@@ -765,7 +827,7 @@
             return values
 
         def advance(stage, *values):
-            return (*values, gy_own) if stage == 1 else values
+            return values
 
     mine = adapter_of(adapter_index, 0)
     down = block_of(down_in, mine)
@@ -775,9 +837,9 @@
     x_all = pair_up(x_own, x_other).astype(F32)
     normed, unit_one, inverse_one = normalize(x_all, ln1_gain, ln1_bias)
     n1 = normed.astype(BF16)
-    u = dot_nt(n1, down_t[: 3 * rank]).astype(BF16)
-    n1, u = start(n1, u)
+    u = dot_nt(down_t[: 3 * rank], n1).astype(BF16)
     qkv_lift, fc1_lift, proj_t, fc2_t = lifts(packs, width, hidden)
+    n1, u, qkv_lift = start(n1, u, qkv_lift)
     if ringed:
         attn_parts = [part for i in range(shards) for part in (z[i], b[i], c[i], d[i])]
     w_in, w_out, qkv = project(n1, u, qkv_lift, attn_parts, attn_moves, attn_place, width)
@@ -811,20 +873,21 @@
         o_heads, lse = attend(qkv_heads, group, near, o_heads)
         logs.append(lse)
         if group == 0:
-            o_heads, qkv_heads, gy_own = advance(1, o_heads, qkv_heads)
+            o_heads, qkv_heads = advance(1, o_heads, qkv_heads)
     (o_heads,) = advance(2, o_heads)
+    gy_own = flows["gy"]
     o = to_rows(o_heads, 1)
     attn_far = dot_nt(o[rows:], w_out)
-    c_part = dot_nt(o, proj_t)
+    c_part = dot_nt(proj_t, o)
     attn_sum = swap(attn_far) + dot_nt(o[:rows], w_out)
-    c_own = (c_part[:rows] + swap(c_part[rows:])).astype(BF16)
-    h = x_all[:rows] + layer_scale[0] * (attn_sum + dot(c_own, out_t[0]))
+    c_own = (c_part[:, :rows] + swap(c_part[:, rows:])).astype(BF16)
+    h = x_all[:rows] + layer_scale[0] * (attn_sum + dot_tn(c_own, out_t[0]))
     normed, unit_two, inverse_two = normalize(h, ln2_gain, ln2_bias)
     n2_own = normed.astype(BF16)
-    n2_own, gy_own = advance(3, n2_own, gy_own)
+    gb_own = (gy_own.astype(F32) * layer_scale[1]).astype(BF16)
+    gb = pair_up(gb_own, swap(gb_own))
+    n2_own, gb = advance(3, n2_own, gb)
     n2_far = swap(n2_own)
-    gy_all = pair_up(gy_own, swap(gy_own))
-    gb = (gy_all.astype(F32) * layer_scale[1]).astype(BF16)
     if ringed:
         ff_parts = [
             part
@@ -833,16 +896,16 @@
         ]
     else:
         ff_parts = fc1_parts + fc2_parts
-    branch_own, branch_far, gn2_own, gn2_far, m_part, m_far, gf_part, gf_far, g_fc1, g_fc2 = mlp(
+    branch_own, branch_far, gn2_own, gn2_far, rank_own, rank_far, g_fc1, g_fc2 = mlp(
         n2_own, n2_far, gb, down_t[3 * rank :], out_t[1], ff_parts, ff_moves, ff_place, fc1_lift, fc2_t
     )
-    m_own = (m_part + swap(m_far)).astype(BF16)
-    gf_own = (gf_part + swap(gf_far)).astype(BF16)
-    branch = branch_own + swap(branch_far).astype(F32) + dot(m_own, out_t[1])
+    ranks = (rank_own + swap(rank_far)).astype(BF16)
+    m_own, gf_own = ranks[:rank], ranks[rank:]
+    branch = branch_own + swap(branch_far).astype(F32) + dot_tn(m_own, out_t[1])
     result_own = (h + layer_scale[1] * branch).astype(BF16)
-    gn2 = gn2_own + swap(gn2_far) + dot(gf_own, down_t[3 * rank :])
-    g_out1 = dot_tn(m_own, gb[:rows])
-    g_down3 = dot_tn(gf_own, n2_own)
+    gn2 = gn2_own + swap(gn2_far) + dot_tn(gf_own, down_t[3 * rank :])
+    g_out1 = dot(m_own, gb[:rows])
+    g_down3 = dot(gf_own, n2_own)
 
     cut = model // 2
     one = jnp.where(context % half == 0, mine, 0)
@@ -886,13 +949,14 @@
     gattn_own, early = fence(gattn_own, early)
     gattn = pair_up(gattn_own, swap(gattn_own))
     early = to_contexts(early)
-    g_out0 = dot_tn(c_own, gattn_own)
-    gc = dot_nt(gattn, out_t[0]).astype(BF16)
-    g_proj = dot_tn(gc, o)
+    g_out0 = dot(c_own, gattn_own)
+    gc = dot_nt(out_t[0], gattn).astype(BF16)
+    g_proj = dot(gc, o)
     mid = to_sides([[columns(g_proj, far, width)] for far in range(sides)], halves([g_out0]))
-    go = (dot(gattn, w_out) + dot(gc, proj_t)).astype(BF16)
-    early, mid, go = fence(early, mid, go)
+    go = (dot(gattn, w_out) + dot_tn(gc, proj_t)).astype(BF16)
     early_line = [early, hop(early, "shard")]
+    early_line[1], early_line[0], mid, go = fence(early_line[1], early, mid, go)
+    early_line.append(hop(early_line[-1], "shard"))
     mid = to_contexts(mid)
     go_heads = to_heads(go, 1)
     g_heads = None
@@ -902,20 +966,23 @@
             g_heads, early_line[-1], mid, result_own = fence(
                 g_heads, early_line[-1], mid, result_own
             )
-            early_line.append(hop(early_line[-1], "shard"))
+            for _ in range(3, shards):
+                early_line.append(hop(early_line[-1], "shard"))
             mid_line = [mid, hop(mid, "shard")]
-            sent = [deliver(result_own, to_home[far]) for far in range(sides)]
-    g_heads, early_line[-1], mid_line[-1] = fence(g_heads, early_line[-1], mid_line[-1])
-    for _ in range(3, shards):
-        early_line.append(hop(early_line[-1], "shard"))
+            sent = send_first(result_own)
+    g_heads, mid_line[-1], early_line[-1], *sent = fence(
+        g_heads, mid_line[-1], early_line[-1], *sent
+    )
+    mid_line.append(hop(mid_line[-1], "shard"))
+    sent = send_second(result_own, sent)
     g = to_rows(g_heads, 3)
 
-    gu_part = dot_nt(g, qkv_lift)
-    gu_own = (gu_part[:rows] + swap(gu_part[rows:])).astype(BF16)
+    gu_part = dot_nt(qkv_lift, g)
+    gu_own = (gu_part[:, :rows] + swap(gu_part[:, rows:])).astype(BF16)
     gn1_far = swap(dot_nt(g[rows:], w_in))
-    g_up = dot_tn(u, g)
-    gn1 = dot_nt(g[:rows], w_in) + gn1_far + dot(gu_own, down_t[: 3 * rank])
-    g_down = dot_tn(gu_own, n1[:rows])
+    g_up = dot(u, g)
+    gn1 = dot_nt(g[:rows], w_in) + gn1_far + dot_tn(gu_own, down_t[: 3 * rank])
+    g_down = dot(gu_own, n1[:rows])
     late_slices = [
         [
             g_up[j * rank : (j + 1) * rank, (far * 3 + j) * width : (far * 3 + j + 1) * width]
@@ -926,52 +993,69 @@
     late = to_sides(late_slices, halves([g_down[j * rank : (j + 1) * rank] for j in range(3)]))
     input_own = gh + norm_back(gn1, unit_one[:rows], inverse_one[:rows], ln1_gain)
     input_own = input_own.astype(BF16)
-    late, input_own, early_line[-1], *sent = fence(late, input_own, early_line[-1], *sent)
     late = to_contexts(late)
-    mid_line.append(hop(mid_line[-1], "shard"))
-    sent += [swap(part) for part in sent]
     late, input_own, mid_line[-1], *sent = fence(late, input_own, mid_line[-1], *sent)
 
-    aways = np.arange(sides)
-    mine_at = (2 * ((side - aways) % sides) + core).astype(jnp.int32)
-    twin_at = (2 * ((side - aways) % sides) + 1 - core).astype(jnp.int32)
+    order = np.tile(np.arange(sides), 2)
+    flip = np.repeat([0, 1], sides)
+    far = jnp.where((core ^ flip) == context, 1 - order, order) if ringed else order
+    where = (2 * ((side - far) % sides) + (core ^ flip)).astype(jnp.int32)
     late_line = [late, hop(late, "shard")]
-    input_sent = [deliver(input_own, to_home[far]) for far in range(sides)]
+    input_sent = send_first(input_own)
     for _ in range(3, shards):
         mid_line.append(hop(mid_line[-1], "shard"))
-    result = settle(sent, jnp.concatenate([mine_at, twin_at]), BF16, images)
+    sent += [swap(part) for part in sent]
     fc1_grad, fc2_grad, early_half = totals(early_line, (hidden, hidden, 2 * cut), adapters)
-    late_line[1], early_half, result, *mid_line = fence(
-        late_line[1], early_half, result, *mid_line
-    )
+    late_line[1], early_half, mid_line[-1], *got = fence(
+        late_line[1], early_half, mid_line[-1], *sent, *input_sent
+    )
+    sent, input_sent = got[: 2 * sides], got[2 * sides :]
     for _ in range(2, shards - 1):
         late_line.append(hop(late_line[-1], "shard"))
+    first_twin = swap(input_sent[0])
+    input_sent = send_second(input_own, input_sent)
     early_twin = swap(early_half)
     proj_grad, mid_half = totals(mid_line, (width, cut), adapters)
-    mid_twin = swap(mid_half)
-    got = fence(late_line[-1], proj_grad, early_half, early_twin, mid_half, mid_twin, *input_sent)
-    late_line[-1], proj_grad, early_half, early_twin, mid_half, mid_twin = got[:6]
-    input_sent = got[6:]
+    result = settle(sent, where, 0, 1, BF16, images)
+    late_line[-1], early_half, early_twin, proj_grad, mid_half, result, first_twin, *input_sent = fence(
+        late_line[-1], early_half, early_twin, proj_grad, mid_half, result, first_twin, *input_sent
+    )
     if shards > 2:
         late_line.append(hop(late_line[-1], "shard"))
-    input_twins = [swap(part) for part in input_sent]
+    mid_twin = swap(mid_half)
+    input_grad = settle(
+        [input_sent[0], first_twin],
+        where,
+        0,
+        sides,
+        F32,
+        images,
+    )
     out_grad = spread(
         core, [mid_half, mid_twin, early_half, early_twin], ((0, 0), (1, 1)), cut
     )
-    input_grad = settle(list(input_sent), mine_at, F32, images)
-    late_line[-1], input_grad, out_grad, *input_twins = fence(
-        late_line[-1], input_grad, out_grad, *input_twins
-    )
-    qkv_grad, late_half = totals(late_line, (3 * width, 3 * cut), adapters)
+    last_sent = list(input_sent[1:])
+    last_twins = [swap(part) for part in last_sent]
+    late_line[-1], input_grad, out_grad, *last_twins = fence(
+        late_line[-1], input_grad, out_grad, *last_twins
+    )
+    qkv_grad, late_half = totals(late_line, (3 * width, 3 * cut), adapters, 3)
     late_twin = swap(late_half)
-    input_grad = settle(input_twins, twin_at, F32, images, input_grad)
+    input_grad = settle(
+        last_sent + last_twins,
+        where,
+        1,
+        sides,
+        F32,
+        images,
+        input_grad,
+    )
     down_grad = spread(
         core,
         [late_half, late_twin, early_half, early_twin],
         ((0, 0), (0, 1), (0, 2), (1, 0)),
         cut,
     )
-    qkv_grad = jnp.transpose(qkv_grad.reshape(adapters, rank, 3, width), (0, 2, 1, 3))
     return (
         result,
         input_grad,

time: 380 us -> 360 us (0.947)
  starting transfers between devices: 78.7 us -> 69.1 us
  waiting for transfers between devices: 87.3 us -> 92.5 us
  other arithmetic: 25.8 us -> 21 us
    ppermute x6 -> x2, waiting for transfers between devices: 32.6 us -> 10.3 us  [deliver(): got = lax.ppermute(value, plane, [(a, b) for a, b in pairs if a != b])]
    ppermute x18, waiting for transfers between devices: 21 us -> 33.1 us  [hop(): return lax.ppermute(value, axis, ring[axis])]
    ppermute x18, starting transfers between devices: 26.4 us -> 15.4 us  [hop(): return lax.ppermute(value, axis, ring[axis])]
    ppermute x0 -> x4, starting transfers between devices: none -> 10.5 us  [the longest x2 6.46 us: send_second(): return [got[0], stays(value, lax.ppermute(got[0], plane, relay[1]))]]
    ppermute x6 -> x2, starting transfers between devices: 17.8 us -> 8.93 us  [deliver(): got = lax.ppermute(value, plane, [(a, b) for a, b in pairs if a != b])]
    ppermute x22 -> x21, waiting for transfers between devices: 2.82 us -> 9.63 us  [swap(): return lax.ppermute(value, 'tensor', twin)]
    ppermute x0 -> x4, waiting for transfers between devices: none -> 5.71 us  [the longest x2 3.18 us: send_second(): return [got[0], stays(value, lax.ppermute(got[0], plane, relay[1]))]]
    ppermute x3, starting transfers between devices: 4.47 us -> 0.37 us  [to_contexts(): return pair_up(block, lax.ppermute(block, 'context', opposite))]
  transfers between devices with their start and end apart: 74 -> 73, of which waited for: 27 -> 29; matrix products, arithmetic and copies ran while one was open for 13% -> 13% of each run, Pallas kernels for 24% -> 25%
where the time goes in v1:
time: 360 us; the launch traced here: 358 us
  Pallas kernels  132 us (37%)
  waiting for transfers between devices  92.5 us (26%)
  starting transfers between devices  69.1 us (19%)
  matrix products  23.6 us (7%)
  other arithmetic  21 us (6%)
  local copies, waits for them, and re-layouts  14.9 us (4%)
  between operations  4.88 us (1%)
    pallas_call x1, Pallas kernels, mlp(): pl.pallas_call(functools.partial(mlp_kernel, block, own, moves, len(parts...  37.2 us
    ppermute x18, waiting for transfers between devices, hop(): return lax.ppermute(value, axis, ring[axis])  33.1 us
    pallas_call x2, Pallas kernels, attend_back(): pl.pallas_call(functools.partial(attend_back_kernel, block, near), grid=(...  31.1 us
    pallas_call x2, Pallas kernels, attend(): pl.pallas_call(functools.partial(attend_kernel, block), grid=(near,), in_...  22.4 us
    ppermute x21, waiting for transfers between devices, cross_to(): return lax.ppermute(value, plane, cross[turn])  20.3 us
    ppermute x21, starting transfers between devices, cross_to(): return lax.ppermute(value, plane, cross[turn])  17.2 us
    ppermute x18, starting transfers between devices, hop(): return lax.ppermute(value, axis, ring[axis])  15.4 us
    pallas_call x3, Pallas kernels, settle(): pl.pallas_call(functools.partial(settle_kernel, len(parts)), grid_spec=pl...  14.2 us
  transfers between devices with their start and end apart: 73, of which 29 were waited for; matrix products, arithmetic and copies ran while one was open for 13% of the time, Pallas kernels for 25%

profile of v1, /device:TPU:1, one launch (start us, length us, event | category | flops | bytes accessed | tf_op | source)
XLA Modules:
  0.0 358.4 jit_solution(14556223998635381660)
XLA Ops:
  2.1 4.5 %collective-permute-start.3 = (bf16[512,1024]{1,0:T(8,128)(2,1)S(1)}, bf16[512,1024]{1,0:T(8,128)(2,1)}, u32[]{:S(2)}, u32[]{:S(2)}) collective-permute-start(bf16[512,1024]{1,0:T(8,128)(2,1)S(1)} %dynamic-slice_bitcast_fusion.1), channel_id=1, source_target_pairs={{4,1},{6,3},{1,4},{3,6},{12,9},{14,11},{9,12},{11,14},{20,17},{22,... | collective-permute-start | bytes 3145736 | tf_op jit(solution)/shard_map/ppermute | solution.py:645
  12.0 10.3 %collective-permute-done.3 = bf16[512,1024]{1,0:T(8,128)(2,1)} collective-permute-done((bf16[512,1024]{1,0:T(8,128)(2,1)S(1)}, bf16[512,1024]{1,0:T(8,128)(2,1)}, u32[]{:S(2)}, u32[]{:S(2)}) %collective-permute-start.3) | collective-permute-done | bytes 1048608 | tf_op jit(solution)/shard_map/ppermute | solution.py:645
  29.8 5.6 %collective-permute-done.5.refs_8_ = bf16[128,1024]{1,0:T(8,128)(2,1)} collective-permute-done((bf16[128,1024]{1,0:T(8,128)(2,1)S(1)}, bf16[128,1024]{1,0:T(8,128)(2,1)}, u32[]{:S(2)}, u32[]{:S(2)}) %collective-permute-start.5) | collective-permute-done | bytes 262176 | tf_op jit(solution)/shard_map/ppermute | solution.py:600
  35.3 8.3 %collective-permute-done.6.refs_5_ = bf16[128,1024]{1,0:T(8,128)(2,1)} collective-permute-done((bf16[128,1024]{1,0:T(8,128)(2,1)S(1)}, bf16[128,1024]{1,0:T(8,128)(2,1)}, u32[]{:S(2)}, u32[]{:S(2)}) %collective-permute-start.6) | collective-permute-done | bytes 262176 | tf_op jit(solution)/shard_map/ppermute | solution.py:692
  78.1 10.2 %project.1 = (bf16[1024,1536]{1,0:T(8,128)(2,1)}, bf16[1024,512]{1,0:T(8,128)(2,1)}, bf16[1024,1536]{1,0:T(8,128)(2,1)}) custom-call(s32[2,16]{1,0:T(2,128)} %pad_add_fusion.place_ref, bf16[1024,1024]{1,0:T(8,128)(2,1)} %copy-done.4, bf16[48,1024]{1,0:T(8,128)(2,1)} %convolution_convert_fusion.1.u_ref, bf16[48,1536]{1,0:T(8,128)(2,1)} %get-tuple-element.180.lift_ref, ...), custom_call_target="tpu_custom_call" | custom-call | flops 1000 | bytes 1000 | tf_op jit(solution)/shard_map/project/pallas_call | solution.py:362
  92.2 4.4 %collective-permute-start.29 = (bf16[512,1024]{1,0:T(8,128)(2,1)S(1)}, bf16[512,1024]{1,0:T(8,128)(2,1)}, u32[]{:S(2)}, u32[]{:S(2)}) collective-permute-start(bf16[512,1024]{1,0:T(8,128)(2,1)S(1)} %dynamic-slice_bitcast_fusion), channel_id=1, source_target_pairs={{4,1},{6,3},{1,4},{3,6},{12,9},{14,11},{9,12},{11,14},{20,17},{22,... | collective-permute-start | bytes 3145736 | tf_op jit(solution)/shard_map/ppermute | solution.py:645
  98.8 11.2 %attend.2 = (bf16[1024,512]{1,0:T(8,128)(2,1)}, f32[2,8,1024]{2,1,0:T(8,128)}) custom-call(bf16[1024,1536]{1,0:T(8,128)(2,1)} %get-tuple-element.198.q_ref.k_ref.v_ref._, bf16[1024,1536]{1,0:T(8,128)(2,1)} %get-tuple-element.198.q_ref.k_ref.v_ref._, bf16[1024,1536]{1,0:T(8,128)(2,1)} %get-tuple-element.198.q_ref.k_ref.v_ref._, ...), custom_call_target="tpu_custom_call" | custom-call | flops 1000 | bytes 1000 | tf_op jit(solution)/shard_map/attend/pallas_call | solution.py:83
  113.2 11.2 %attend.3 = (bf16[1024,512]{1,0:T(8,128)(2,1)}, f32[2,8,1024]{2,1,0:T(8,128)}) custom-call(bf16[1024,1536]{1,0:T(8,128)(2,1)} %get-tuple-element.198.q_ref.k_ref.v_ref._, bf16[1024,1536]{1,0:T(8,128)(2,1)} %get-tuple-element.198.q_ref.k_ref.v_ref._, bf16[1024,1536]{1,0:T(8,128)(2,1)} %get-tuple-element.198.q_ref.k_ref.v_ref._, ...), custom_call_target="tpu_custom_call", output_to_operand_aliasing={{0}: (3, {})} | custom-call | flops 1000 | bytes 1000 | tf_op jit(solution)/shard_map/attend/pallas_call | solution.py:83
  140.7 7.0 %collective-permute-done.33.refs_13_ = bf16[256,1024]{1,0:T(8,128)(2,1)} collective-permute-done((bf16[256,1024]{1,0:T(8,128)(2,1)}, bf16[256,1024]{1,0:T(8,128)(2,1)}, u32[]{:S(2)}, u32[]{:S(2)}) %collective-permute-start.33) | collective-permute-done | bytes 524320 | tf_op jit(solution)/shard_map/ppermute | solution.py:600
  154.7 3.5 collective-permute-done.37.refs_15_
  158.2 37.2 %mlp.1 = (f32[512,1024]{1,0:T(8,128)}, bf16[512,1024]{1,0:T(8,128)(2,1)}, f32[512,1024]{1,0:T(8,128)}, f32[512,1024]{1,0:T(8,128)}, f32[32,512]{1,0:T(8,128)}, /...) custom-call(s32[2,32]{1,0:T(2,128)} %add_add_fusion.place_ref, ...), custom_call_target="tpu_custom_call" | custom-call | flops 1000 | bytes 1000 | tf_op jit(solution)/shard_map/mlp/pallas_call | solution.py:280
  216.1 4.2 %collective-permute-done.42 = bf16[2,16,3200]{2,1,0:T(8,128)(2,1)S(1)} collective-permute-done((bf16[2,16,3200]{2,1,0:T(8,128)(2,1)S(1)}, bf16[2,16,3200]{2,1,0:T(8,128)(2,1)S(1)}, u32[]{:S(2)}, u32[]{:S(2)}) %collective-permute-start.42) | collective-permute-done | bytes 204832 | tf_op jit(solution)/shard_map/ppermute | solution.py:938
  226.6 5.4 %collective-permute-done.43.refs_1_ = bf16[4,16,3200]{2,1,0:T(8,128)(2,1)} collective-permute-done((bf16[4,16,3200]{2,1,0:T(8,128)(2,1)S(1)}, bf16[4,16,3200]{2,1,0:T(8,128)(2,1)}, u32[]{:S(2)}, u32[]{:S(2)}) %collective-permute-start.43) | collective-permute-done | bytes 409632 | tf_op jit(solution)/shard_map/ppermute | solution.py:600
  232.8 15.8 %attend_back.2._ = bf16[1024,1536]{1,0:T(8,128)(2,1)} custom-call(bf16[1024,1536]{1,0:T(8,128)(2,1)} %get-tuple-element.198.q_ref.k_ref.v_ref._, bf16[1024,1536]{1,0:T(8,128)(2,1)} %get-tuple-element.198.q_ref.k_ref.v_ref._, bf16[1024,1536]{1,0:T(8,128)(2,1)} %get-tuple-element.198.q_ref.k_ref.v_ref._, bf16[1024,512]{1,0:T(8,128)(2,1)} %add_convert_fusion.3.go_ref, ...), custom_call_target="tpu_custom_call" | custom-call | flops 1000 | bytes 1000 | tf_op jit(solution)/shard_map/attend_back/pallas_call | solution.py:156
  249.5 3.7 %collective-permute-start.52 = (bf16[512,1024]{1,0:T(8,128)(2,1)S(1)}, bf16[512,1024]{1,0:T(8,128)(2,1)S(1)}, u32[]{:S(2)}, u32[]{:S(2)}) collective-permute-start(bf16[512,1024]{1,0:T(8,128)(2,1)S(1)} %add_convert_fusion.2), channel_id=1, source_target_pairs={{0,2},{1,4},{2,0},{3,6},{4,1},{5,7},{6,3},{7,5},{8,10},{9,12},{10,... | collective-permute-start | bytes 3145736 | tf_op jit(solution)/shard_map/ppermute | solution.py:665
  254.5 15.4 %attend_back.3 = bf16[1024,1536]{1,0:T(8,128)(2,1)} custom-call(bf16[1024,1536]{1,0:T(8,128)(2,1)} %get-tuple-element.198.q_ref.k_ref.v_ref._, bf16[1024,1536]{1,0:T(8,128)(2,1)} %get-tuple-element.198.q_ref.k_ref.v_ref._, bf16[1024,1536]{1,0:T(8,128)(2,1)} %get-tuple-element.198.q_ref.k_ref.v_ref._, ...), custom_call_target="tpu_custom_call", output_to_operand_aliasing={{}: (6, {})} | custom-call | flops 1000 | bytes 1000 | tf_op jit(solution)/shard_map/attend_back/pallas_call | solution.py:156
  270.0 3.5 fusion.54
  274.1 3.3 collective-permute-start.59
  279.9 3.7 %collective-permute-done.53 = f32[48,512]{1,0:T(8,128)S(1)} collective-permute-done((f32[48,512]{1,0:T(8,128)S(1)}, f32[48,512]{1,0:T(8,128)S(1)}, u32[]{:S(2)}, u32[]{:S(2)}) %collective-permute-start.53) | collective-permute-done | bytes 98336 | tf_op jit(solution)/shard_map/ppermute | solution.py:603
  285.8 5.7 %collective-permute-done.55 = bf16[16,2432]{1,0:T(8,128)(2,1)S(1)} collective-permute-done((bf16[16,2432]{1,0:T(8,128)(2,1)S(1)}, bf16[16,2432]{1,0:T(8,128)(2,1)S(1)}, u32[]{:S(2)}, u32[]{:S(2)}) %collective-permute-start.55) | collective-permute-done | bytes 77856 | tf_op jit(solution)/shard_map/ppermute | solution.py:927
  307.5 7.2 %collective-permute-done.61.refs_3_ = bf16[4,16,896]{2,1,0:T(8,128)(2,1)} collective-permute-done((bf16[4,16,896]{2,1,0:T(8,128)(2,1)}, bf16[4,16,896]{2,1,0:T(8,128)(2,1)}, u32[]{:S(2)}, u32[]{:S(2)}) %collective-permute-start.61) | collective-permute-done | bytes 114720 | tf_op jit(solution)/shard_map/ppermute | solution.py:600
  324.6 5.3 %settle.3 = bf16[4,512,1024]{2,1,0:T(8,128)(2,1)} custom-call(s32[4]{0:T(128)} %xor_add_fusion.where_ref, bf16[512,1024]{1,0:T(8,128)(2,1)} %copy-done.24, bf16[512,1024]{1,0:T(8,128)(2,1)} %copy-done.14, bf16[512,1024]{1,0:T(8,128)(2,1)} %collective-permute-done.62.refs_2_, bf16[512,1024]{1,0:T(8,128)(2,1)} %collective-permute-done.63.refs_3_), custom_call_target="tpu_custom_call" | custom-call | tf_op jit(solution)/shard_map/settle/pallas_call | solution.py:525
  336.4 4.4 %settle.4.refs_2_ = f32[4,512,1024]{2,1,0:T(8,128)} custom-call(s32[4]{0:T(128)} %xor_add_fusion.where_ref, bf16[512,1024]{1,0:T(8,128)(2,1)} %collective-permute-done.64.refs_0_, bf16[512,1024]{1,0:T(8,128)(2,1)} %collective-permute-done.67.refs_1_), custom_call_target="tpu_custom_call" | custom-call | tf_op jit(solution)/shard_map/settle/pallas_call | solution.py:525
  349.8 4.5 %settle.5 = f32[4,512,1024]{2,1,0:T(8,128)} custom-call(s32[4]{0:T(128)} %xor_add_fusion.where_ref, bf16[512,1024]{1,0:T(8,128)(2,1)} %copy-done.17, bf16[512,1024]{1,0:T(8,128)(2,1)} %copy-done.26, f32[4,512,1024]{2,1,0:T(8,128)} %settle.4.refs_2_), custom_call_target="tpu_custom_call", output_to_operand_aliasing={{}: (3, {})} | custom-call | tf_op jit(solution)/shard_map/settle/pallas_call | solution.py:525
  (400 shorter events, 158.1 us)
Async XLA Ops:
  2.1 20.1 %collective-permute-start.3 = (bf16[512,1024]{1,0:T(8,128)(2,1)S(1)}, bf16[512,1024]{1,0:T(8,128)(2,1)}, u32[]{:S(2)}, u32[]{:S(2)}) collective-permute-start(bf16[512,1024]{1,0:T(8,128)(2,1)S(1)} %dynamic-slice_bitcast_fusion.1), channel_id=1, source_target_pairs={{4,1},{6,3},{1,4},{3,6},{12,9},{14,11},{9,12},{11,14},{20,17},{22,... | collective-permute-start | bytes 3145736 | tf_op jit(solution)/shard_map/ppermute | solution.py:645
  6.8 20.0 %collective-permute-start.4 = (bf16[256,1024]{1,0:T(8,128)(2,1)S(1)}, bf16[256,1024]{1,0:T(8,128)(2,1)}, u32[]{:S(2)}, u32[]{:S(2)}) collective-permute-start(bf16[256,1024]{1,0:T(8,128)(2,1)S(1)} %constant_dynamic-update-slice_fusion.refs_0_), channel_id=1, source_target_pairs={{0,8},{8,16},{16,24},{24,0},{1,9},{9,17},{17,25},{25,1},{2,10},{10... | collective-permute-start | bytes 1572872 | tf_op jit(solution)/shard_map/ppermute | solution.py:600
  8.2 18.5 %collective-permute-start = (bf16[128,1024]{1,0:T(8,128)(2,1)S(1)}, bf16[128,1024]{1,0:T(8,128)(2,1)S(1)}, u32[]{:S(2)}, u32[]{:S(2)}) collective-permute-start(bf16[128,1024]{1,0:T(8,128)(2,1)S(1)} %pad_maximum_fusion.3.refs_0_), channel_id=1, source_target_pairs={{0,8},{8,16},{16,24},{24,0},{1,9},{9,17},{17,25},{25,1},{2,10},{10... | collective-permute-start | bytes 786440 | tf_op jit(solution)/shard_map/ppermute | solution.py:600
  9.5 17.2 %collective-permute-start.1 = (bf16[128,1024]{1,0:T(8,128)(2,1)S(1)}, bf16[128,1024]{1,0:T(8,128)(2,1)S(1)}, u32[]{:S(2)}, u32[]{:S(2)}) collective-permute-start(bf16[128,1024]{1,0:T(8,128)(2,1)S(1)} %pad_maximum_fusion.3.refs_0_), channel_id=1, source_target_pairs={{0,2},{1,5},{2,0},{3,7},{4,6},{5,1},{6,4},{7,3},{8,10},{9,13},{10,... | collective-permute-start | bytes 786440 | tf_op jit(solution)/shard_map/ppermute | solution.py:692
  9.5 17.2 %collective-permute-start.2 = (bf16[128,1024]{1,0:T(8,128)(2,1)S(1)}, bf16[128,1024]{1,0:T(8,128)(2,1)}, u32[]{:S(2)}, u32[]{:S(2)}) collective-permute-start(bf16[128,1024]{1,0:T(8,128)(2,1)S(1)} %pad_maximum_fusion.3.refs_0_), channel_id=1, source_target_pairs={{0,4},{1,3},{2,6},{3,1},{4,0},{5,7},{6,2},{7,5},{8,12},{9,11},{10,... | collective-permute-start | bytes 786440 | tf_op jit(solution)/shard_map/ppermute | solution.py:692
  26.8 16.9 %collective-permute-start.9 = (bf16[256,1024]{1,0:T(8,128)(2,1)S(1)}, bf16[256,1024]{1,0:T(8,128)(2,1)}, u32[]{:S(2)}, u32[]{:S(2)}) collective-permute-start(bf16[256,1024]{1,0:T(8,128)(2,1)S(1)} %constant_dynamic-update-slice_fusion.refs_0_), channel_id=1, source_target_pairs={{0,2},{1,5},{2,0},{3,7},{4,6},{5,1},{6,4},{7,3},{8,10},{9,13},{10,... | collective-permute-start | bytes 1572872 | tf_op jit(solution)/shard_map/ppermute | solution.py:692
  27.3 16.3 %collective-permute-start.6 = (bf16[128,1024]{1,0:T(8,128)(2,1)S(1)}, bf16[128,1024]{1,0:T(8,128)(2,1)}, u32[]{:S(2)}, u32[]{:S(2)}) collective-permute-start(bf16[128,1024]{1,0:T(8,128)(2,1)S(1)} %collective-permute-done.refs_4_), channel_id=1, source_target_pairs={{0,2},{1,5},{2,0},{3,7},{4,6},{5,1},{6,4},{7,3},{8,10},{9,13},{10,... | collective-permute-start | bytes 786440 | tf_op jit(solution)/shard_map/ppermute | solution.py:692
  28.3 15.3 %collective-permute-start.7 = (bf16[128,1024]{1,0:T(8,128)(2,1)S(1)}, bf16[128,1024]{1,0:T(8,128)(2,1)S(1)}, u32[]{:S(2)}, u32[]{:S(2)}) collective-permute-start(bf16[128,1024]{1,0:T(8,128)(2,1)S(1)} %collective-permute-done.refs_4_), channel_id=1, source_target_pairs={{0,4},{1,3},{2,6},{3,1},{4,0},{5,7},{6,2},{7,5},{8,12},{9,11},{10,... | collective-permute-start | bytes 786440 | tf_op jit(solution)/shard_map/ppermute | solution.py:692
  92.2 32.2 %collective-permute-start.29 = (bf16[512,1024]{1,0:T(8,128)(2,1)S(1)}, bf16[512,1024]{1,0:T(8,128)(2,1)}, u32[]{:S(2)}, u32[]{:S(2)}) collective-permute-start(bf16[512,1024]{1,0:T(8,128)(2,1)S(1)} %dynamic-slice_bitcast_fusion), channel_id=1, source_target_pairs={{4,1},{6,3},{1,4},{3,6},{12,9},{14,11},{9,12},{11,14},{20,17},{22,... | collective-permute-start | bytes 3145736 | tf_op jit(solution)/shard_map/ppermute | solution.py:645
  96.6 15.1 %collective-permute-start.24 = (bf16[256,1024]{1,0:T(8,128)(2,1)}, bf16[256,1024]{1,0:T(8,128)(2,1)S(1)}, u32[]{:S(2)}, u32[]{:S(2)}) collective-permute-start(bf16[256,1024]{1,0:T(8,128)(2,1)} %collective-permute-done.20.refs_8_), channel_id=1, source_target_pairs={{0,8},{8,16},{16,24},{24,0},{1,9},{9,17},{17,25},{25,1},{2,10},{10... | collective-permute-start | bytes 1572872 | tf_op jit(solution)/shard_map/ppermute | solution.py:600
  97.6 28.7 %collective-permute-start.26 = (bf16[256,1024]{1,0:T(8,128)(2,1)}, bf16[256,1024]{1,0:T(8,128)(2,1)}, u32[]{:S(2)}, u32[]{:S(2)}) collective-permute-start(bf16[256,1024]{1,0:T(8,128)(2,1)} %collective-permute-done.4.refs_4_), channel_id=1, source_target_pairs={{0,4},{1,3},{2,6},{3,1},{4,0},{5,7},{6,2},{7,5},{8,12},{9,11},{10,... | collective-permute-start | bytes 1572872 | tf_op jit(solution)/shard_map/ppermute | solution.py:692
  111.7 15.7 %collective-permute-start.25 = (bf16[256,1024]{1,0:T(8,128)(2,1)}, bf16[256,1024]{1,0:T(8,128)(2,1)}, u32[]{:S(2)}, u32[]{:S(2)}) collective-permute-start(bf16[256,1024]{1,0:T(8,128)(2,1)} %collective-permute-done.21.refs_5_), channel_id=1, source_target_pairs={{0,8},{8,16},{16,24},{24,0},{1,9},{9,17},{17,25},{25,1},{2,10},{10... | collective-permute-start | bytes 1572872 | tf_op jit(solution)/shard_map/ppermute | solution.py:600
  111.7 15.7 %collective-permute-start.27 = (bf16[256,1024]{1,0:T(8,128)(2,1)}, bf16[256,1024]{1,0:T(8,128)(2,1)}, u32[]{:S(2)}, u32[]{:S(2)}) collective-permute-start(bf16[256,1024]{1,0:T(8,128)(2,1)} %collective-permute-done.20.refs_8_), channel_id=1, source_target_pairs={{0,4},{1,3},{2,6},{3,1},{4,0},{5,7},{6,2},{7,5},{8,12},{9,11},{10,... | collective-permute-start | bytes 1572872 | tf_op jit(solution)/shard_map/ppermute | solution.py:692
  132.0 15.6 %collective-permute-start.33 = (bf16[256,1024]{1,0:T(8,128)(2,1)}, bf16[256,1024]{1,0:T(8,128)(2,1)}, u32[]{:S(2)}, u32[]{:S(2)}) collective-permute-start(bf16[256,1024]{1,0:T(8,128)(2,1)} %collective-permute-done.25.refs_9_), channel_id=1, source_target_pairs={{0,8},{8,16},{16,24},{24,0},{1,9},{9,17},{17,25},{25,1},{2,10},{10... | collective-permute-start | bytes 1572872 | tf_op jit(solution)/shard_map/ppermute | solution.py:600
  132.3 16.2 %collective-permute-start.35 = (bf16[256,1024]{1,0:T(8,128)(2,1)}, bf16[256,1024]{1,0:T(8,128)(2,1)}, u32[]{:S(2)}, u32[]{:S(2)}) collective-permute-start(bf16[256,1024]{1,0:T(8,128)(2,1)} %collective-permute-done.25.refs_9_), channel_id=1, source_target_pairs={{0,4},{1,3},{2,6},{3,1},{4,0},{5,7},{6,2},{7,5},{8,12},{9,11},{10,... | collective-permute-start | bytes 1572872 | tf_op jit(solution)/shard_map/ppermute | solution.py:692
  195.5 36.7 %collective-permute-start.49 = (bf16[512,1024]{1,0:T(8,128)(2,1)}, bf16[512,1024]{1,0:T(8,128)(2,1)S(1)}, u32[]{:S(2)}, u32[]{:S(2)}) collective-permute-start(bf16[512,1024]{1,0:T(8,128)(2,1)} %get-tuple-element.238), channel_id=1, source_target_pairs={{0,1},{1,0},{2,3},{3,2},{4,5},{5,4},{6,7},{7,6},{8,9},{9,8},{10,11... | collective-permute-start | bytes 3145736 | tf_op jit(solution)/shard_map/ppermute | solution.py:603
  232.0 16.7 %collective-permute-start.48 = (bf16[2,16,896]{2,1,0:T(8,128)(2,1)S(1)}, bf16[2,16,896]{2,1,0:T(8,128)(2,1)}, u32[]{:S(2)}, u32[]{:S(2)}) collective-permute-start(bf16[2,16,896]{2,1,0:T(8,128)(2,1)S(1)} %pad_maximum_fusion.8), channel_id=1, source_target_pairs={{0,4},{4,0},{1,5},{5,1},{2,6},{6,2},{3,7},{7,3},{8,12},{12,8},{9,1... | collective-permute-start | bytes 172040 | tf_op jit(solution)/shard_map/ppermute | solution.py:938
  232.2 17.3 %collective-permute-start.47 = (bf16[4,16,3200]{2,1,0:T(8,128)(2,1)}, bf16[4,16,3200]{2,1,0:T(8,128)(2,1)}, u32[]{:S(2)}, u32[]{:S(2)}) collective-permute-start(bf16[4,16,3200]{2,1,0:T(8,128)(2,1)} %collective-permute-done.43.refs_1_), channel_id=1, source_target_pairs={{0,8},{8,16},{16,24},{24,0},{1,9},{9,17},{17,25},{25,1},{2,10},{10... | collective-permute-start | bytes 1228808 | tf_op jit(solution)/shard_map/ppermute | solution.py:600
  249.5 20.4 %collective-permute-start.52 = (bf16[512,1024]{1,0:T(8,128)(2,1)S(1)}, bf16[512,1024]{1,0:T(8,128)(2,1)S(1)}, u32[]{:S(2)}, u32[]{:S(2)}) collective-permute-start(bf16[512,1024]{1,0:T(8,128)(2,1)S(1)} %add_convert_fusion.2), channel_id=1, source_target_pairs={{0,2},{1,4},{2,0},{3,6},{4,1},{5,7},{6,3},{7,5},{8,10},{9,12},{10,... | collective-permute-start | bytes 3145736 | tf_op jit(solution)/shard_map/ppermute | solution.py:665
  253.2 16.7 %collective-permute-start.51 = (bf16[4,16,3200]{2,1,0:T(8,128)(2,1)}, bf16[4,16,3200]{2,1,0:T(8,128)(2,1)S(1)}, u32[]{:S(2)}, u32[]{:S(2)}) collective-permute-start(bf16[4,16,3200]{2,1,0:T(8,128)(2,1)} %collective-permute-done.47.refs_2_), channel_id=1, source_target_pairs={{0,8},{8,16},{16,24},{24,0},{1,9},{9,17},{17,25},{25,1},{2,10},{10... | collective-permute-start | bytes 1228808 | tf_op jit(solution)/shard_map/ppermute | solution.py:600
  253.3 16.6 %collective-permute-start.50 = (bf16[4,16,896]{2,1,0:T(8,128)(2,1)S(1)}, bf16[4,16,896]{2,1,0:T(8,128)(2,1)}, u32[]{:S(2)}, u32[]{:S(2)}) collective-permute-start(bf16[4,16,896]{2,1,0:T(8,128)(2,1)S(1)} %pad_maximum_fusion.7.refs_0_), channel_id=1, source_target_pairs={{0,8},{8,16},{16,24},{24,0},{1,9},{9,17},{17,25},{25,1},{2,10},{10... | collective-permute-start | bytes 344072 | tf_op jit(solution)/shard_map/ppermute | solution.py:600
  274.1 22.9 %collective-permute-start.59 = (bf16[512,1024]{1,0:T(8,128)(2,1)S(1)}, bf16[512,1024]{1,0:T(8,128)(2,1)S(1)}, u32[]{:S(2)}, u32[]{:S(2)}) collective-permute-start(bf16[512,1024]{1,0:T(8,128)(2,1)S(1)} %collective-permute-done.52.refs_0_), channel_id=1, source_target_pairs={{1,3},{3,1},{4,6},{6,4},{9,11},{11,9},{12,14},{14,12},{17,19},{19,... | collective-permute-start | bytes 3145736 | tf_op jit(solution)/shard_map/ppermute | solution.py:670
  279.3 17.9 %collective-permute-start.57 = (f32[512,1024]{1,0:T(8,128)S(1)}, f32[512,1024]{1,0:T(8,128)S(1)}, u32[]{:S(2)}, u32[]{:S(2)}) collective-permute-start(f32[512,1024]{1,0:T(8,128)S(1)} %fusion.1), channel_id=1, source_target_pairs={{0,1},{1,0},{2,3},{3,2},{4,5},{5,4},{6,7},{7,6},{8,9},{9,8},{10,11... | collective-permute-start | bytes 6291464 | tf_op jit(solution)/shard_map/ppermute | solution.py:603
  317.2 15.8 %collective-permute-start.68 = (bf16[512,1024]{1,0:T(8,128)(2,1)}, bf16[512,1024]{1,0:T(8,128)(2,1)}, u32[]{:S(2)}, u32[]{:S(2)}) collective-permute-start(bf16[512,1024]{1,0:T(8,128)(2,1)} %collective-permute-done.64.refs_0_), channel_id=1, source_target_pairs={{1,3},{3,1},{4,6},{6,4},{9,11},{11,9},{12,14},{14,12},{17,19},{19,... | collective-permute-start | bytes 3145736 | tf_op jit(solution)/shard_map/ppermute | solution.py:670
  (131 other events, 1253.9 us)

commit v2 on v1

--- a/solution.py
+++ b/solution.py
@@ -187,7 +187,7 @@
     branch_own, branch_far, gn_own, gn_far = outs[:4]
     rank_own, rank_far, gf1_out, gf2_out = outs[4:]
     w1_all, w2_all, n_ref, f_ref, gm_ref, branch_ref, gn_ref = scratch[:7]
-    rank_ref, gf1_ref, gf2_ref, sems, row_sems = scratch[7:]
+    rank_ref, gf1_ref, gf2_ref, cast_ref, sems, row_sems, out_sems = scratch[7:]
     rank = f_ref.shape[0]
     rows = n_ref.shape[0]
     chunk = u1_ref.shape[1]
@@ -219,6 +219,17 @@
             copy.wait()
         f_ref[...] = dot_nt(down_ref[...], n_ref[...]).astype(BF16)
 
+    final = pl.program_id(0) == pl.num_programs(0) - 1
+
+    def leave(i, at, to, home):
+        branch = branch_ref.at[at, :] if home else cast_ref.at[to, :]
+        target = branch_own if home else branch_far
+        gn_target = gn_own if home else gn_far
+        return [
+            pltpu.make_async_copy(branch, target.at[to, :], out_sems.at[0, i]),
+            pltpu.make_async_copy(gn_ref.at[at, :], gn_target.at[to, :], out_sems.at[1, i]),
+        ]
+
     for which, target in enumerate((w1_all, w2_all)):
         area = target.at[:, at_chunk]
         pltpu.make_async_copy(area, area, sems.at[which, pl.program_id(0)]).wait()
@@ -243,6 +254,19 @@
         rank_ref[rank:, at] += dot_nt(u1, gz)
         gf1_ref[...] += dot(f_ref[:, at], gz)
         gf2_ref[...] += dot(gm_ref[:, at], a)
+
+        @pl.when(jnp.logical_and(final, i < own // block))
+        def _():
+            for copy in leave(i, at, at, True):
+                copy.start()
+
+        @pl.when(jnp.logical_and(final, i >= own // block))
+        def _():
+            to = pl.ds(pl.multiple_of(i * block - own, block), block)
+            cast_ref[to, :] = branch_ref[at, :].astype(BF16)
+            for copy in leave(i, at, to, False):
+                copy.start()
+
         return carry
 
     lax.fori_loop(0, rows // block, step, 0)
@@ -253,10 +277,12 @@
     def _():
         rank_own[...] = rank_ref[:, :own]
         rank_far[...] = rank_ref[:, own:]
-        branch_own[...] = branch_ref[:own, :]
-        branch_far[...] = branch_ref[own:, :].astype(BF16)
-        gn_own[...] = gn_ref[:own, :]
-        gn_far[...] = gn_ref[own:, :]
+        for i in range(rows // block):
+            home = i < own // block
+            at = pl.ds(i * block, block)
+            to = at if home else pl.ds(i * block - own, block)
+            for copy in leave(i, at, to, home):
+                copy.wait()
 
 
 def mlp(n_own, n_far, gb, down, up, parts, moves, place, u1, d2):
@@ -265,7 +291,7 @@
     hidden = u1.shape[1]
     rank = down.shape[0]
     chunk = min(512, hidden)
-    block = min(256, rows)
+    block = min(256, own)
     whole = lambda shape: pl.BlockSpec(shape, lambda j, place: (0, 0))
     part = lambda depth: pl.BlockSpec((depth, chunk), lambda j, place: (0, j))
     far = rows - own
@@ -290,7 +316,9 @@
                 part(rank),
             ]
             + [pl.BlockSpec(memory_space=pl.ANY)] * (2 + len(parts)),
-            out_specs=[whole(shape) for shape, _ in shapes] + [part(rank), part(rank)],
+            out_specs=[pl.BlockSpec(memory_space=pl.ANY)] * 4
+            + [whole(shape) for shape, _ in shapes[4:]]
+            + [part(rank), part(rank)],
             scratch_shapes=[
                 pltpu.VMEM((model, hidden), BF16),
                 pltpu.VMEM((model, hidden), BF16),
@@ -302,8 +330,10 @@
                 pltpu.VMEM((2 * rank, rows), F32),
                 pltpu.VMEM((rank, chunk), F32),
                 pltpu.VMEM((rank, chunk), F32),
+                pltpu.VMEM((far, model), BF16),
                 pltpu.SemaphoreType.DMA((2, hidden // chunk)),
                 pltpu.SemaphoreType.DMA((2,)),
+                pltpu.SemaphoreType.DMA((2, rows // block)),
             ],
         ),
         out_shape=[jax.ShapeDtypeStruct(*shape) for shape in shapes]
@@ -928,14 +958,16 @@
             packed.append(pack)
         return jnp.stack(packed)
 
-    def to_contexts(block):
-        if half > 1:
-            total = lax.psum(block.astype(F32), "context", axis_index_groups=steps)
-            block = total.astype(BF16)
-            opposite = [(i, (i + half) % contexts) for i in range(contexts)]
-        else:
-            opposite = ring["context"]
-        return pair_up(block, lax.ppermute(block, "context", opposite))
+    opposite = [(i, (i + half) % contexts) for i in range(contexts)]
+
+    def merge(block):
+        if half == 1:
+            return block
+        total = lax.psum(block.astype(F32), "context", axis_index_groups=steps)
+        return total.astype(BF16)
+
+    def over(block):
+        return lax.ppermute(block, "context", opposite)
 
     def columns(array, far, size):
         return array[:, far * size : (far + 1) * size]
@@ -946,35 +978,44 @@
     )
     gh = gy_own.astype(F32) + norm_back(gn2, unit_two, inverse_two, ln2_gain)
     gattn_own = (layer_scale[0] * gh).astype(BF16)
-    gattn_own, early = fence(gattn_own, early)
-    gattn = pair_up(gattn_own, swap(gattn_own))
-    early = to_contexts(early)
+    gattn_far, early = fence(swap(gattn_own), early)
+    gattn = pair_up(gattn_own, gattn_far)
+    early_line = [merge(early)]
+    early_line.append(hop(early_line[0], "shard"))
+    early_over = [over(early_line[0])]
     g_out0 = dot(c_own, gattn_own)
     gc = dot_nt(out_t[0], gattn).astype(BF16)
     g_proj = dot(gc, o)
     mid = to_sides([[columns(g_proj, far, width)] for far in range(sides)], halves([g_out0]))
     go = (dot(gattn, w_out) + dot_tn(gc, proj_t)).astype(BF16)
-    early_line = [early, hop(early, "shard")]
-    early_line[1], early_line[0], mid, go = fence(early_line[1], early, mid, go)
-    early_line.append(hop(early_line[-1], "shard"))
-    mid = to_contexts(mid)
+    early_line[1], early_over[0], mid, go, result_own = fence(
+        early_line[1], early_over[0], mid, go, result_own
+    )
+    early_line.append(hop(early_line[1], "shard"))
+    early_over.append(over(early_line[1]))
+    mid = merge(mid)
+    mid_over = over(mid)
+    sent = send_first(result_own)
     go_heads = to_heads(go, 1)
     g_heads = None
     for group in range(group_count):
         g_heads = attend_back(qkv_heads, go_heads, o_heads, logs[group], group, near, g_heads)
         if group == 0:
-            g_heads, early_line[-1], mid, result_own = fence(
-                g_heads, early_line[-1], mid, result_own
+            g_heads, mid_over, early_line[2], *sent = fence(
+                g_heads, mid_over, early_line[2], *sent
             )
+            early_over.append(over(early_line[2]))
             for _ in range(3, shards):
                 early_line.append(hop(early_line[-1], "shard"))
-            mid_line = [mid, hop(mid, "shard")]
-            sent = send_first(result_own)
-    g_heads, mid_line[-1], early_line[-1], *sent = fence(
-        g_heads, mid_line[-1], early_line[-1], *sent
-    )
-    mid_line.append(hop(mid_line[-1], "shard"))
-    sent = send_second(result_own, sent)
+            mid_line = [pair_up(mid, mid_over)]
+            mid_line.append(hop(mid_line[0], "shard"))
+            sent = send_second(result_own, sent)
+    g_heads, mid_line[1], early_over[1], early_over[2], *got = fence(
+        g_heads, mid_line[1], early_over[1], early_over[2], *early_line[3:], *sent
+    )
+    early_line[3:], sent = got[: shards - 3], got[shards - 3 :]
+    early_over.extend([over(block) for block in early_line[3:]])
+    mid_line.append(hop(mid_line[1], "shard"))
     g = to_rows(g_heads, 3)
 
     gu_part = dot_nt(qkv_lift, g)
@@ -993,63 +1034,56 @@
     late = to_sides(late_slices, halves([g_down[j * rank : (j + 1) * rank] for j in range(3)]))
     input_own = gh + norm_back(gn1, unit_one[:rows], inverse_one[:rows], ln1_gain)
     input_own = input_own.astype(BF16)
-    late = to_contexts(late)
-    late, input_own, mid_line[-1], *sent = fence(late, input_own, mid_line[-1], *sent)
+    late_line = [merge(late)]
+    late_line.append(hop(late_line[0], "shard"))
+    late_over = [over(late_line[0])]
+    last_over = early_over[3:]
+    late_line[1], late_over[0], input_own, mid_line[2], *got = fence(
+        late_line[1], late_over[0], input_own, mid_line[2], *last_over, *sent
+    )
+    early_over[3:], sent = got[: len(last_over)], got[len(last_over) :]
 
     order = np.tile(np.arange(sides), 2)
     flip = np.repeat([0, 1], sides)
     far = jnp.where((core ^ flip) == context, 1 - order, order) if ringed else order
     where = (2 * ((side - far) % sides) + (core ^ flip)).astype(jnp.int32)
-    late_line = [late, hop(late, "shard")]
+    late_line.append(hop(late_line[1], "shard"))
     input_sent = send_first(input_own)
     for _ in range(3, shards):
         mid_line.append(hop(mid_line[-1], "shard"))
-    sent += [swap(part) for part in sent]
-    fc1_grad, fc2_grad, early_half = totals(early_line, (hidden, hidden, 2 * cut), adapters)
-    late_line[1], early_half, mid_line[-1], *got = fence(
-        late_line[1], early_half, mid_line[-1], *sent, *input_sent
-    )
-    sent, input_sent = got[: 2 * sides], got[2 * sides :]
-    for _ in range(2, shards - 1):
+    sent = list(sent) + [swap(part) for part in sent]
+    fc1_grad, fc2_grad, early_half = totals(
+        early_line + early_over, (hidden, hidden, 2 * cut), adapters
+    )
+    late_line[1], late_line[2], early_half, *got = fence(
+        late_line[1], late_line[2], early_half, *sent, *mid_line
+    )
+    sent, mid_line = got[: 2 * sides], got[2 * sides :]
+    for _ in range(3, shards):
         late_line.append(hop(late_line[-1], "shard"))
+    late_over.append(over(late_line[1]))
+    early_twin = swap(early_half)
+    result = settle(sent, where, 0, 1, BF16, images)
+    proj_grad, mid_half = totals(mid_line, (width, cut), adapters)
+    late_line[-1], late_over[1], early_half, early_twin, mid_half, result, *input_sent = fence(
+        late_line[-1], late_over[1], early_half, early_twin, mid_half, result, *input_sent
+    )
+    late_over.extend([over(block) for block in late_line[2:]])
     first_twin = swap(input_sent[0])
     input_sent = send_second(input_own, input_sent)
-    early_twin = swap(early_half)
-    proj_grad, mid_half = totals(mid_line, (width, cut), adapters)
-    result = settle(sent, where, 0, 1, BF16, images)
-    late_line[-1], early_half, early_twin, proj_grad, mid_half, result, first_twin, *input_sent = fence(
-        late_line[-1], early_half, early_twin, proj_grad, mid_half, result, first_twin, *input_sent
-    )
-    if shards > 2:
-        late_line.append(hop(late_line[-1], "shard"))
     mid_twin = swap(mid_half)
-    input_grad = settle(
-        [input_sent[0], first_twin],
-        where,
-        0,
-        sides,
-        F32,
-        images,
-    )
+    input_grad = settle([input_sent[0], first_twin], where, 0, sides, F32, images)
     out_grad = spread(
         core, [mid_half, mid_twin, early_half, early_twin], ((0, 0), (1, 1)), cut
     )
-    last_sent = list(input_sent[1:])
-    last_twins = [swap(part) for part in last_sent]
-    late_line[-1], input_grad, out_grad, *last_twins = fence(
-        late_line[-1], input_grad, out_grad, *last_twins
-    )
-    qkv_grad, late_half = totals(late_line, (3 * width, 3 * cut), adapters, 3)
+    late_line[0], input_grad, out_grad, *late_over = fence(
+        late_line[0], input_grad, out_grad, *late_over
+    )
+    qkv_grad, late_half = totals(late_line + late_over, (3 * width, 3 * cut), adapters, 3)
+    late_half, qkv_grad, *input_sent = fence(late_half, qkv_grad, *input_sent)
     late_twin = swap(late_half)
-    input_grad = settle(
-        last_sent + last_twins,
-        where,
-        1,
-        sides,
-        F32,
-        images,
-        input_grad,
-    )
+    last_twins = [swap(part) for part in input_sent[1:]]
+    input_grad = settle(input_sent[1:] + last_twins, where, 1, sides, F32, images, input_grad)
     down_grad = spread(
         core,
         [late_half, late_twin, early_half, early_twin],

time: 360 us -> 349 us (0.969)
  waiting for transfers between devices: 92.5 us -> 73.2 us
  starting transfers between devices: 69.1 us -> 73.6 us
  local copies, waits for them, and re-layouts: 14.9 us -> 19.2 us
    ppermute x3 -> x9, starting transfers between devices: 0.37 us -> 7.39 us  [over(): return lax.ppermute(block, 'context', opposite)]
    ppermute x3 -> x9, waiting for transfers between devices: 4.99 us -> 0.02 us  [over(): return lax.ppermute(block, 'context', opposite)]
    ppermute x3, waiting for transfers between devices: 8.52 us -> 3.64 us  [to_sides(): pack = lax.ppermute(pack, 'tensor', send)]
    ppermute x18, waiting for transfers between devices: 33.1 us -> 28.4 us  [hop(): return lax.ppermute(value, axis, ring[axis])]
    unnamed x175 -> x178, local copies, waits for them, and re-layouts: 8.02 us -> 11.9 us
  transfers between devices with their start and end apart: 73 -> 79, of which waited for: 29 -> 26; matrix products, arithmetic and copies ran while one was open for 13% -> 12% of each run, Pallas kernels for 25% -> 26%
where the time goes in v2:
time: 349 us; the launch traced here: 347 us
  Pallas kernels  130 us (37%)
  starting transfers between devices  73.6 us (21%)
  waiting for transfers between devices  73.2 us (21%)
  matrix products  25.1 us (7%)
  other arithmetic  21.1 us (6%)
  local copies, waits for them, and re-layouts  19.2 us (6%)
  between operations  4.88 us (1%)
    pallas_call x1, Pallas kernels, mlp(): pl.pallas_call(functools.partial(mlp_kernel, block, own, moves, len(parts...  35.6 us
    pallas_call x2, Pallas kernels, attend_back(): pl.pallas_call(functools.partial(attend_back_kernel, block, near), grid=(...  30.8 us
    ppermute x18, waiting for transfers between devices, hop(): return lax.ppermute(value, axis, ring[axis])  28.4 us
    pallas_call x2, Pallas kernels, attend(): pl.pallas_call(functools.partial(attend_kernel, block), grid=(near,), in_...  22.4 us
    ppermute x21, waiting for transfers between devices, cross_to(): return lax.ppermute(value, plane, cross[turn])  19.8 us
    ppermute x21, starting transfers between devices, cross_to(): return lax.ppermute(value, plane, cross[turn])  19.6 us
    pallas_call x3, Pallas kernels, settle(): pl.pallas_call(functools.partial(settle_kernel, len(parts)), grid_spec=pl...  14.3 us
    ppermute x18, starting transfers between devices, hop(): return lax.ppermute(value, axis, ring[axis])  13.5 us
  transfers between devices with their start and end apart: 79, of which 26 were waited for; matrix products, arithmetic and copies ran while one was open for 12% of the time, Pallas kernels for 26%

profile of v2, /device:TPU:1, one launch (start us, length us, event | category | flops | bytes accessed | tf_op | source)
XLA Modules:
  0.0 347.5 jit_solution(16392048559771300017)
XLA Ops:
  2.1 4.5 %collective-permute-start.3 = (bf16[512,1024]{1,0:T(8,128)(2,1)S(1)}, bf16[512,1024]{1,0:T(8,128)(2,1)}, u32[]{:S(2)}, u32[]{:S(2)}) collective-permute-start(bf16[512,1024]{1,0:T(8,128)(2,1)S(1)} %dynamic-slice_bitcast_fusion.1), channel_id=1, source_target_pairs={{4,1},{6,3},{1,4},{3,6},{12,9},{14,11},{9,12},{11,14},{20,17},{22,... | collective-permute-start | bytes 3145736 | tf_op jit(solution)/shard_map/ppermute | solution.py:675
  12.0 10.3 %collective-permute-done.3 = bf16[512,1024]{1,0:T(8,128)(2,1)} collective-permute-done((bf16[512,1024]{1,0:T(8,128)(2,1)S(1)}, bf16[512,1024]{1,0:T(8,128)(2,1)}, u32[]{:S(2)}, u32[]{:S(2)}) %collective-permute-start.3) | collective-permute-done | bytes 1048608 | tf_op jit(solution)/shard_map/ppermute | solution.py:675
  29.8 5.6 %collective-permute-done.5.refs_8_ = bf16[128,1024]{1,0:T(8,128)(2,1)} collective-permute-done((bf16[128,1024]{1,0:T(8,128)(2,1)S(1)}, bf16[128,1024]{1,0:T(8,128)(2,1)}, u32[]{:S(2)}, u32[]{:S(2)}) %collective-permute-start.5) | collective-permute-done | bytes 262176 | tf_op jit(solution)/shard_map/ppermute | solution.py:630
  35.3 8.3 %collective-permute-done.6.refs_5_ = bf16[128,1024]{1,0:T(8,128)(2,1)} collective-permute-done((bf16[128,1024]{1,0:T(8,128)(2,1)S(1)}, bf16[128,1024]{1,0:T(8,128)(2,1)}, u32[]{:S(2)}, u32[]{:S(2)}) %collective-permute-start.6) | collective-permute-done | bytes 262176 | tf_op jit(solution)/shard_map/ppermute | solution.py:722
  62.3 4.0 %subtract_multiply_fusion = (f32[1024,1024]{1,0:T(8,128)}, bf16[1024,1024]{1,0:T(8,128)(2,1)S(1)}) fusion(f32[1024]{0:T(1024)} %add_rsqrt_fusion, f32[1024]{0:T(1024)S(1)} %broadcast_multiply_fusion, bf16[512,1024]{1,0:T(8,128)(2,1)S(1)} %collective-permute-done.14, bf16[512,1024]{1,0:T(8,128)(2,1)S(1)} %broadcast_select_fusion.3, f32[1024]{0:T(1024)S(1)} %copy-done.72, ...), kind=kLoop, calls=%fused_computation.2 | loop fusion | flops 9437184 | bytes 8404992 | tf_op jit(solution)/shard_map/mul | solution.py:573
  78.9 10.2 %project.1 = (bf16[1024,1536]{1,0:T(8,128)(2,1)}, bf16[1024,512]{1,0:T(8,128)(2,1)}, bf16[1024,1536]{1,0:T(8,128)(2,1)}) custom-call(s32[2,16]{1,0:T(2,128)} %pad_add_fusion.place_ref, bf16[1024,1024]{1,0:T(8,128)(2,1)} %copy-done.4, bf16[48,1024]{1,0:T(8,128)(2,1)} %convolution_convert_fusion.1.u_ref, bf16[48,1536]{1,0:T(8,128)(2,1)} %get-tuple-element.193.lift_ref, ...), custom_call_target="tpu_custom_call" | custom-call | flops 1000 | bytes 1000 | tf_op jit(solution)/shard_map/project/pallas_call | solution.py:392
  92.5 4.7 %collective-permute-start.29 = (bf16[512,1024]{1,0:T(8,128)(2,1)S(1)}, bf16[512,1024]{1,0:T(8,128)(2,1)}, u32[]{:S(2)}, u32[]{:S(2)}) collective-permute-start(bf16[512,1024]{1,0:T(8,128)(2,1)S(1)} %dynamic-slice_bitcast_fusion), channel_id=1, source_target_pairs={{4,1},{6,3},{1,4},{3,6},{12,9},{14,11},{9,12},{11,14},{20,17},{22,... | collective-permute-start | bytes 3145736 | tf_op jit(solution)/shard_map/ppermute | solution.py:675
  99.2 11.2 %attend.2 = (bf16[1024,512]{1,0:T(8,128)(2,1)}, f32[2,8,1024]{2,1,0:T(8,128)}) custom-call(bf16[1024,1536]{1,0:T(8,128)(2,1)} %get-tuple-element.211.q_ref.k_ref.v_ref._, bf16[1024,1536]{1,0:T(8,128)(2,1)} %get-tuple-element.211.q_ref.k_ref.v_ref._, bf16[1024,1536]{1,0:T(8,128)(2,1)} %get-tuple-element.211.q_ref.k_ref.v_ref._, ...), custom_call_target="tpu_custom_call" | custom-call | flops 1000 | bytes 1000 | tf_op jit(solution)/shard_map/attend/pallas_call | solution.py:83
  114.4 11.2 %attend.3 = (bf16[1024,512]{1,0:T(8,128)(2,1)}, f32[2,8,1024]{2,1,0:T(8,128)}) custom-call(bf16[1024,1536]{1,0:T(8,128)(2,1)} %get-tuple-element.211.q_ref.k_ref.v_ref._, bf16[1024,1536]{1,0:T(8,128)(2,1)} %get-tuple-element.211.q_ref.k_ref.v_ref._, bf16[1024,1536]{1,0:T(8,128)(2,1)} %get-tuple-element.211.q_ref.k_ref.v_ref._, ...), custom_call_target="tpu_custom_call", output_to_operand_aliasing={{0}: (3, {})} | custom-call | flops 1000 | bytes 1000 | tf_op jit(solution)/shard_map/attend/pallas_call | solution.py:83
  142.0 5.9 %collective-permute-done.33.refs_13_ = bf16[256,1024]{1,0:T(8,128)(2,1)} collective-permute-done((bf16[256,1024]{1,0:T(8,128)(2,1)}, bf16[256,1024]{1,0:T(8,128)(2,1)}, u32[]{:S(2)}, u32[]{:S(2)}) %collective-permute-start.33) | collective-permute-done | bytes 524320 | tf_op jit(solution)/shard_map/ppermute | solution.py:630
  154.3 4.5 %collective-permute-done.37.refs_15_ = bf16[256,1024]{1,0:T(8,128)(2,1)} collective-permute-done((bf16[256,1024]{1,0:T(8,128)(2,1)}, bf16[256,1024]{1,0:T(8,128)(2,1)}, u32[]{:S(2)}, u32[]{:S(2)}) %collective-permute-start.37) | collective-permute-done | bytes 524320 | tf_op jit(solution)/shard_map/ppermute | solution.py:722
  158.8 35.6 %mlp.1 = (f32[512,1024]{1,0:T(8,128)}, bf16[512,1024]{1,0:T(8,128)(2,1)}, f32[512,1024]{1,0:T(8,128)}, f32[512,1024]{1,0:T(8,128)}, f32[32,512]{1,0:T(8,128)}, /...) custom-call(s32[2,32]{1,0:T(2,128)} %add_add_fusion.place_ref, ...), custom_call_target="tpu_custom_call" | custom-call | flops 1000 | bytes 1000 | tf_op jit(solution)/shard_map/mlp/pallas_call | solution.py:306
  197.0 3.6 %collective-permute-done.39 = f32[32,512]{1,0:T(8,128)S(1)} collective-permute-done((f32[32,512]{1,0:T(8,128)}, f32[32,512]{1,0:T(8,128)S(1)}, u32[]{:S(2)}, u32[]{:S(2)}) %collective-permute-start.39) | collective-permute-done | bytes 65568 | tf_op jit(solution)/shard_map/ppermute | solution.py:633
  220.6 5.2 %collective-permute-done.43.refs_1_ = bf16[2,16,3200]{2,1,0:T(8,128)(2,1)} collective-permute-done((bf16[2,16,3200]{2,1,0:T(8,128)(2,1)S(1)}, bf16[2,16,3200]{2,1,0:T(8,128)(2,1)}, u32[]{:S(2)}, u32[]{:S(2)}) %collective-permute-start.43) | collective-permute-done | bytes 204832 | tf_op jit(solution)/shard_map/ppermute | solution.py:630
  227.4 15.4 %attend_back.2._ = bf16[1024,1536]{1,0:T(8,128)(2,1)} custom-call(bf16[1024,1536]{1,0:T(8,128)(2,1)} %get-tuple-element.211.q_ref.k_ref.v_ref._, bf16[1024,1536]{1,0:T(8,128)(2,1)} %get-tuple-element.211.q_ref.k_ref.v_ref._, bf16[1024,1536]{1,0:T(8,128)(2,1)} %get-tuple-element.211.q_ref.k_ref.v_ref._, bf16[1024,512]{1,0:T(8,128)(2,1)} %add_convert_fusion.3.go_ref, ...), custom_call_target="tpu_custom_call" | custom-call | flops 1000 | bytes 1000 | tf_op jit(solution)/shard_map/attend_back/pallas_call | solution.py:156
  249.5 15.4 %attend_back.3 = bf16[1024,1536]{1,0:T(8,128)(2,1)} custom-call(bf16[1024,1536]{1,0:T(8,128)(2,1)} %get-tuple-element.211.q_ref.k_ref.v_ref._, bf16[1024,1536]{1,0:T(8,128)(2,1)} %get-tuple-element.211.q_ref.k_ref.v_ref._, bf16[1024,1536]{1,0:T(8,128)(2,1)} %get-tuple-element.211.q_ref.k_ref.v_ref._, ...), custom_call_target="tpu_custom_call", output_to_operand_aliasing={{}: (6, {})} | custom-call | flops 1000 | bytes 1000 | tf_op jit(solution)/shard_map/attend_back/pallas_call | solution.py:156
  267.1 3.9 %fusion.1 = f32[512,1024]{1,0:T(8,128)S(1)} fusion(bf16[1024,1536]{1,0:T(8,128)(2,1)} %get-tuple-element.258, bf16[1024,1536]{1,0:T(8,128)(2,1)S(1)} %copy-done.2), kind=kOutput, calls=%fused_computation.23 | convolution fusion | flops 1610612736 | bytes 6815744 | tf_op jit(solution)/shard_map/dot_general | solution.py:29
  274.6 3.3 collective-permute-start.61
  284.1 3.5 %collective-permute-done.58 = bf16[16,2432]{1,0:T(8,128)(2,1)S(1)} collective-permute-done((bf16[16,2432]{1,0:T(8,128)(2,1)S(1)}, bf16[16,2432]{1,0:T(8,128)(2,1)S(1)}, u32[]{:S(2)}, u32[]{:S(2)}) %collective-permute-start.58) | collective-permute-done | bytes 77856 | tf_op jit(solution)/shard_map/ppermute | solution.py:957
  302.0 5.8 %collective-permute-done.67.refs_3_ = bf16[4,16,896]{2,1,0:T(8,128)(2,1)S(1)} collective-permute-done((bf16[4,16,896]{2,1,0:T(8,128)(2,1)}, bf16[4,16,896]{2,1,0:T(8,128)(2,1)S(1)}, u32[]{:S(2)}, u32[]{:S(2)}) %collective-permute-start.67) | collective-permute-done | bytes 114720 | tf_op jit(solution)/shard_map/ppermute | solution.py:630
  312.0 5.4 %settle.3 = bf16[4,512,1024]{2,1,0:T(8,128)(2,1)} custom-call(s32[4]{0:T(128)} %xor_add_fusion.where_ref, bf16[512,1024]{1,0:T(8,128)(2,1)} %copy-done.21, bf16[512,1024]{1,0:T(8,128)(2,1)} %copy-done.14, bf16[512,1024]{1,0:T(8,128)(2,1)} %collective-permute-done.65.refs_2_, bf16[512,1024]{1,0:T(8,128)(2,1)} %collective-permute-done.66.refs_3_), custom_call_target="tpu_custom_call" | custom-call | tf_op jit(solution)/shard_map/settle/pallas_call | solution.py:555
  325.7 4.4 %settle.4.refs_2_ = f32[4,512,1024]{2,1,0:T(8,128)} custom-call(s32[4]{0:T(128)} %xor_add_fusion.where_ref, bf16[512,1024]{1,0:T(8,128)(2,1)} %collective-permute-done.71.refs_0_, bf16[512,1024]{1,0:T(8,128)(2,1)} %collective-permute-done.72.refs_1_), custom_call_target="tpu_custom_call" | custom-call | tf_op jit(solution)/shard_map/settle/pallas_call | solution.py:555
  338.8 3.1 spread.3
  343.0 4.5 %settle.5 = f32[4,512,1024]{2,1,0:T(8,128)} custom-call(s32[4]{0:T(128)} %xor_add_fusion.where_ref, bf16[512,1024]{1,0:T(8,128)(2,1)} %copy-done.15, bf16[512,1024]{1,0:T(8,128)(2,1)} %copy-done.23, f32[4,512,1024]{2,1,0:T(8,128)} %settle.4.refs_2_), custom_call_target="tpu_custom_call", output_to_operand_aliasing={{}: (3, {})} | custom-call | tf_op jit(solution)/shard_map/settle/pallas_call | solution.py:555
  (411 shorter events, 153.1 us)
Async XLA Ops:
  2.1 20.1 %collective-permute-start.3 = (bf16[512,1024]{1,0:T(8,128)(2,1)S(1)}, bf16[512,1024]{1,0:T(8,128)(2,1)}, u32[]{:S(2)}, u32[]{:S(2)}) collective-permute-start(bf16[512,1024]{1,0:T(8,128)(2,1)S(1)} %dynamic-slice_bitcast_fusion.1), channel_id=1, source_target_pairs={{4,1},{6,3},{1,4},{3,6},{12,9},{14,11},{9,12},{11,14},{20,17},{22,... | collective-permute-start | bytes 3145736 | tf_op jit(solution)/shard_map/ppermute | solution.py:675
  6.8 20.0 %collective-permute-start.4 = (bf16[256,1024]{1,0:T(8,128)(2,1)S(1)}, bf16[256,1024]{1,0:T(8,128)(2,1)}, u32[]{:S(2)}, u32[]{:S(2)}) collective-permute-start(bf16[256,1024]{1,0:T(8,128)(2,1)S(1)} %constant_dynamic-update-slice_fusion.refs_0_), channel_id=1, source_target_pairs={{0,8},{8,16},{16,24},{24,0},{1,9},{9,17},{17,25},{25,1},{2,10},{10... | collective-permute-start | bytes 1572872 | tf_op jit(solution)/shard_map/ppermute | solution.py:630
  8.2 18.6 %collective-permute-start = (bf16[128,1024]{1,0:T(8,128)(2,1)S(1)}, bf16[128,1024]{1,0:T(8,128)(2,1)S(1)}, u32[]{:S(2)}, u32[]{:S(2)}) collective-permute-start(bf16[128,1024]{1,0:T(8,128)(2,1)S(1)} %pad_maximum_fusion.7.refs_0_), channel_id=1, source_target_pairs={{0,8},{8,16},{16,24},{24,0},{1,9},{9,17},{17,25},{25,1},{2,10},{10... | collective-permute-start | bytes 786440 | tf_op jit(solution)/shard_map/ppermute | solution.py:630
  9.5 17.2 %collective-permute-start.1 = (bf16[128,1024]{1,0:T(8,128)(2,1)S(1)}, bf16[128,1024]{1,0:T(8,128)(2,1)S(1)}, u32[]{:S(2)}, u32[]{:S(2)}) collective-permute-start(bf16[128,1024]{1,0:T(8,128)(2,1)S(1)} %pad_maximum_fusion.7.refs_0_), channel_id=1, source_target_pairs={{0,2},{1,5},{2,0},{3,7},{4,6},{5,1},{6,4},{7,3},{8,10},{9,13},{10,... | collective-permute-start | bytes 786440 | tf_op jit(solution)/shard_map/ppermute | solution.py:722
  9.5 17.2 %collective-permute-start.2 = (bf16[128,1024]{1,0:T(8,128)(2,1)S(1)}, bf16[128,1024]{1,0:T(8,128)(2,1)}, u32[]{:S(2)}, u32[]{:S(2)}) collective-permute-start(bf16[128,1024]{1,0:T(8,128)(2,1)S(1)} %pad_maximum_fusion.7.refs_0_), channel_id=1, source_target_pairs={{0,4},{1,3},{2,6},{3,1},{4,0},{5,7},{6,2},{7,5},{8,12},{9,11},{10,... | collective-permute-start | bytes 786440 | tf_op jit(solution)/shard_map/ppermute | solution.py:722
  26.8 16.9 %collective-permute-start.9 = (bf16[256,1024]{1,0:T(8,128)(2,1)S(1)}, bf16[256,1024]{1,0:T(8,128)(2,1)S(1)}, u32[]{:S(2)}, u32[]{:S(2)}) collective-permute-start(bf16[256,1024]{1,0:T(8,128)(2,1)S(1)} %constant_dynamic-update-slice_fusion.refs_0_), channel_id=1, source_target_pairs={{0,2},{1,5},{2,0},{3,7},{4,6},{5,1},{6,4},{7,3},{8,10},{9,13},{10,... | collective-permute-start | bytes 1572872 | tf_op jit(solution)/shard_map/ppermute | solution.py:722
  27.3 16.3 %collective-permute-start.6 = (bf16[128,1024]{1,0:T(8,128)(2,1)S(1)}, bf16[128,1024]{1,0:T(8,128)(2,1)}, u32[]{:S(2)}, u32[]{:S(2)}) collective-permute-start(bf16[128,1024]{1,0:T(8,128)(2,1)S(1)} %collective-permute-done.refs_4_), channel_id=1, source_target_pairs={{0,2},{1,5},{2,0},{3,7},{4,6},{5,1},{6,4},{7,3},{8,10},{9,13},{10,... | collective-permute-start | bytes 786440 | tf_op jit(solution)/shard_map/ppermute | solution.py:722
  92.5 33.1 %collective-permute-start.29 = (bf16[512,1024]{1,0:T(8,128)(2,1)S(1)}, bf16[512,1024]{1,0:T(8,128)(2,1)}, u32[]{:S(2)}, u32[]{:S(2)}) collective-permute-start(bf16[512,1024]{1,0:T(8,128)(2,1)S(1)} %dynamic-slice_bitcast_fusion), channel_id=1, source_target_pairs={{4,1},{6,3},{1,4},{3,6},{12,9},{14,11},{9,12},{11,14},{20,17},{22,... | collective-permute-start | bytes 3145736 | tf_op jit(solution)/shard_map/ppermute | solution.py:675
  98.0 29.4 %collective-permute-start.26 = (bf16[256,1024]{1,0:T(8,128)(2,1)}, bf16[256,1024]{1,0:T(8,128)(2,1)}, u32[]{:S(2)}, u32[]{:S(2)}) collective-permute-start(bf16[256,1024]{1,0:T(8,128)(2,1)} %collective-permute-done.4.refs_4_), channel_id=1, source_target_pairs={{0,4},{1,3},{2,6},{3,1},{4,0},{5,7},{6,2},{7,5},{8,12},{9,11},{10,... | collective-permute-start | bytes 1572872 | tf_op jit(solution)/shard_map/ppermute | solution.py:722
  112.5 15.6 %collective-permute-start.25 = (bf16[256,1024]{1,0:T(8,128)(2,1)}, bf16[256,1024]{1,0:T(8,128)(2,1)}, u32[]{:S(2)}, u32[]{:S(2)}) collective-permute-start(bf16[256,1024]{1,0:T(8,128)(2,1)} %collective-permute-done.21.refs_5_), channel_id=1, source_target_pairs={{0,8},{8,16},{16,24},{24,0},{1,9},{9,17},{17,25},{25,1},{2,10},{10... | collective-permute-start | bytes 1572872 | tf_op jit(solution)/shard_map/ppermute | solution.py:630
  132.3 15.6 %collective-permute-start.33 = (bf16[256,1024]{1,0:T(8,128)(2,1)}, bf16[256,1024]{1,0:T(8,128)(2,1)}, u32[]{:S(2)}, u32[]{:S(2)}) collective-permute-start(bf16[256,1024]{1,0:T(8,128)(2,1)} %collective-permute-done.25.refs_9_), channel_id=1, source_target_pairs={{0,8},{8,16},{16,24},{24,0},{1,9},{9,17},{17,25},{25,1},{2,10},{10... | collective-permute-start | bytes 1572872 | tf_op jit(solution)/shard_map/ppermute | solution.py:630
  132.5 16.2 %collective-permute-start.35 = (bf16[256,1024]{1,0:T(8,128)(2,1)}, bf16[256,1024]{1,0:T(8,128)(2,1)}, u32[]{:S(2)}, u32[]{:S(2)}) collective-permute-start(bf16[256,1024]{1,0:T(8,128)(2,1)} %collective-permute-done.25.refs_9_), channel_id=1, source_target_pairs={{0,4},{1,3},{2,6},{3,1},{4,0},{5,7},{6,2},{7,5},{8,12},{9,11},{10,... | collective-permute-start | bytes 1572872 | tf_op jit(solution)/shard_map/ppermute | solution.py:722
  195.6 17.9 %collective-permute-start.47 = (bf16[512,1024]{1,0:T(8,128)(2,1)}, bf16[512,1024]{1,0:T(8,128)(2,1)S(1)}, u32[]{:S(2)}, u32[]{:S(2)}) collective-permute-start(bf16[512,1024]{1,0:T(8,128)(2,1)} %get-tuple-element.246), channel_id=1, source_target_pairs={{0,1},{1,0},{2,3},{3,2},{4,5},{5,4},{6,7},{7,6},{8,9},{9,8},{10,11... | collective-permute-start | bytes 3145736 | tf_op jit(solution)/shard_map/ppermute | solution.py:633
  225.8 17.0 %collective-permute-start.50 = (bf16[512,1024]{1,0:T(8,128)(2,1)}, bf16[512,1024]{1,0:T(8,128)(2,1)S(1)}, u32[]{:S(2)}, u32[]{:S(2)}) collective-permute-start(bf16[512,1024]{1,0:T(8,128)(2,1)} %add_convert_fusion.2), channel_id=1, source_target_pairs={{0,2},{1,4},{2,0},{3,6},{4,1},{5,7},{6,3},{7,5},{8,10},{9,12},{10,... | collective-permute-start | bytes 3145736 | tf_op jit(solution)/shard_map/ppermute | solution.py:695
  226.7 16.1 %collective-permute-start.49 = (bf16[2,16,3200]{2,1,0:T(8,128)(2,1)}, bf16[2,16,3200]{2,1,0:T(8,128)(2,1)}, u32[]{:S(2)}, u32[]{:S(2)}) collective-permute-start(bf16[2,16,3200]{2,1,0:T(8,128)(2,1)} %collective-permute-done.43.refs_1_), channel_id=1, source_target_pairs={{0,8},{8,16},{16,24},{24,0},{1,9},{9,17},{17,25},{25,1},{2,10},{10... | collective-permute-start | bytes 614408 | tf_op jit(solution)/shard_map/ppermute | solution.py:630
  242.8 22.0 %collective-permute-start.55 = (bf16[512,1024]{1,0:T(8,128)(2,1)S(1)}, bf16[512,1024]{1,0:T(8,128)(2,1)S(1)}, u32[]{:S(2)}, u32[]{:S(2)}) collective-permute-start(bf16[512,1024]{1,0:T(8,128)(2,1)S(1)} %collective-permute-done.50.refs_0_), channel_id=1, source_target_pairs={{1,3},{3,1},{4,6},{6,4},{9,11},{11,9},{12,14},{14,12},{17,19},{19,... | collective-permute-start | bytes 3145736 | tf_op jit(solution)/shard_map/ppermute | solution.py:700
  246.1 18.9 %collective-permute-start.52 = (bf16[2,16,3200]{2,1,0:T(8,128)(2,1)}, bf16[2,16,3200]{2,1,0:T(8,128)(2,1)}, u32[]{:S(2)}, u32[]{:S(2)}) collective-permute-start(bf16[2,16,3200]{2,1,0:T(8,128)(2,1)} %collective-permute-done.43.refs_1_), channel_id=1, source_target_pairs={{0,4},{4,0},{1,5},{5,1},{2,6},{6,2},{3,7},{7,3},{8,12},{12,8},{9,1... | collective-permute-start | bytes 614408 | tf_op jit(solution)/shard_map/ppermute | solution.py:970
  246.3 18.7 %collective-permute-start.53 = (bf16[2,16,3200]{2,1,0:T(8,128)(2,1)}, bf16[2,16,3200]{2,1,0:T(8,128)(2,1)}, u32[]{:S(2)}, u32[]{:S(2)}) collective-permute-start(bf16[2,16,3200]{2,1,0:T(8,128)(2,1)} %collective-permute-done.49.refs_2_), channel_id=1, source_target_pairs={{0,4},{4,0},{1,5},{5,1},{2,6},{6,2},{3,7},{7,3},{8,12},{12,8},{9,1... | collective-permute-start | bytes 614408 | tf_op jit(solution)/shard_map/ppermute | solution.py:970
  247.5 17.5 %collective-permute-start.54 = (bf16[2,16,3200]{2,1,0:T(8,128)(2,1)}, bf16[2,16,3200]{2,1,0:T(8,128)(2,1)}, u32[]{:S(2)}, u32[]{:S(2)}) collective-permute-start(bf16[2,16,3200]{2,1,0:T(8,128)(2,1)} %collective-permute-done.49.refs_2_), channel_id=1, source_target_pairs={{0,8},{8,16},{16,24},{24,0},{1,9},{9,17},{17,25},{25,1},{2,10},{10... | collective-permute-start | bytes 614408 | tf_op jit(solution)/shard_map/ppermute | solution.py:630
  248.4 16.6 %collective-permute-start.51 = (bf16[4,16,896]{2,1,0:T(8,128)(2,1)S(1)}, bf16[4,16,896]{2,1,0:T(8,128)(2,1)}, u32[]{:S(2)}, u32[]{:S(2)}) collective-permute-start(bf16[4,16,896]{2,1,0:T(8,128)(2,1)S(1)} %constant_dynamic-update-slice_fusion.12.refs_0_), channel_id=1, source_target_pairs={{0,8},{8,16},{16,24},{24,0},{1,9},{9,17},{17,25},{25,1},{2,10},{10... | collective-permute-start | bytes 344072 | tf_op jit(solution)/shard_map/ppermute | solution.py:630
  274.6 16.3 %collective-permute-start.61 = (f32[512,1024]{1,0:T(8,128)S(1)}, f32[512,1024]{1,0:T(8,128)S(1)}, u32[]{:S(2)}, u32[]{:S(2)}) collective-permute-start(f32[512,1024]{1,0:T(8,128)S(1)} %fusion.1), channel_id=1, source_target_pairs={{0,1},{1,0},{2,3},{3,2},{4,5},{5,4},{6,7},{7,6},{8,9},{9,8},{10,11... | collective-permute-start | bytes 6291464 | tf_op jit(solution)/shard_map/ppermute | solution.py:633
  278.0 15.7 %collective-permute-start.63 = (bf16[2,16,3200]{2,1,0:T(8,128)(2,1)}, bf16[2,16,3200]{2,1,0:T(8,128)(2,1)S(1)}, u32[]{:S(2)}, u32[]{:S(2)}) collective-permute-start(bf16[2,16,3200]{2,1,0:T(8,128)(2,1)} %collective-permute-done.54.refs_3_), channel_id=1, source_target_pairs={{0,4},{4,0},{1,5},{5,1},{2,6},{6,2},{3,7},{7,3},{8,12},{12,8},{9,1... | collective-permute-start | bytes 614408 | tf_op jit(solution)/shard_map/ppermute | solution.py:970
  296.2 21.2 %collective-permute-start.71 = (bf16[512,1024]{1,0:T(8,128)(2,1)S(1)}, bf16[512,1024]{1,0:T(8,128)(2,1)}, u32[]{:S(2)}, u32[]{:S(2)}) collective-permute-start(bf16[512,1024]{1,0:T(8,128)(2,1)S(1)} %add_convert_fusion.1), channel_id=1, source_target_pairs={{0,2},{1,4},{2,0},{3,6},{4,1},{5,7},{6,3},{7,5},{8,10},{9,12},{10,... | collective-permute-start | bytes 3145736 | tf_op jit(solution)/shard_map/ppermute | solution.py:695
  318.2 15.7 %collective-permute-start.76 = (bf16[512,1024]{1,0:T(8,128)(2,1)}, bf16[512,1024]{1,0:T(8,128)(2,1)S(1)}, u32[]{:S(2)}, u32[]{:S(2)}) collective-permute-start(bf16[512,1024]{1,0:T(8,128)(2,1)} %collective-permute-done.71.refs_0_), channel_id=1, source_target_pairs={{1,3},{3,1},{4,6},{6,4},{9,11},{11,9},{12,14},{14,12},{17,19},{19,... | collective-permute-start | bytes 3145736 | tf_op jit(solution)/shard_map/ppermute | solution.py:700
  (138 other events, 1215.2 us)

commit v3 on v2

--- a/solution.py
+++ b/solution.py
@@ -930,6 +930,7 @@
         n2_own, n2_far, gb, down_t[3 * rank :], out_t[1], ff_parts, ff_moves, ff_place, fc1_lift, fc2_t
     )
     ranks = (rank_own + swap(rank_far)).astype(BF16)
+    ranks, gn2_far, branch_far = fence(ranks, gn2_far, branch_far)
     m_own, gf_own = ranks[:rank], ranks[rank:]
     branch = branch_own + swap(branch_far).astype(F32) + dot_tn(m_own, out_t[1])
     result_own = (h + layer_scale[1] * branch).astype(BF16)
@@ -1010,10 +1011,9 @@
             mid_line = [pair_up(mid, mid_over)]
             mid_line.append(hop(mid_line[0], "shard"))
             sent = send_second(result_own, sent)
-    g_heads, mid_line[1], early_over[1], early_over[2], *got = fence(
-        g_heads, mid_line[1], early_over[1], early_over[2], *early_line[3:], *sent
-    )
-    early_line[3:], sent = got[: shards - 3], got[shards - 3 :]
+    g_heads, mid_line[1], early_over[1], early_over[2], *early_line[3:] = fence(
+        g_heads, mid_line[1], early_over[1], early_over[2], *early_line[3:]
+    )
     early_over.extend([over(block) for block in early_line[3:]])
     mid_line.append(hop(mid_line[1], "shard"))
     g = to_rows(g_heads, 3)

time: 349 us -> 344 us (0.986)
    ppermute x9, starting transfers between devices: 7.39 us -> 11.3 us  [over(): return lax.ppermute(block, 'context', opposite)]
    unnamed x178 -> x200, local copies, waits for them, and re-layouts: 11.9 us -> 10.2 us
  transfers between devices with their start and end apart: 79 -> 79, of which waited for: 26 -> 27; matrix products, arithmetic and copies ran while one was open for 12% -> 13% of each run, Pallas kernels for 26% -> 26%
where the time goes in v3:
time: 344 us; the launch traced here: 342 us
  Pallas kernels  130 us (38%)
  starting transfers between devices  73.5 us (21%)
  waiting for transfers between devices  72.3 us (21%)
  matrix products  25.6 us (7%)
  other arithmetic  18.9 us (5%)
  local copies, waits for them, and re-layouts  16.2 us (5%)
  between operations  5.02 us (1%)
    pallas_call x1, Pallas kernels, mlp(): pl.pallas_call(functools.partial(mlp_kernel, block, own, moves, len(parts...  35.6 us
    pallas_call x2, Pallas kernels, attend_back(): pl.pallas_call(functools.partial(attend_back_kernel, block, near), grid=(...  30.8 us
    ppermute x18, waiting for transfers between devices, hop(): return lax.ppermute(value, axis, ring[axis])  29.1 us
    pallas_call x2, Pallas kernels, attend(): pl.pallas_call(functools.partial(attend_kernel, block), grid=(near,), in_...  22.4 us
    ppermute x21, waiting for transfers between devices, cross_to(): return lax.ppermute(value, plane, cross[turn])  21.4 us
    ppermute x21, starting transfers between devices, cross_to(): return lax.ppermute(value, plane, cross[turn])  18.6 us
    pallas_call x3, Pallas kernels, settle(): pl.pallas_call(functools.partial(settle_kernel, len(parts)), grid_spec=pl...  14.3 us
    ppermute x21, starting transfers between devices, swap(): return lax.ppermute(value, 'tensor', twin)  12 us
  transfers between devices with their start and end apart: 79, of which 27 were waited for; matrix products, arithmetic and copies ran while one was open for 13% of the time, Pallas kernels for 26%

profile of v3, /device:TPU:1, one launch (start us, length us, event | category | flops | bytes accessed | tf_op | source)
XLA Modules:
  0.0 341.9 jit_solution(2500564538171388192)
XLA Ops:
  2.1 4.5 %collective-permute-start.3 = (bf16[512,1024]{1,0:T(8,128)(2,1)S(1)}, bf16[512,1024]{1,0:T(8,128)(2,1)}, u32[]{:S(2)}, u32[]{:S(2)}) collective-permute-start(bf16[512,1024]{1,0:T(8,128)(2,1)S(1)} %dynamic-slice_bitcast_fusion.1), channel_id=1, source_target_pairs={{4,1},{6,3},{1,4},{3,6},{12,9},{14,11},{9,12},{11,14},{20,17},{22,... | collective-permute-start | bytes 3145736 | tf_op jit(solution)/shard_map/ppermute | solution.py:675
  12.0 10.3 %collective-permute-done.3 = bf16[512,1024]{1,0:T(8,128)(2,1)} collective-permute-done((bf16[512,1024]{1,0:T(8,128)(2,1)S(1)}, bf16[512,1024]{1,0:T(8,128)(2,1)}, u32[]{:S(2)}, u32[]{:S(2)}) %collective-permute-start.3) | collective-permute-done | bytes 1048608 | tf_op jit(solution)/shard_map/ppermute | solution.py:675
  29.7 5.6 %collective-permute-done.5.refs_8_ = bf16[128,1024]{1,0:T(8,128)(2,1)} collective-permute-done((bf16[128,1024]{1,0:T(8,128)(2,1)S(1)}, bf16[128,1024]{1,0:T(8,128)(2,1)}, u32[]{:S(2)}, u32[]{:S(2)}) %collective-permute-start.5) | collective-permute-done | bytes 262176 | tf_op jit(solution)/shard_map/ppermute | solution.py:630
  35.3 8.3 %collective-permute-done.6.refs_5_ = bf16[128,1024]{1,0:T(8,128)(2,1)} collective-permute-done((bf16[128,1024]{1,0:T(8,128)(2,1)S(1)}, bf16[128,1024]{1,0:T(8,128)(2,1)}, u32[]{:S(2)}, u32[]{:S(2)}) %collective-permute-start.6) | collective-permute-done | bytes 262176 | tf_op jit(solution)/shard_map/ppermute | solution.py:722
  61.8 3.2 subtract_multiply_fusion
  66.6 3.0 collective-permute-done.17.refs_11_
  78.3 10.2 %project.1 = (bf16[1024,1536]{1,0:T(8,128)(2,1)}, bf16[1024,512]{1,0:T(8,128)(2,1)}, bf16[1024,1536]{1,0:T(8,128)(2,1)}) custom-call(s32[2,16]{1,0:T(2,128)} %pad_add_fusion.place_ref, bf16[1024,1024]{1,0:T(8,128)(2,1)} %copy-done.4, bf16[48,1024]{1,0:T(8,128)(2,1)} %convolution_convert_fusion.1.u_ref, bf16[48,1536]{1,0:T(8,128)(2,1)} %get-tuple-element.194.lift_ref, ...), custom_call_target="tpu_custom_call" | custom-call | flops 1000 | bytes 1000 | tf_op jit(solution)/shard_map/project/pallas_call | solution.py:392
  92.4 4.6 %collective-permute-start.29 = (bf16[512,1024]{1,0:T(8,128)(2,1)S(1)}, bf16[512,1024]{1,0:T(8,128)(2,1)}, u32[]{:S(2)}, u32[]{:S(2)}) collective-permute-start(bf16[512,1024]{1,0:T(8,128)(2,1)S(1)} %dynamic-slice_bitcast_fusion), channel_id=1, source_target_pairs={{4,1},{6,3},{1,4},{3,6},{12,9},{14,11},{9,12},{11,14},{20,17},{22,... | collective-permute-start | bytes 3145736 | tf_op jit(solution)/shard_map/ppermute | solution.py:675
  98.9 11.2 %attend.2 = (bf16[1024,512]{1,0:T(8,128)(2,1)}, f32[2,8,1024]{2,1,0:T(8,128)}) custom-call(bf16[1024,1536]{1,0:T(8,128)(2,1)} %get-tuple-element.212.q_ref.k_ref.v_ref._, bf16[1024,1536]{1,0:T(8,128)(2,1)} %get-tuple-element.212.q_ref.k_ref.v_ref._, bf16[1024,1536]{1,0:T(8,128)(2,1)} %get-tuple-element.212.q_ref.k_ref.v_ref._, ...), custom_call_target="tpu_custom_call" | custom-call | flops 1000 | bytes 1000 | tf_op jit(solution)/shard_map/attend/pallas_call | solution.py:83
  113.8 11.2 %attend.3 = (bf16[1024,512]{1,0:T(8,128)(2,1)}, f32[2,8,1024]{2,1,0:T(8,128)}) custom-call(bf16[1024,1536]{1,0:T(8,128)(2,1)} %get-tuple-element.212.q_ref.k_ref.v_ref._, bf16[1024,1536]{1,0:T(8,128)(2,1)} %get-tuple-element.212.q_ref.k_ref.v_ref._, bf16[1024,1536]{1,0:T(8,128)(2,1)} %get-tuple-element.212.q_ref.k_ref.v_ref._, ...), custom_call_target="tpu_custom_call", output_to_operand_aliasing={{0}: (3, {})} | custom-call | flops 1000 | bytes 1000 | tf_op jit(solution)/shard_map/attend/pallas_call | solution.py:83
  141.5 6.1 %collective-permute-done.33.refs_13_ = bf16[256,1024]{1,0:T(8,128)(2,1)} collective-permute-done((bf16[256,1024]{1,0:T(8,128)(2,1)}, bf16[256,1024]{1,0:T(8,128)(2,1)}, u32[]{:S(2)}, u32[]{:S(2)}) %collective-permute-start.33) | collective-permute-done | bytes 524320 | tf_op jit(solution)/shard_map/ppermute | solution.py:630
  153.8 4.5 %collective-permute-done.37.refs_15_ = bf16[256,1024]{1,0:T(8,128)(2,1)} collective-permute-done((bf16[256,1024]{1,0:T(8,128)(2,1)}, bf16[256,1024]{1,0:T(8,128)(2,1)}, u32[]{:S(2)}, u32[]{:S(2)}) %collective-permute-start.37) | collective-permute-done | bytes 524320 | tf_op jit(solution)/shard_map/ppermute | solution.py:722
  158.3 35.6 %mlp.1 = (f32[512,1024]{1,0:T(8,128)}, bf16[512,1024]{1,0:T(8,128)(2,1)}, f32[512,1024]{1,0:T(8,128)}, f32[512,1024]{1,0:T(8,128)}, f32[32,512]{1,0:T(8,128)}, /...) custom-call(s32[2,32]{1,0:T(2,128)} %add_add_fusion.place_ref, ...), custom_call_target="tpu_custom_call" | custom-call | flops 1000 | bytes 1000 | tf_op jit(solution)/shard_map/mlp/pallas_call | solution.py:306
  217.5 5.0 %collective-permute-done.43.refs_1_ = bf16[2,16,3200]{2,1,0:T(8,128)(2,1)S(1)} collective-permute-done((bf16[2,16,3200]{2,1,0:T(8,128)(2,1)S(1)}, bf16[2,16,3200]{2,1,0:T(8,128)(2,1)S(1)}, u32[]{:S(2)}, u32[]{:S(2)}) %collective-permute-start.43) | collective-permute-done | bytes 204832 | tf_op jit(solution)/shard_map/ppermute | solution.py:630
  225.5 15.3 %attend_back.2._ = bf16[1024,1536]{1,0:T(8,128)(2,1)} custom-call(bf16[1024,1536]{1,0:T(8,128)(2,1)} %get-tuple-element.212.q_ref.k_ref.v_ref._, bf16[1024,1536]{1,0:T(8,128)(2,1)} %get-tuple-element.212.q_ref.k_ref.v_ref._, bf16[1024,1536]{1,0:T(8,128)(2,1)} %get-tuple-element.212.q_ref.k_ref.v_ref._, bf16[1024,512]{1,0:T(8,128)(2,1)} %add_convert_fusion.3.go_ref, ...), custom_call_target="tpu_custom_call" | custom-call | flops 1000 | bytes 1000 | tf_op jit(solution)/shard_map/attend_back/pallas_call | solution.py:156
  246.2 15.4 %attend_back.3 = bf16[1024,1536]{1,0:T(8,128)(2,1)} custom-call(bf16[1024,1536]{1,0:T(8,128)(2,1)} %get-tuple-element.212.q_ref.k_ref.v_ref._, bf16[1024,1536]{1,0:T(8,128)(2,1)} %get-tuple-element.212.q_ref.k_ref.v_ref._, bf16[1024,1536]{1,0:T(8,128)(2,1)} %get-tuple-element.212.q_ref.k_ref.v_ref._, ...), custom_call_target="tpu_custom_call", output_to_operand_aliasing={{}: (6, {})} | custom-call | flops 1000 | bytes 1000 | tf_op jit(solution)/shard_map/attend_back/pallas_call | solution.py:156
  262.4 4.3 %fusion.1 = f32[512,1024]{1,0:T(8,128)S(1)} fusion(bf16[1024,1536]{1,0:T(8,128)(2,1)} %get-tuple-element.261, bf16[1024,1536]{1,0:T(8,128)(2,1)} %attend_back.3), kind=kOutput, calls=%fused_computation.23 | convolution fusion | flops 1610612736 | bytes 6815744 | tf_op jit(solution)/shard_map/dot_general | solution.py:29
  271.0 3.2 collective-permute-start.62
  278.6 3.5 %collective-permute-done.57 = bf16[16,2432]{1,0:T(8,128)(2,1)S(1)} collective-permute-done((bf16[16,2432]{1,0:T(8,128)(2,1)S(1)}, bf16[16,2432]{1,0:T(8,128)(2,1)S(1)}, u32[]{:S(2)}, u32[]{:S(2)}) %collective-permute-start.57) | collective-permute-done | bytes 77856 | tf_op jit(solution)/shard_map/ppermute | solution.py:958
  296.5 6.3 %collective-permute-done.67.refs_3_ = bf16[4,16,896]{2,1,0:T(8,128)(2,1)S(1)} collective-permute-done((bf16[4,16,896]{2,1,0:T(8,128)(2,1)}, bf16[4,16,896]{2,1,0:T(8,128)(2,1)S(1)}, u32[]{:S(2)}, u32[]{:S(2)}) %collective-permute-start.67) | collective-permute-done | bytes 114720 | tf_op jit(solution)/shard_map/ppermute | solution.py:630
  306.5 5.4 %settle.3 = bf16[4,512,1024]{2,1,0:T(8,128)(2,1)} custom-call(s32[4]{0:T(128)} %xor_add_fusion.where_ref, bf16[512,1024]{1,0:T(8,128)(2,1)} %copy-done.21, bf16[512,1024]{1,0:T(8,128)(2,1)} %copy-done.14, bf16[512,1024]{1,0:T(8,128)(2,1)} %collective-permute-done.65.refs_2_, bf16[512,1024]{1,0:T(8,128)(2,1)} %collective-permute-done.66.refs_3_), custom_call_target="tpu_custom_call" | custom-call | tf_op jit(solution)/shard_map/settle/pallas_call | solution.py:555
  320.3 4.4 %settle.4.refs_2_ = f32[4,512,1024]{2,1,0:T(8,128)} custom-call(s32[4]{0:T(128)} %xor_add_fusion.where_ref, bf16[512,1024]{1,0:T(8,128)(2,1)} %collective-permute-done.71.refs_0_, bf16[512,1024]{1,0:T(8,128)(2,1)} %collective-permute-done.72.refs_1_), custom_call_target="tpu_custom_call" | custom-call | tf_op jit(solution)/shard_map/settle/pallas_call | solution.py:555
  333.2 3.1 spread.3
  337.4 4.5 %settle.5 = f32[4,512,1024]{2,1,0:T(8,128)} custom-call(s32[4]{0:T(128)} %xor_add_fusion.where_ref, bf16[512,1024]{1,0:T(8,128)(2,1)} %copy-done.15, bf16[512,1024]{1,0:T(8,128)(2,1)} %copy-done.23, f32[4,512,1024]{2,1,0:T(8,128)} %settle.4.refs_2_), custom_call_target="tpu_custom_call", output_to_operand_aliasing={{}: (3, {})} | custom-call | tf_op jit(solution)/shard_map/settle/pallas_call | solution.py:555
  (434 shorter events, 148.1 us)
Async XLA Ops:
  2.1 20.1 %collective-permute-start.3 = (bf16[512,1024]{1,0:T(8,128)(2,1)S(1)}, bf16[512,1024]{1,0:T(8,128)(2,1)}, u32[]{:S(2)}, u32[]{:S(2)}) collective-permute-start(bf16[512,1024]{1,0:T(8,128)(2,1)S(1)} %dynamic-slice_bitcast_fusion.1), channel_id=1, source_target_pairs={{4,1},{6,3},{1,4},{3,6},{12,9},{14,11},{9,12},{11,14},{20,17},{22,... | collective-permute-start | bytes 3145736 | tf_op jit(solution)/shard_map/ppermute | solution.py:675
  6.8 20.0 %collective-permute-start.4 = (bf16[256,1024]{1,0:T(8,128)(2,1)S(1)}, bf16[256,1024]{1,0:T(8,128)(2,1)}, u32[]{:S(2)}, u32[]{:S(2)}) collective-permute-start(bf16[256,1024]{1,0:T(8,128)(2,1)S(1)} %constant_dynamic-update-slice_fusion.refs_0_), channel_id=1, source_target_pairs={{0,8},{8,16},{16,24},{24,0},{1,9},{9,17},{17,25},{25,1},{2,10},{10... | collective-permute-start | bytes 1572872 | tf_op jit(solution)/shard_map/ppermute | solution.py:630
  8.2 18.5 %collective-permute-start = (bf16[128,1024]{1,0:T(8,128)(2,1)S(1)}, bf16[128,1024]{1,0:T(8,128)(2,1)S(1)}, u32[]{:S(2)}, u32[]{:S(2)}) collective-permute-start(bf16[128,1024]{1,0:T(8,128)(2,1)S(1)} %pad_maximum_fusion.7.refs_0_), channel_id=1, source_target_pairs={{0,8},{8,16},{16,24},{24,0},{1,9},{9,17},{17,25},{25,1},{2,10},{10... | collective-permute-start | bytes 786440 | tf_op jit(solution)/shard_map/ppermute | solution.py:630
  9.5 17.2 %collective-permute-start.1 = (bf16[128,1024]{1,0:T(8,128)(2,1)S(1)}, bf16[128,1024]{1,0:T(8,128)(2,1)S(1)}, u32[]{:S(2)}, u32[]{:S(2)}) collective-permute-start(bf16[128,1024]{1,0:T(8,128)(2,1)S(1)} %pad_maximum_fusion.7.refs_0_), channel_id=1, source_target_pairs={{0,2},{1,5},{2,0},{3,7},{4,6},{5,1},{6,4},{7,3},{8,10},{9,13},{10,... | collective-permute-start | bytes 786440 | tf_op jit(solution)/shard_map/ppermute | solution.py:722
  9.5 17.2 %collective-permute-start.2 = (bf16[128,1024]{1,0:T(8,128)(2,1)S(1)}, bf16[128,1024]{1,0:T(8,128)(2,1)}, u32[]{:S(2)}, u32[]{:S(2)}) collective-permute-start(bf16[128,1024]{1,0:T(8,128)(2,1)S(1)} %pad_maximum_fusion.7.refs_0_), channel_id=1, source_target_pairs={{0,4},{1,3},{2,6},{3,1},{4,0},{5,7},{6,2},{7,5},{8,12},{9,11},{10,... | collective-permute-start | bytes 786440 | tf_op jit(solution)/shard_map/ppermute | solution.py:722
  26.7 16.9 %collective-permute-start.9 = (bf16[256,1024]{1,0:T(8,128)(2,1)S(1)}, bf16[256,1024]{1,0:T(8,128)(2,1)S(1)}, u32[]{:S(2)}, u32[]{:S(2)}) collective-permute-start(bf16[256,1024]{1,0:T(8,128)(2,1)S(1)} %constant_dynamic-update-slice_fusion.refs_0_), channel_id=1, source_target_pairs={{0,2},{1,5},{2,0},{3,7},{4,6},{5,1},{6,4},{7,3},{8,10},{9,13},{10,... | collective-permute-start | bytes 1572872 | tf_op jit(solution)/shard_map/ppermute | solution.py:722
  27.3 16.3 %collective-permute-start.6 = (bf16[128,1024]{1,0:T(8,128)(2,1)S(1)}, bf16[128,1024]{1,0:T(8,128)(2,1)}, u32[]{:S(2)}, u32[]{:S(2)}) collective-permute-start(bf16[128,1024]{1,0:T(8,128)(2,1)S(1)} %collective-permute-done.refs_4_), channel_id=1, source_target_pairs={{0,2},{1,5},{2,0},{3,7},{4,6},{5,1},{6,4},{7,3},{8,10},{9,13},{10,... | collective-permute-start | bytes 786440 | tf_op jit(solution)/shard_map/ppermute | solution.py:722
  92.4 32.7 %collective-permute-start.29 = (bf16[512,1024]{1,0:T(8,128)(2,1)S(1)}, bf16[512,1024]{1,0:T(8,128)(2,1)}, u32[]{:S(2)}, u32[]{:S(2)}) collective-permute-start(bf16[512,1024]{1,0:T(8,128)(2,1)S(1)} %dynamic-slice_bitcast_fusion), channel_id=1, source_target_pairs={{4,1},{6,3},{1,4},{3,6},{12,9},{14,11},{9,12},{11,14},{20,17},{22,... | collective-permute-start | bytes 3145736 | tf_op jit(solution)/shard_map/ppermute | solution.py:675
  97.7 29.2 %collective-permute-start.26 = (bf16[256,1024]{1,0:T(8,128)(2,1)}, bf16[256,1024]{1,0:T(8,128)(2,1)}, u32[]{:S(2)}, u32[]{:S(2)}) collective-permute-start(bf16[256,1024]{1,0:T(8,128)(2,1)} %collective-permute-done.4.refs_4_), channel_id=1, source_target_pairs={{0,4},{1,3},{2,6},{3,1},{4,0},{5,7},{6,2},{7,5},{8,12},{9,11},{10,... | collective-permute-start | bytes 1572872 | tf_op jit(solution)/shard_map/ppermute | solution.py:722
  112.2 15.4 %collective-permute-start.25 = (bf16[256,1024]{1,0:T(8,128)(2,1)}, bf16[256,1024]{1,0:T(8,128)(2,1)}, u32[]{:S(2)}, u32[]{:S(2)}) collective-permute-start(bf16[256,1024]{1,0:T(8,128)(2,1)} %collective-permute-done.21.refs_5_), channel_id=1, source_target_pairs={{0,8},{8,16},{16,24},{24,0},{1,9},{9,17},{17,25},{25,1},{2,10},{10... | collective-permute-start | bytes 1572872 | tf_op jit(solution)/shard_map/ppermute | solution.py:630
  112.2 15.4 %collective-permute-start.27 = (bf16[256,1024]{1,0:T(8,128)(2,1)}, bf16[256,1024]{1,0:T(8,128)(2,1)}, u32[]{:S(2)}, u32[]{:S(2)}) collective-permute-start(bf16[256,1024]{1,0:T(8,128)(2,1)} %collective-permute-done.20.refs_8_), channel_id=1, source_target_pairs={{0,4},{1,3},{2,6},{3,1},{4,0},{5,7},{6,2},{7,5},{8,12},{9,11},{10,... | collective-permute-start | bytes 1572872 | tf_op jit(solution)/shard_map/ppermute | solution.py:722
  132.0 15.6 %collective-permute-start.33 = (bf16[256,1024]{1,0:T(8,128)(2,1)}, bf16[256,1024]{1,0:T(8,128)(2,1)}, u32[]{:S(2)}, u32[]{:S(2)}) collective-permute-start(bf16[256,1024]{1,0:T(8,128)(2,1)} %collective-permute-done.25.refs_9_), channel_id=1, source_target_pairs={{0,8},{8,16},{16,24},{24,0},{1,9},{9,17},{17,25},{25,1},{2,10},{10... | collective-permute-start | bytes 1572872 | tf_op jit(solution)/shard_map/ppermute | solution.py:630
  132.2 16.2 %collective-permute-start.35 = (bf16[256,1024]{1,0:T(8,128)(2,1)}, bf16[256,1024]{1,0:T(8,128)(2,1)}, u32[]{:S(2)}, u32[]{:S(2)}) collective-permute-start(bf16[256,1024]{1,0:T(8,128)(2,1)} %collective-permute-done.25.refs_9_), channel_id=1, source_target_pairs={{0,4},{1,3},{2,6},{3,1},{4,0},{5,7},{6,2},{7,5},{8,12},{9,11},{10,... | collective-permute-start | bytes 1572872 | tf_op jit(solution)/shard_map/ppermute | solution.py:722
  222.5 18.5 %collective-permute-start.50 = (bf16[512,1024]{1,0:T(8,128)(2,1)}, bf16[512,1024]{1,0:T(8,128)(2,1)S(1)}, u32[]{:S(2)}, u32[]{:S(2)}) collective-permute-start(bf16[512,1024]{1,0:T(8,128)(2,1)} %add_convert_fusion.2), channel_id=1, source_target_pairs={{0,2},{1,4},{2,0},{3,6},{4,1},{5,7},{6,3},{7,5},{8,10},{9,12},{10,... | collective-permute-start | bytes 3145736 | tf_op jit(solution)/shard_map/ppermute | solution.py:695
  223.4 17.6 %collective-permute-start.49 = (bf16[2,16,3200]{2,1,0:T(8,128)(2,1)S(1)}, bf16[2,16,3200]{2,1,0:T(8,128)(2,1)S(1)}, u32[]{:S(2)}, u32[]{:S(2)}) collective-permute-start(bf16[2,16,3200]{2,1,0:T(8,128)(2,1)S(1)} %collective-permute-done.43.refs_1_), channel_id=1, source_target_pairs={{0,8},{8,16},{16,24},{24,0},{1,9},{9,17},{17,25},{25,1},{2,10},{10... | collective-permute-start | bytes 614408 | tf_op jit(solution)/shard_map/ppermute | solution.py:630
  224.0 37.6 %collective-permute-start.52 = (bf16[2,16,3200]{2,1,0:T(8,128)(2,1)S(1)}, bf16[2,16,3200]{2,1,0:T(8,128)(2,1)S(1)}, u32[]{:S(2)}, u32[]{:S(2)}) collective-permute-start(bf16[2,16,3200]{2,1,0:T(8,128)(2,1)S(1)} %collective-permute-done.43.refs_1_), channel_id=1, source_target_pairs={{0,4},{4,0},{1,5},{5,1},{2,6},{6,2},{3,7},{7,3},{8,12},{12,8},{9,1... | collective-permute-start | bytes 614408 | tf_op jit(solution)/shard_map/ppermute | solution.py:971
  224.0 16.9 %collective-permute-start.48 = (bf16[2,16,896]{2,1,0:T(8,128)(2,1)S(1)}, bf16[2,16,896]{2,1,0:T(8,128)(2,1)S(1)}, u32[]{:S(2)}, u32[]{:S(2)}) collective-permute-start(bf16[2,16,896]{2,1,0:T(8,128)(2,1)S(1)} %pad_maximum_fusion.11), channel_id=1, source_target_pairs={{0,4},{4,0},{1,5},{5,1},{2,6},{6,2},{3,7},{7,3},{8,12},{12,8},{9,1... | collective-permute-start | bytes 172040 | tf_op jit(solution)/shard_map/ppermute | solution.py:971
  241.0 20.7 %collective-permute-start.53 = (bf16[2,16,3200]{2,1,0:T(8,128)(2,1)S(1)}, bf16[2,16,3200]{2,1,0:T(8,128)(2,1)S(1)}, u32[]{:S(2)}, u32[]{:S(2)}) collective-permute-start(bf16[2,16,3200]{2,1,0:T(8,128)(2,1)S(1)} %collective-permute-done.49.refs_2_), channel_id=1, source_target_pairs={{0,4},{4,0},{1,5},{5,1},{2,6},{6,2},{3,7},{7,3},{8,12},{12,8},{9,1... | collective-permute-start | bytes 614408 | tf_op jit(solution)/shard_map/ppermute | solution.py:971
  243.0 18.7 %collective-permute-start.54 = (bf16[2,16,3200]{2,1,0:T(8,128)(2,1)S(1)}, bf16[2,16,3200]{2,1,0:T(8,128)(2,1)}, u32[]{:S(2)}, u32[]{:S(2)}) collective-permute-start(bf16[2,16,3200]{2,1,0:T(8,128)(2,1)S(1)} %collective-permute-done.49.refs_2_), channel_id=1, source_target_pairs={{0,8},{8,16},{16,24},{24,0},{1,9},{9,17},{17,25},{25,1},{2,10},{10... | collective-permute-start | bytes 614408 | tf_op jit(solution)/shard_map/ppermute | solution.py:630
  243.6 18.1 %collective-permute-start.51 = (bf16[4,16,896]{2,1,0:T(8,128)(2,1)S(1)}, bf16[4,16,896]{2,1,0:T(8,128)(2,1)}, u32[]{:S(2)}, u32[]{:S(2)}) collective-permute-start(bf16[4,16,896]{2,1,0:T(8,128)(2,1)S(1)} %constant_dynamic-update-slice_fusion.12.refs_0_), channel_id=1, source_target_pairs={{0,8},{8,16},{16,24},{24,0},{1,9},{9,17},{17,25},{25,1},{2,10},{10... | collective-permute-start | bytes 344072 | tf_op jit(solution)/shard_map/ppermute | solution.py:630
  244.3 38.2 %collective-permute-start.63 = (bf16[512,1024]{1,0:T(8,128)(2,1)S(1)}, bf16[512,1024]{1,0:T(8,128)(2,1)S(1)}, u32[]{:S(2)}, u32[]{:S(2)}) collective-permute-start(bf16[512,1024]{1,0:T(8,128)(2,1)S(1)} %collective-permute-done.50.refs_0_), channel_id=1, source_target_pairs={{1,3},{3,1},{4,6},{6,4},{9,11},{11,9},{12,14},{14,12},{17,19},{19,... | collective-permute-start | bytes 3145736 | tf_op jit(solution)/shard_map/ppermute | solution.py:700
  271.0 17.0 %collective-permute-start.62 = (bf16[2,16,3200]{2,1,0:T(8,128)(2,1)}, bf16[2,16,3200]{2,1,0:T(8,128)(2,1)S(1)}, u32[]{:S(2)}, u32[]{:S(2)}) collective-permute-start(bf16[2,16,3200]{2,1,0:T(8,128)(2,1)} %collective-permute-done.54.refs_3_), channel_id=1, source_target_pairs={{0,4},{4,0},{1,5},{5,1},{2,6},{6,2},{3,7},{7,3},{8,12},{12,8},{9,1... | collective-permute-start | bytes 614408 | tf_op jit(solution)/shard_map/ppermute | solution.py:971
  291.2 20.7 %collective-permute-start.71 = (bf16[512,1024]{1,0:T(8,128)(2,1)S(1)}, bf16[512,1024]{1,0:T(8,128)(2,1)}, u32[]{:S(2)}, u32[]{:S(2)}) collective-permute-start(bf16[512,1024]{1,0:T(8,128)(2,1)S(1)} %add_convert_fusion.1), channel_id=1, source_target_pairs={{0,2},{1,4},{2,0},{3,6},{4,1},{5,7},{6,3},{7,5},{8,10},{9,12},{10,... | collective-permute-start | bytes 3145736 | tf_op jit(solution)/shard_map/ppermute | solution.py:695
  312.6 15.7 %collective-permute-start.76 = (bf16[512,1024]{1,0:T(8,128)(2,1)}, bf16[512,1024]{1,0:T(8,128)(2,1)S(1)}, u32[]{:S(2)}, u32[]{:S(2)}) collective-permute-start(bf16[512,1024]{1,0:T(8,128)(2,1)} %collective-permute-done.71.refs_0_), channel_id=1, source_target_pairs={{1,3},{3,1},{4,6},{6,4},{9,11},{11,9},{12,14},{14,12},{17,19},{19,... | collective-permute-start | bytes 3145736 | tf_op jit(solution)/shard_map/ppermute | solution.py:700
  (150 other events, 1335.6 us)

commit v4 on v3

--- a/solution.py
+++ b/solution.py
@@ -290,7 +290,7 @@
     rows = gb.shape[0]
     hidden = u1.shape[1]
     rank = down.shape[0]
-    chunk = min(512, hidden)
+    chunk = min(1024, hidden)
     block = min(256, own)
     whole = lambda shape: pl.BlockSpec(shape, lambda j, place: (0, 0))
     part = lambda depth: pl.BlockSpec((depth, chunk), lambda j, place: (0, j))

time: 344 us -> 355 us (1.032)
  starting transfers between devices: 73.5 us -> 83.1 us
    ppermute x18, starting transfers between devices: 12 us -> 21.9 us  [hop(): return lax.ppermute(value, axis, ring[axis])]
  transfers between devices with their start and end apart: 79 -> 79, of which waited for: 27 -> 26; matrix products, arithmetic and copies ran while one was open for 13% -> 13% of each run, Pallas kernels for 26% -> 26%
where the time goes in v4:
time: 355 us; the launch traced here: 349 us
  Pallas kernels  128 us (36%)
  starting transfers between devices  83.1 us (23%)
  waiting for transfers between devices  72.3 us (20%)
  matrix products  25.6 us (7%)
  other arithmetic  18.9 us (5%)
  local copies, waits for them, and re-layouts  16.3 us (5%)
  between operations  5.22 us (1%)
    pallas_call x1, Pallas kernels, mlp(): pl.pallas_call(functools.partial(mlp_kernel, block, own, moves, len(parts...  33.2 us
    pallas_call x2, Pallas kernels, attend_back(): pl.pallas_call(functools.partial(attend_back_kernel, block, near), grid=(...  30.7 us
    ppermute x18, waiting for transfers between devices, hop(): return lax.ppermute(value, axis, ring[axis])  29.3 us
    pallas_call x2, Pallas kernels, attend(): pl.pallas_call(functools.partial(attend_kernel, block), grid=(near,), in_...  22.4 us
    ppermute x18, starting transfers between devices, hop(): return lax.ppermute(value, axis, ring[axis])  21.9 us
    ppermute x21, waiting for transfers between devices, cross_to(): return lax.ppermute(value, plane, cross[turn])  21.4 us
    ppermute x21, starting transfers between devices, cross_to(): return lax.ppermute(value, plane, cross[turn])  18.6 us
    pallas_call x3, Pallas kernels, settle(): pl.pallas_call(functools.partial(settle_kernel, len(parts)), grid_spec=pl...  14.3 us
  transfers between devices with their start and end apart: 79, of which 26 were waited for; matrix products, arithmetic and copies ran while one was open for 13% of the time, Pallas kernels for 26%

profile of v4, /device:TPU:1, one launch (start us, length us, event | category | flops | bytes accessed | tf_op | source)
XLA Modules:
  0.0 349.4 jit_solution(4279221366846137485)
XLA Ops:
  2.1 4.5 %collective-permute-start.3 = (bf16[512,1024]{1,0:T(8,128)(2,1)S(1)}, bf16[512,1024]{1,0:T(8,128)(2,1)}, u32[]{:S(2)}, u32[]{:S(2)}) collective-permute-start(bf16[512,1024]{1,0:T(8,128)(2,1)S(1)} %dynamic-slice_bitcast_fusion.1), channel_id=1, source_target_pairs={{4,1},{6,3},{1,4},{3,6},{12,9},{14,11},{9,12},{11,14},{20,17},{22,... | collective-permute-start | bytes 3145736 | tf_op jit(solution)/shard_map/ppermute | solution.py:675
  12.0 10.3 %collective-permute-done.3 = bf16[512,1024]{1,0:T(8,128)(2,1)} collective-permute-done((bf16[512,1024]{1,0:T(8,128)(2,1)S(1)}, bf16[512,1024]{1,0:T(8,128)(2,1)}, u32[]{:S(2)}, u32[]{:S(2)}) %collective-permute-start.3) | collective-permute-done | bytes 1048608 | tf_op jit(solution)/shard_map/ppermute | solution.py:675
  29.7 5.6 %collective-permute-done.5.refs_8_ = bf16[128,1024]{1,0:T(8,128)(2,1)} collective-permute-done((bf16[128,1024]{1,0:T(8,128)(2,1)S(1)}, bf16[128,1024]{1,0:T(8,128)(2,1)}, u32[]{:S(2)}, u32[]{:S(2)}) %collective-permute-start.5) | collective-permute-done | bytes 262176 | tf_op jit(solution)/shard_map/ppermute | solution.py:630
  35.3 8.3 %collective-permute-done.6.refs_5_ = bf16[128,1024]{1,0:T(8,128)(2,1)} collective-permute-done((bf16[128,1024]{1,0:T(8,128)(2,1)S(1)}, bf16[128,1024]{1,0:T(8,128)(2,1)}, u32[]{:S(2)}, u32[]{:S(2)}) %collective-permute-start.6) | collective-permute-done | bytes 262176 | tf_op jit(solution)/shard_map/ppermute | solution.py:722
  61.8 3.2 subtract_multiply_fusion
  78.3 10.2 %project.1 = (bf16[1024,1536]{1,0:T(8,128)(2,1)}, bf16[1024,512]{1,0:T(8,128)(2,1)}, bf16[1024,1536]{1,0:T(8,128)(2,1)}) custom-call(s32[2,16]{1,0:T(2,128)} %pad_add_fusion.place_ref, bf16[1024,1024]{1,0:T(8,128)(2,1)} %copy-done.4, bf16[48,1024]{1,0:T(8,128)(2,1)} %convolution_convert_fusion.1.u_ref, bf16[48,1536]{1,0:T(8,128)(2,1)} %get-tuple-element.194.lift_ref, ...), custom_call_target="tpu_custom_call" | custom-call | flops 1000 | bytes 1000 | tf_op jit(solution)/shard_map/project/pallas_call | solution.py:392
  92.4 4.6 %collective-permute-start.29 = (bf16[512,1024]{1,0:T(8,128)(2,1)S(1)}, bf16[512,1024]{1,0:T(8,128)(2,1)}, u32[]{:S(2)}, u32[]{:S(2)}) collective-permute-start(bf16[512,1024]{1,0:T(8,128)(2,1)S(1)} %dynamic-slice_bitcast_fusion), channel_id=1, source_target_pairs={{4,1},{6,3},{1,4},{3,6},{12,9},{14,11},{9,12},{11,14},{20,17},{22,... | collective-permute-start | bytes 3145736 | tf_op jit(solution)/shard_map/ppermute | solution.py:675
  98.9 11.2 %attend.2 = (bf16[1024,512]{1,0:T(8,128)(2,1)}, f32[2,8,1024]{2,1,0:T(8,128)}) custom-call(bf16[1024,1536]{1,0:T(8,128)(2,1)} %get-tuple-element.212.q_ref.k_ref.v_ref._, bf16[1024,1536]{1,0:T(8,128)(2,1)} %get-tuple-element.212.q_ref.k_ref.v_ref._, bf16[1024,1536]{1,0:T(8,128)(2,1)} %get-tuple-element.212.q_ref.k_ref.v_ref._, ...), custom_call_target="tpu_custom_call" | custom-call | flops 1000 | bytes 1000 | tf_op jit(solution)/shard_map/attend/pallas_call | solution.py:83
  113.8 11.2 %attend.3 = (bf16[1024,512]{1,0:T(8,128)(2,1)}, f32[2,8,1024]{2,1,0:T(8,128)}) custom-call(bf16[1024,1536]{1,0:T(8,128)(2,1)} %get-tuple-element.212.q_ref.k_ref.v_ref._, bf16[1024,1536]{1,0:T(8,128)(2,1)} %get-tuple-element.212.q_ref.k_ref.v_ref._, bf16[1024,1536]{1,0:T(8,128)(2,1)} %get-tuple-element.212.q_ref.k_ref.v_ref._, ...), custom_call_target="tpu_custom_call", output_to_operand_aliasing={{0}: (3, {})} | custom-call | flops 1000 | bytes 1000 | tf_op jit(solution)/shard_map/attend/pallas_call | solution.py:83
  141.5 6.2 %collective-permute-done.33.refs_13_ = bf16[256,1024]{1,0:T(8,128)(2,1)} collective-permute-done((bf16[256,1024]{1,0:T(8,128)(2,1)}, bf16[256,1024]{1,0:T(8,128)(2,1)}, u32[]{:S(2)}, u32[]{:S(2)}) %collective-permute-start.33) | collective-permute-done | bytes 524320 | tf_op jit(solution)/shard_map/ppermute | solution.py:630
  153.8 4.5 %collective-permute-done.37.refs_15_ = bf16[256,1024]{1,0:T(8,128)(2,1)} collective-permute-done((bf16[256,1024]{1,0:T(8,128)(2,1)}, bf16[256,1024]{1,0:T(8,128)(2,1)}, u32[]{:S(2)}, u32[]{:S(2)}) %collective-permute-start.37) | collective-permute-done | bytes 524320 | tf_op jit(solution)/shard_map/ppermute | solution.py:722
  158.3 33.2 %mlp.1 = (f32[512,1024]{1,0:T(8,128)}, bf16[512,1024]{1,0:T(8,128)(2,1)}, f32[512,1024]{1,0:T(8,128)}, f32[512,1024]{1,0:T(8,128)}, f32[32,512]{1,0:T(8,128)}, /...) custom-call(s32[2,32]{1,0:T(2,128)} %add_add_fusion.place_ref, ...), custom_call_target="tpu_custom_call" | custom-call | flops 1000 | bytes 1000 | tf_op jit(solution)/shard_map/mlp/pallas_call | solution.py:306
  215.2 5.0 %collective-permute-done.43.refs_1_ = bf16[2,16,3200]{2,1,0:T(8,128)(2,1)S(1)} collective-permute-done((bf16[2,16,3200]{2,1,0:T(8,128)(2,1)S(1)}, bf16[2,16,3200]{2,1,0:T(8,128)(2,1)S(1)}, u32[]{:S(2)}, u32[]{:S(2)}) %collective-permute-start.43) | collective-permute-done | bytes 204832 | tf_op jit(solution)/shard_map/ppermute | solution.py:630
  221.1 10.1 %collective-permute-start.49 = (bf16[2,16,3200]{2,1,0:T(8,128)(2,1)S(1)}, bf16[2,16,3200]{2,1,0:T(8,128)(2,1)S(1)}, u32[]{:S(2)}, u32[]{:S(2)}) collective-permute-start(bf16[2,16,3200]{2,1,0:T(8,128)(2,1)S(1)} %collective-permute-done.43.refs_1_), channel_id=1, source_target_pairs={{0,8},{8,16},{16,24},{24,0},{1,9},{9,17},{17,25},{25,1},{2,10},{10... | collective-permute-start | bytes 614408 | tf_op jit(solution)/shard_map/ppermute | solution.py:630
  232.7 15.3 %attend_back.2._ = bf16[1024,1536]{1,0:T(8,128)(2,1)} custom-call(bf16[1024,1536]{1,0:T(8,128)(2,1)} %get-tuple-element.212.q_ref.k_ref.v_ref._, bf16[1024,1536]{1,0:T(8,128)(2,1)} %get-tuple-element.212.q_ref.k_ref.v_ref._, bf16[1024,1536]{1,0:T(8,128)(2,1)} %get-tuple-element.212.q_ref.k_ref.v_ref._, bf16[1024,512]{1,0:T(8,128)(2,1)} %add_convert_fusion.3.go_ref, ...), custom_call_target="tpu_custom_call" | custom-call | flops 1000 | bytes 1000 | tf_op jit(solution)/shard_map/attend_back/pallas_call | solution.py:156
  252.2 15.4 %attend_back.3 = bf16[1024,1536]{1,0:T(8,128)(2,1)} custom-call(bf16[1024,1536]{1,0:T(8,128)(2,1)} %get-tuple-element.212.q_ref.k_ref.v_ref._, bf16[1024,1536]{1,0:T(8,128)(2,1)} %get-tuple-element.212.q_ref.k_ref.v_ref._, bf16[1024,1536]{1,0:T(8,128)(2,1)} %get-tuple-element.212.q_ref.k_ref.v_ref._, ...), custom_call_target="tpu_custom_call", output_to_operand_aliasing={{}: (6, {})} | custom-call | flops 1000 | bytes 1000 | tf_op jit(solution)/shard_map/attend_back/pallas_call | solution.py:156
  268.4 4.3 %fusion.1 = f32[512,1024]{1,0:T(8,128)S(1)} fusion(bf16[1024,1536]{1,0:T(8,128)(2,1)} %get-tuple-element.261, bf16[1024,1536]{1,0:T(8,128)(2,1)} %attend_back.3), kind=kOutput, calls=%fused_computation.23 | convolution fusion | flops 1610612736 | bytes 6815744 | tf_op jit(solution)/shard_map/dot_general | solution.py:29
  277.0 4.4 %collective-permute-start.62 = (bf16[2,16,3200]{2,1,0:T(8,128)(2,1)}, bf16[2,16,3200]{2,1,0:T(8,128)(2,1)S(1)}, u32[]{:S(2)}, u32[]{:S(2)}) collective-permute-start(bf16[2,16,3200]{2,1,0:T(8,128)(2,1)} %collective-permute-done.54.refs_3_), channel_id=1, source_target_pairs={{0,4},{4,0},{1,5},{5,1},{2,6},{6,2},{3,7},{7,3},{8,12},{12,8},{9,1... | collective-permute-start | bytes 614408 | tf_op jit(solution)/shard_map/ppermute | solution.py:971
  285.9 3.5 %collective-permute-done.57 = bf16[16,2432]{1,0:T(8,128)(2,1)S(1)} collective-permute-done((bf16[16,2432]{1,0:T(8,128)(2,1)S(1)}, bf16[16,2432]{1,0:T(8,128)(2,1)S(1)}, u32[]{:S(2)}, u32[]{:S(2)}) %collective-permute-start.57) | collective-permute-done | bytes 77856 | tf_op jit(solution)/shard_map/ppermute | solution.py:958
  303.8 6.4 %collective-permute-done.67.refs_3_ = bf16[4,16,896]{2,1,0:T(8,128)(2,1)S(1)} collective-permute-done((bf16[4,16,896]{2,1,0:T(8,128)(2,1)}, bf16[4,16,896]{2,1,0:T(8,128)(2,1)S(1)}, u32[]{:S(2)}, u32[]{:S(2)}) %collective-permute-start.67) | collective-permute-done | bytes 114720 | tf_op jit(solution)/shard_map/ppermute | solution.py:630
  313.8 5.4 %settle.3 = bf16[4,512,1024]{2,1,0:T(8,128)(2,1)} custom-call(s32[4]{0:T(128)} %xor_add_fusion.where_ref, bf16[512,1024]{1,0:T(8,128)(2,1)} %copy-done.21, bf16[512,1024]{1,0:T(8,128)(2,1)} %copy-done.14, bf16[512,1024]{1,0:T(8,128)(2,1)} %collective-permute-done.65.refs_2_, bf16[512,1024]{1,0:T(8,128)(2,1)} %collective-permute-done.66.refs_3_), custom_call_target="tpu_custom_call" | custom-call | tf_op jit(solution)/shard_map/settle/pallas_call | solution.py:555
  327.6 4.4 %settle.4.refs_2_ = f32[4,512,1024]{2,1,0:T(8,128)} custom-call(s32[4]{0:T(128)} %xor_add_fusion.where_ref, bf16[512,1024]{1,0:T(8,128)(2,1)} %collective-permute-done.71.refs_0_, bf16[512,1024]{1,0:T(8,128)(2,1)} %collective-permute-done.72.refs_1_), custom_call_target="tpu_custom_call" | custom-call | tf_op jit(solution)/shard_map/settle/pallas_call | solution.py:555
  340.6 3.1 spread.3
  344.7 4.5 %settle.5 = f32[4,512,1024]{2,1,0:T(8,128)} custom-call(s32[4]{0:T(128)} %xor_add_fusion.where_ref, bf16[512,1024]{1,0:T(8,128)(2,1)} %copy-done.15, bf16[512,1024]{1,0:T(8,128)(2,1)} %copy-done.23, f32[4,512,1024]{2,1,0:T(8,128)} %settle.4.refs_2_), custom_call_target="tpu_custom_call", output_to_operand_aliasing={{}: (3, {})} | custom-call | tf_op jit(solution)/shard_map/settle/pallas_call | solution.py:555
  (434 shorter events, 149.3 us)
Async XLA Ops:
  2.1 20.1 %collective-permute-start.3 = (bf16[512,1024]{1,0:T(8,128)(2,1)S(1)}, bf16[512,1024]{1,0:T(8,128)(2,1)}, u32[]{:S(2)}, u32[]{:S(2)}) collective-permute-start(bf16[512,1024]{1,0:T(8,128)(2,1)S(1)} %dynamic-slice_bitcast_fusion.1), channel_id=1, source_target_pairs={{4,1},{6,3},{1,4},{3,6},{12,9},{14,11},{9,12},{11,14},{20,17},{22,... | collective-permute-start | bytes 3145736 | tf_op jit(solution)/shard_map/ppermute | solution.py:675
  6.8 20.0 %collective-permute-start.4 = (bf16[256,1024]{1,0:T(8,128)(2,1)S(1)}, bf16[256,1024]{1,0:T(8,128)(2,1)}, u32[]{:S(2)}, u32[]{:S(2)}) collective-permute-start(bf16[256,1024]{1,0:T(8,128)(2,1)S(1)} %constant_dynamic-update-slice_fusion.refs_0_), channel_id=1, source_target_pairs={{0,8},{8,16},{16,24},{24,0},{1,9},{9,17},{17,25},{25,1},{2,10},{10... | collective-permute-start | bytes 1572872 | tf_op jit(solution)/shard_map/ppermute | solution.py:630
  8.2 18.5 %collective-permute-start = (bf16[128,1024]{1,0:T(8,128)(2,1)S(1)}, bf16[128,1024]{1,0:T(8,128)(2,1)S(1)}, u32[]{:S(2)}, u32[]{:S(2)}) collective-permute-start(bf16[128,1024]{1,0:T(8,128)(2,1)S(1)} %pad_maximum_fusion.7.refs_0_), channel_id=1, source_target_pairs={{0,8},{8,16},{16,24},{24,0},{1,9},{9,17},{17,25},{25,1},{2,10},{10... | collective-permute-start | bytes 786440 | tf_op jit(solution)/shard_map/ppermute | solution.py:630
  9.5 17.2 %collective-permute-start.1 = (bf16[128,1024]{1,0:T(8,128)(2,1)S(1)}, bf16[128,1024]{1,0:T(8,128)(2,1)S(1)}, u32[]{:S(2)}, u32[]{:S(2)}) collective-permute-start(bf16[128,1024]{1,0:T(8,128)(2,1)S(1)} %pad_maximum_fusion.7.refs_0_), channel_id=1, source_target_pairs={{0,2},{1,5},{2,0},{3,7},{4,6},{5,1},{6,4},{7,3},{8,10},{9,13},{10,... | collective-permute-start | bytes 786440 | tf_op jit(solution)/shard_map/ppermute | solution.py:722
  9.5 17.2 %collective-permute-start.2 = (bf16[128,1024]{1,0:T(8,128)(2,1)S(1)}, bf16[128,1024]{1,0:T(8,128)(2,1)}, u32[]{:S(2)}, u32[]{:S(2)}) collective-permute-start(bf16[128,1024]{1,0:T(8,128)(2,1)S(1)} %pad_maximum_fusion.7.refs_0_), channel_id=1, source_target_pairs={{0,4},{1,3},{2,6},{3,1},{4,0},{5,7},{6,2},{7,5},{8,12},{9,11},{10,... | collective-permute-start | bytes 786440 | tf_op jit(solution)/shard_map/ppermute | solution.py:722
  26.7 16.9 %collective-permute-start.9 = (bf16[256,1024]{1,0:T(8,128)(2,1)S(1)}, bf16[256,1024]{1,0:T(8,128)(2,1)S(1)}, u32[]{:S(2)}, u32[]{:S(2)}) collective-permute-start(bf16[256,1024]{1,0:T(8,128)(2,1)S(1)} %constant_dynamic-update-slice_fusion.refs_0_), channel_id=1, source_target_pairs={{0,2},{1,5},{2,0},{3,7},{4,6},{5,1},{6,4},{7,3},{8,10},{9,13},{10,... | collective-permute-start | bytes 1572872 | tf_op jit(solution)/shard_map/ppermute | solution.py:722
  27.3 16.3 %collective-permute-start.6 = (bf16[128,1024]{1,0:T(8,128)(2,1)S(1)}, bf16[128,1024]{1,0:T(8,128)(2,1)}, u32[]{:S(2)}, u32[]{:S(2)}) collective-permute-start(bf16[128,1024]{1,0:T(8,128)(2,1)S(1)} %collective-permute-done.refs_4_), channel_id=1, source_target_pairs={{0,2},{1,5},{2,0},{3,7},{4,6},{5,1},{6,4},{7,3},{8,10},{9,13},{10,... | collective-permute-start | bytes 786440 | tf_op jit(solution)/shard_map/ppermute | solution.py:722
  92.4 32.7 %collective-permute-start.29 = (bf16[512,1024]{1,0:T(8,128)(2,1)S(1)}, bf16[512,1024]{1,0:T(8,128)(2,1)}, u32[]{:S(2)}, u32[]{:S(2)}) collective-permute-start(bf16[512,1024]{1,0:T(8,128)(2,1)S(1)} %dynamic-slice_bitcast_fusion), channel_id=1, source_target_pairs={{4,1},{6,3},{1,4},{3,6},{12,9},{14,11},{9,12},{11,14},{20,17},{22,... | collective-permute-start | bytes 3145736 | tf_op jit(solution)/shard_map/ppermute | solution.py:675
  97.7 29.2 %collective-permute-start.26 = (bf16[256,1024]{1,0:T(8,128)(2,1)}, bf16[256,1024]{1,0:T(8,128)(2,1)}, u32[]{:S(2)}, u32[]{:S(2)}) collective-permute-start(bf16[256,1024]{1,0:T(8,128)(2,1)} %collective-permute-done.4.refs_4_), channel_id=1, source_target_pairs={{0,4},{1,3},{2,6},{3,1},{4,0},{5,7},{6,2},{7,5},{8,12},{9,11},{10,... | collective-permute-start | bytes 1572872 | tf_op jit(solution)/shard_map/ppermute | solution.py:722
  112.2 15.4 %collective-permute-start.25 = (bf16[256,1024]{1,0:T(8,128)(2,1)}, bf16[256,1024]{1,0:T(8,128)(2,1)}, u32[]{:S(2)}, u32[]{:S(2)}) collective-permute-start(bf16[256,1024]{1,0:T(8,128)(2,1)} %collective-permute-done.21.refs_5_), channel_id=1, source_target_pairs={{0,8},{8,16},{16,24},{24,0},{1,9},{9,17},{17,25},{25,1},{2,10},{10... | collective-permute-start | bytes 1572872 | tf_op jit(solution)/shard_map/ppermute | solution.py:630
  132.0 15.7 %collective-permute-start.33 = (bf16[256,1024]{1,0:T(8,128)(2,1)}, bf16[256,1024]{1,0:T(8,128)(2,1)}, u32[]{:S(2)}, u32[]{:S(2)}) collective-permute-start(bf16[256,1024]{1,0:T(8,128)(2,1)} %collective-permute-done.25.refs_9_), channel_id=1, source_target_pairs={{0,8},{8,16},{16,24},{24,0},{1,9},{9,17},{17,25},{25,1},{2,10},{10... | collective-permute-start | bytes 1572872 | tf_op jit(solution)/shard_map/ppermute | solution.py:630
  132.3 16.2 %collective-permute-start.35 = (bf16[256,1024]{1,0:T(8,128)(2,1)}, bf16[256,1024]{1,0:T(8,128)(2,1)}, u32[]{:S(2)}, u32[]{:S(2)}) collective-permute-start(bf16[256,1024]{1,0:T(8,128)(2,1)} %collective-permute-done.25.refs_9_), channel_id=1, source_target_pairs={{0,4},{1,3},{2,6},{3,1},{4,0},{5,7},{6,2},{7,5},{8,12},{9,11},{10,... | collective-permute-start | bytes 1572872 | tf_op jit(solution)/shard_map/ppermute | solution.py:722
  220.2 27.9 %collective-permute-start.50 = (bf16[512,1024]{1,0:T(8,128)(2,1)}, bf16[512,1024]{1,0:T(8,128)(2,1)S(1)}, u32[]{:S(2)}, u32[]{:S(2)}) collective-permute-start(bf16[512,1024]{1,0:T(8,128)(2,1)} %add_convert_fusion.2), channel_id=1, source_target_pairs={{0,2},{1,4},{2,0},{3,6},{4,1},{5,7},{6,3},{7,5},{8,10},{9,12},{10,... | collective-permute-start | bytes 3145736 | tf_op jit(solution)/shard_map/ppermute | solution.py:695
  221.1 27.0 %collective-permute-start.49 = (bf16[2,16,3200]{2,1,0:T(8,128)(2,1)S(1)}, bf16[2,16,3200]{2,1,0:T(8,128)(2,1)S(1)}, u32[]{:S(2)}, u32[]{:S(2)}) collective-permute-start(bf16[2,16,3200]{2,1,0:T(8,128)(2,1)S(1)} %collective-permute-done.43.refs_1_), channel_id=1, source_target_pairs={{0,8},{8,16},{16,24},{24,0},{1,9},{9,17},{17,25},{25,1},{2,10},{10... | collective-permute-start | bytes 614408 | tf_op jit(solution)/shard_map/ppermute | solution.py:630
  231.3 36.3 %collective-permute-start.52 = (bf16[2,16,3200]{2,1,0:T(8,128)(2,1)S(1)}, bf16[2,16,3200]{2,1,0:T(8,128)(2,1)S(1)}, u32[]{:S(2)}, u32[]{:S(2)}) collective-permute-start(bf16[2,16,3200]{2,1,0:T(8,128)(2,1)S(1)} %collective-permute-done.43.refs_1_), channel_id=1, source_target_pairs={{0,4},{4,0},{1,5},{5,1},{2,6},{6,2},{3,7},{7,3},{8,12},{12,8},{9,1... | collective-permute-start | bytes 614408 | tf_op jit(solution)/shard_map/ppermute | solution.py:971
  231.3 16.8 %collective-permute-start.48 = (bf16[2,16,896]{2,1,0:T(8,128)(2,1)S(1)}, bf16[2,16,896]{2,1,0:T(8,128)(2,1)S(1)}, u32[]{:S(2)}, u32[]{:S(2)}) collective-permute-start(bf16[2,16,896]{2,1,0:T(8,128)(2,1)S(1)} %pad_maximum_fusion.11), channel_id=1, source_target_pairs={{0,4},{4,0},{1,5},{5,1},{2,6},{6,2},{3,7},{7,3},{8,12},{12,8},{9,1... | collective-permute-start | bytes 172040 | tf_op jit(solution)/shard_map/ppermute | solution.py:971
  248.1 19.5 %collective-permute-start.53 = (bf16[2,16,3200]{2,1,0:T(8,128)(2,1)S(1)}, bf16[2,16,3200]{2,1,0:T(8,128)(2,1)S(1)}, u32[]{:S(2)}, u32[]{:S(2)}) collective-permute-start(bf16[2,16,3200]{2,1,0:T(8,128)(2,1)S(1)} %collective-permute-done.49.refs_2_), channel_id=1, source_target_pairs={{0,4},{4,0},{1,5},{5,1},{2,6},{6,2},{3,7},{7,3},{8,12},{12,8},{9,1... | collective-permute-start | bytes 614408 | tf_op jit(solution)/shard_map/ppermute | solution.py:971
  248.2 19.4 %collective-permute-start.54 = (bf16[2,16,3200]{2,1,0:T(8,128)(2,1)S(1)}, bf16[2,16,3200]{2,1,0:T(8,128)(2,1)}, u32[]{:S(2)}, u32[]{:S(2)}) collective-permute-start(bf16[2,16,3200]{2,1,0:T(8,128)(2,1)S(1)} %collective-permute-done.49.refs_2_), channel_id=1, source_target_pairs={{0,8},{8,16},{16,24},{24,0},{1,9},{9,17},{17,25},{25,1},{2,10},{10... | collective-permute-start | bytes 614408 | tf_op jit(solution)/shard_map/ppermute | solution.py:630
  248.9 18.7 %collective-permute-start.51 = (bf16[4,16,896]{2,1,0:T(8,128)(2,1)S(1)}, bf16[4,16,896]{2,1,0:T(8,128)(2,1)}, u32[]{:S(2)}, u32[]{:S(2)}) collective-permute-start(bf16[4,16,896]{2,1,0:T(8,128)(2,1)S(1)} %constant_dynamic-update-slice_fusion.12.refs_0_), channel_id=1, source_target_pairs={{0,8},{8,16},{16,24},{24,0},{1,9},{9,17},{17,25},{25,1},{2,10},{10... | collective-permute-start | bytes 344072 | tf_op jit(solution)/shard_map/ppermute | solution.py:630
  250.0 39.8 %collective-permute-start.63 = (bf16[512,1024]{1,0:T(8,128)(2,1)S(1)}, bf16[512,1024]{1,0:T(8,128)(2,1)S(1)}, u32[]{:S(2)}, u32[]{:S(2)}) collective-permute-start(bf16[512,1024]{1,0:T(8,128)(2,1)S(1)} %collective-permute-done.50.refs_0_), channel_id=1, source_target_pairs={{1,3},{3,1},{4,6},{6,4},{9,11},{11,9},{12,14},{14,12},{17,19},{19,... | collective-permute-start | bytes 3145736 | tf_op jit(solution)/shard_map/ppermute | solution.py:700
  276.3 16.5 %collective-permute-start.60 = (f32[512,1024]{1,0:T(8,128)S(1)}, f32[512,1024]{1,0:T(8,128)S(1)}, u32[]{:S(2)}, u32[]{:S(2)}) collective-permute-start(f32[512,1024]{1,0:T(8,128)S(1)} %fusion.1), channel_id=1, source_target_pairs={{0,1},{1,0},{2,3},{3,2},{4,5},{5,4},{6,7},{7,6},{8,9},{9,8},{10,11... | collective-permute-start | bytes 6291464 | tf_op jit(solution)/shard_map/ppermute | solution.py:633
  277.0 18.2 %collective-permute-start.62 = (bf16[2,16,3200]{2,1,0:T(8,128)(2,1)}, bf16[2,16,3200]{2,1,0:T(8,128)(2,1)S(1)}, u32[]{:S(2)}, u32[]{:S(2)}) collective-permute-start(bf16[2,16,3200]{2,1,0:T(8,128)(2,1)} %collective-permute-done.54.refs_3_), channel_id=1, source_target_pairs={{0,4},{4,0},{1,5},{5,1},{2,6},{6,2},{3,7},{7,3},{8,12},{12,8},{9,1... | collective-permute-start | bytes 614408 | tf_op jit(solution)/shard_map/ppermute | solution.py:971
  298.5 20.8 %collective-permute-start.71 = (bf16[512,1024]{1,0:T(8,128)(2,1)S(1)}, bf16[512,1024]{1,0:T(8,128)(2,1)}, u32[]{:S(2)}, u32[]{:S(2)}) collective-permute-start(bf16[512,1024]{1,0:T(8,128)(2,1)S(1)} %add_convert_fusion.1), channel_id=1, source_target_pairs={{0,2},{1,4},{2,0},{3,6},{4,1},{5,7},{6,3},{7,5},{8,10},{9,12},{10,... | collective-permute-start | bytes 3145736 | tf_op jit(solution)/shard_map/ppermute | solution.py:695
  320.0 15.7 %collective-permute-start.76 = (bf16[512,1024]{1,0:T(8,128)(2,1)}, bf16[512,1024]{1,0:T(8,128)(2,1)S(1)}, u32[]{:S(2)}, u32[]{:S(2)}) collective-permute-start(bf16[512,1024]{1,0:T(8,128)(2,1)} %collective-permute-done.71.refs_0_), channel_id=1, source_target_pairs={{1,3},{3,1},{4,6},{6,4},{9,11},{11,9},{12,14},{14,12},{17,19},{19,... | collective-permute-start | bytes 3145736 | tf_op jit(solution)/shard_map/ppermute | solution.py:700
  (150 other events, 1352.8 us)
